TPU v7x, 256 devices: a whole 4x4x8 slice. The times are simulated.
256 devices in a mesh: seq: 32 (over y, x, core), rep: 8 (over z).
Axes of the slice: x: 4, y: 4, z: 8, core: 2. Of those that a mesh axis runs over, the one named last changes fastest.
Arguments:
- tokens: bfloat16 [8, 4096, 1024], P('rep', 'seq'), may hold values from -16 to 16
- cotangent: bfloat16 [8, 4096, 1024], P('rep', 'seq'), may hold values from -6 to 6
- weights: bfloat16 [4, 1024, 512], replicated, may hold values from -0.1875 to 0.1875
- neighbour_lists: int32 [8, 32, 27], P('rep'), may hold values from 0 to 31, as said below
- neighbour_counts: int32 [8, 32], P('rep'), may hold values from 1 to 27, as said below
Outputs:
- output: bfloat16 [8, 4096, 1024], P('rep', 'seq')
- d_inputs: bfloat16 [8, 4096, 1024], P('rep', 'seq')
- weight_grads: float32 [4, 1024, 512], P(None, ('seq', 'rep'))
Inputs may be any that keep to these rules, and one draw needn't show every extreme that they name: `neighbour_lists`: slot 0 of every list is the block itself; the live slots of a list name distinct blocks of the same replica's slab; dead slots hold the block's own position. `neighbour_counts`: in each replica some block has min(27, 32) live slots.
All inputs are finite; a program needn't handle non-finite values.
Results may differ from a plain program's by a relative error of at most 0.023.
The roundings to bfloat16 on the way count: a program that leaves them out, or rounds other values in their place, can miss the bound.
Values may be sent and summed in bfloat16 or wider, within the bound.
No kernel may reach another device: no remote copies, remote signals or barrier semaphores. Data moves between devices by JAX's collectives and lax.ppermute only.
A program may use at most 128 MiB of HBM per device.

v0:
```python
import jax
import jax.numpy as jnp
from jax import lax
from jax.experimental import pallas as pl
from jax.experimental.pallas import tpu as pltpu
from jax.sharding import Mesh, PartitionSpec as P


HEADS = 8
HEAD_DIM = 64
BLOCK = 128
MAXN = 27
GROUP = 4
SLOTS = 28
BF = jnp.bfloat16
F32 = jnp.float32
INTERPRET = False


def dot(a, b):
    return jnp.dot(a, b, preferred_element_type=F32)


def dot_t(a, b):
    return lax.dot_general(a, b, (((1,), (1,)), ((), ())), preferred_element_type=F32)


def grant(mib):
    return pltpu.CompilerParams(vmem_limit_bytes=mib << 20)


def vmem(count):
    return [pl.BlockSpec(memory_space=pltpu.VMEM) for _ in range(count)]


def position(high, low):
    return (high // 4) * 16 + (low // 2) * 8 + (high // 2 % 2) * 4 + (low % 2) * 2 + high % 2


def project_kernel(tok_ref, cot_ref, w_ref, kv_ref, qd_ref, xt_ref, rows):
    step = pl.program_id(0)

    @pl.when(step < 3)
    def _():
        rows[step] = dot(tok_ref[...], w_ref[0]).astype(BF)

    @pl.when(step == 3)
    def _():
        rows[3] = dot(cot_ref[...], w_ref[0]).astype(BF)
        for head in range(HEADS):
            cols = slice(head * HEAD_DIM, (head + 1) * HEAD_DIM)
            scaled = (rows[0, :, cols].astype(F32) * 0.125).astype(BF)
            pair = jnp.concatenate([rows[1, :, cols], rows[2, :, cols]], axis=1)
            for low in range(4):
                kv_ref[position(head, low)] = pair
            qd_ref[head] = jnp.concatenate([scaled, rows[3, :, cols]], axis=1)

    @pl.when(step == 0)
    def _():
        xt_ref[0] = tok_ref[...].T

    @pl.when(step == 1)
    def _():
        xt_ref[1] = cot_ref[...].T


def project(tok, cot, weights):
    rows, width = tok.shape
    whole = lambda step: (0, 0)
    whole3 = lambda step: (0, 0, 0)
    return pl.pallas_call(
        project_kernel,
        grid=(4,),
        in_specs=[
            pl.BlockSpec((rows, width), whole),
            pl.BlockSpec((rows, width), whole),
            pl.BlockSpec((1, width, HEADS * HEAD_DIM), lambda step: (step, 0, 0)),
        ],
        out_specs=[
            pl.BlockSpec((32, rows, 128), whole3),
            pl.BlockSpec((HEADS, rows, 128), whole3),
            pl.BlockSpec((2, width, rows), whole3),
        ],
        out_shape=[
            jax.ShapeDtypeStruct((32, rows, 128), BF),
            jax.ShapeDtypeStruct((HEADS, rows, 128), BF),
            jax.ShapeDtypeStruct((2, width, rows), BF),
        ],
        scratch_shapes=[pltpu.VMEM((4, rows, HEADS * HEAD_DIM), BF)],
        compiler_params=grant(56),
        interpret=INTERPRET,
        name="project",
    )(tok, cot, weights)


def attend_kernel(
    lists_ref, counts_ref, group_ref,
    qd_ref, kvs,
    y_ref, out0, out1, out2, out3,
    kvt, acc, s_scr, p_scr, places,
):
    step = pl.program_id(0)
    group = group_ref[0]
    block = position(step, group)

    @pl.when(step == 0)
    def _():
        for idx in range(32):
            kvt[idx] = kvs[idx].T
        acc[...] = jnp.zeros_like(acc)

    count = counts_ref[block]
    trips = (count + GROUP - 1) // GROUP

    def place(slot):
        raw = lists_ref[block, jnp.minimum(slot, MAXN - 1)]
        where = jnp.where(slot < count, raw, block)
        places[slot] = where
        return where

    qd = qd_ref[0]
    qdt = qd.T
    upper = lax.broadcasted_iota(jnp.int32, (128, 128), 0) < HEAD_DIM
    left = lax.broadcasted_iota(jnp.int32, (128, 128), 1) < HEAD_DIM
    zero = jnp.zeros((128, 128), BF)
    w_in = jnp.concatenate([jnp.where(upper, qdt, zero), jnp.where(upper, zero, qdt)], axis=1)
    w_back = jnp.concatenate([jnp.where(left, qd, zero), jnp.where(left, zero, qd)], axis=0)
    span = GROUP * 128

    def scores(trip, top):
        stack = jnp.concatenate(
            [kvs[place(trip * GROUP + i)] for i in range(GROUP)], axis=0
        )
        both = dot(stack, w_in)
        base = pl.multiple_of(trip * span, span)
        s_scr[pl.ds(base, span), :] = both[:, :128]
        p_scr[pl.ds(base, span), :] = both[:, 128:]
        return jnp.maximum(top, jnp.max(both[:, :128].reshape(span // 8, 8, 128), axis=0))

    top = lax.fori_loop(0, trips, scores, jnp.full((8, 128), -3e38, F32))
    row_max = jnp.max(top, axis=0, keepdims=True)

    def mix(trip, carry):
        total, mixed = carry
        base = pl.multiple_of(trip * span, span)
        parts, values = [], []
        for i in range(GROUP):
            slot = trip * GROUP + i
            shift = jnp.where(slot < count, row_max, 1e30)
            e = jnp.exp(s_scr[pl.ds(base + i * 128, 128), :] - shift)
            s_scr[pl.ds(base + i * 128, 128), :] = e
            total = total + jnp.sum(e.reshape(16, 8, 128), axis=0)
            parts.append(e.astype(BF))
            values.append(kvt[places[slot], HEAD_DIM:, :])
        mixed = mixed + dot(jnp.concatenate(values, axis=1), jnp.concatenate(parts, axis=0))
        return total, mixed

    total, mixed = lax.fori_loop(
        0, trips, mix, (jnp.zeros((8, 128), F32), jnp.zeros((HEAD_DIM, 128), F32))
    )
    inverse = 1.0 / jnp.sum(total, axis=0, keepdims=True)
    attended = (mixed * inverse).astype(BF)
    delta = jnp.sum(
        qdt[HEAD_DIM:, :].astype(F32) * attended.astype(F32), axis=0, keepdims=True
    )

    def back(trip, dq):
        base = pl.multiple_of(trip * span, span)
        dss, pairs, keys, targets = [], [], [], []
        for i in range(GROUP):
            rows = pl.ds(base + i * 128, 128)
            normed = s_scr[rows, :] * inverse
            ds = (normed * (p_scr[rows, :] - delta)).astype(BF)
            dss.append(ds)
            pairs.append(jnp.concatenate([ds, normed.astype(BF)], axis=1))
            where = places[trip * GROUP + i]
            targets.append(where)
            keys.append(kvt[where, :HEAD_DIM, :])
        dq = dq + dot(jnp.concatenate(keys, axis=1), jnp.concatenate(dss, axis=0))
        grads = dot(jnp.concatenate(pairs, axis=0), w_back)
        for i in range(GROUP):
            acc[targets[i]] += grads[i * 128 : (i + 1) * 128]
        return dq

    dq = lax.fori_loop(0, trips, back, jnp.zeros((HEAD_DIM, 128), F32))
    y_ref[0] = jnp.concatenate([dq * 0.125, attended.astype(F32)], axis=0).T.astype(BF)

    @pl.when(step == 7)
    def _():
        for part, ref in enumerate((out0, out1, out2, out3)):
            for idx in range(8):
                ref[idx] = acc[position(idx, group ^ part)].astype(ref.dtype)


def attend(lists, counts, group, qd, kv):
    whole3 = lambda step, *_: (0, 0, 0)
    piece = pl.BlockSpec((8, 128, 128), whole3)
    each = pl.BlockSpec((1, 128, 128), lambda step, *_: (step, 0, 0))
    shape = lambda dtype: jax.ShapeDtypeStruct((8, 128, 128), dtype)
    return pl.pallas_call(
        attend_kernel,
        grid_spec=pltpu.PrefetchScalarGridSpec(
            num_scalar_prefetch=3,
            grid=(8,),
            in_specs=[each, pl.BlockSpec((32, 128, 128), whole3)],
            out_specs=[each] + [piece] * 4,
            scratch_shapes=[
                pltpu.VMEM((32, 128, 128), BF),
                pltpu.VMEM((32, 128, 128), F32),
                pltpu.VMEM((SLOTS * 128, 128), F32),
                pltpu.VMEM((SLOTS * 128, 128), F32),
                pltpu.SMEM((SLOTS,), jnp.int32),
            ],
        ),
        out_shape=[shape(BF), shape(F32), shape(BF), shape(BF), shape(BF)],
        cost_estimate=pl.CostEstimate(
            flops=30_000_000_000, bytes_accessed=4_000_000, transcendentals=4_000_000
        ),
        compiler_params=grant(28),
        interpret=INTERPRET,
        name="attend",
    )(lists, counts, group, qd, kv)


def ordered(y_ref, place):
    return jnp.concatenate([y_ref[place ^ k] for k in (0, 2, 4, 6, 1, 3, 5, 7)], axis=0)


def first_grads_kernel(place_ref, y_ref, *refs):
    xs, out_ref = refs[:8], refs[8]
    y = ordered(y_ref, place_ref[0])
    tok = dot(jnp.concatenate([x[0] for x in xs], axis=1), y)
    cot = dot(jnp.concatenate([x[1] for x in xs], axis=1), y)
    left = lax.broadcasted_iota(jnp.int32, tok.shape, 1) < HEAD_DIM
    out_ref[...] = jnp.where(left, tok, cot)


def second_grads_kernel(place_ref, part0, part1, part2, part3, first_ref, *refs):
    xs, out_ref, mine_refs, y_ref = refs[:8], refs[8], refs[9:17], refs[17]
    y_ref[...] = (
        part0[...]
        + part1[...].astype(F32)
        + part2[...].astype(F32)
        + part3[...].astype(F32)
    ).astype(BF)
    y = ordered(y_ref, place_ref[0])
    for k, ref in enumerate(mine_refs):
        ref[...] = y_ref[place_ref[0] ^ k]
    second = dot(jnp.concatenate([x[0] for x in xs], axis=1), y)
    rows = out_ref.shape[1] // 2
    for index in range(out_ref.shape[0]):
        mine = slice(index * rows, (index + 1) * rows)
        out_ref[index] = jnp.concatenate([first_ref[mine], second[mine]], axis=0).astype(BF)


def grads_call(kernel, place, operands, outs, scratch=()):
    return pl.pallas_call(
        kernel,
        in_specs=[pl.BlockSpec(memory_space=pltpu.SMEM)] + vmem(len(operands)),
        out_specs=vmem(len(outs)),
        out_shape=outs,
        scratch_shapes=list(scratch),
        cost_estimate=pl.CostEstimate(
            flops=2_000_000_000, bytes_accessed=4_000_000, transcendentals=0
        ),
        compiler_params=grant(16),
        interpret=INTERPRET,
    )(place, *operands)


def gather_kernel(in_ref, out_ref):
    replicas, rows = in_ref.shape[0] // 32, in_ref.shape[1] // 2
    parts = []
    for head in range(HEADS):
        total = None
        for low in range(4):
            start = position(head, low) * replicas
            term = jnp.sum(in_ref[start : start + replicas].astype(F32), axis=0)
            total = term if total is None else total + term
        parts.append(total)
    for half, (near, far) in enumerate(((0, 3), (1, 2))):
        mine = slice(half * rows, (half + 1) * rows)
        out_ref[near] = jnp.concatenate([p[mine, :HEAD_DIM] for p in parts], axis=1)
        out_ref[far] = jnp.concatenate([p[mine, HEAD_DIM:] for p in parts], axis=1)


def small_call(kernel, operands, shape, dtype):
    return pl.pallas_call(
        kernel,
        in_specs=vmem(len(operands)),
        out_specs=pl.BlockSpec(memory_space=pltpu.VMEM),
        out_shape=jax.ShapeDtypeStruct(shape, dtype),
        compiler_params=grant(4),
        interpret=INTERPRET,
    )(*operands)


def halves(pieces):
    first = jnp.concatenate([piece[:, :HEAD_DIM] for piece in pieces], axis=1)
    second = jnp.concatenate([piece[:, HEAD_DIM:] for piece in pieces], axis=1)
    return first, second


def output_kernel(y_ref, wq_ref, wo_ref, out_ref, part_ref):
    dq, attended = halves([y_ref[head] for head in range(HEADS)])
    out_ref[...] = dot_t(attended, wo_ref[0]).astype(BF)
    part_ref[...] = dot_t(dq, wq_ref[0])


def inputs_kernel(place_ref, *refs):
    pieces, (part_ref, wk_ref, wv_ref, out_ref, heads) = refs[:8], refs[8:]
    for k, piece in enumerate(pieces):
        heads[place_ref[0] ^ k] = piece[...]
    dk, dv = halves([heads[head] for head in range(HEADS)])
    out_ref[...] = (part_ref[...] + dot_t(dk, wk_ref[0]) + dot_t(dv, wv_ref[0])).astype(BF)


def products_call(kernel, place, arrays, weights, picks, outs, scratch=()):
    whole = lambda array: pl.BlockSpec(array.shape, lambda step: (0,) * array.ndim)
    width = weights.shape[1]
    pick = lambda m: pl.BlockSpec((1, width, HEADS * HEAD_DIM), lambda step: (m, 0, 0))
    return pl.pallas_call(
        kernel,
        grid=(1,),
        in_specs=[pl.BlockSpec(memory_space=pltpu.SMEM) for _ in place]
        + [whole(array) for array in arrays]
        + [pick(m) for m in picks],
        out_specs=[pl.BlockSpec((BLOCK, width), lambda step: (0, 0)) for _ in outs],
        out_shape=[jax.ShapeDtypeStruct((BLOCK, width), dtype) for dtype in outs],
        scratch_shapes=list(scratch),
        cost_estimate=pl.CostEstimate(
            flops=500_000_000, bytes_accessed=4_000_000, transcendentals=0
        ),
        compiler_params=grant(12),
        interpret=INTERPRET,
    )(*place, *arrays, *[weights for _ in picks])


ROW = ("y_low", "x_low")
HEAD = ("y_high", "x_high", "core")
SEQ = ("y_high", "y_low", "x_high", "x_low", "core")


def across(array, axes, flip):
    size = 1 << len(axes)
    return lax.ppermute(array, axes, [(i, i ^ flip) for i in range(size)])


def body(tokens, cotangent, weights, neighbour_lists, neighbour_counts):
    width = tokens.shape[2]
    replicas = lax.axis_size("rep")
    rows = width // (32 * replicas)
    group = lax.axis_index(ROW).astype(jnp.int32).reshape(1)
    place = lax.axis_index(HEAD).astype(jnp.int32).reshape(1)
    swap = lambda array: lax.all_to_all(array, HEAD, 0, 0, tiled=True)

    kv, qd, xt = project(tokens[0], cotangent[0], weights)
    qd = swap(qd)
    kv = lax.all_to_all(kv, SEQ, 0, 0, tiled=True)
    xt, kv = lax.optimization_barrier((xt, kv))
    xs = [xt] + [across(xt, HEAD, k) for k in (2, 4, 6)]
    y, *parts = attend(neighbour_lists[0], neighbour_counts[0], group, qd, kv)
    xs, y = lax.optimization_barrier((xs, y))
    xs = xs + [across(x, HEAD, 1) for x in xs]
    parts = [parts[0]] + [across(parts[k], ROW, k) for k in (1, 2, 3)]
    home = swap(y)
    (first,) = grads_call(
        first_grads_kernel, place, [y, *xs],
        [jax.ShapeDtypeStruct((width, 128), F32)],
    )
    output, partial = products_call(output_kernel, (), (home,), weights, (0, 3), (BF, F32))
    terms, *y2 = grads_call(
        second_grads_kernel, place, [*parts, first, *xs],
        [
            jax.ShapeDtypeStruct((width // rows, 2 * rows, 128), BF),
        ]
        + [jax.ShapeDtypeStruct((128, 128), BF)] * 8,
        [pltpu.VMEM((8, 128, 128), BF)],
    )
    home = y2[:1] + [across(y2[k], HEAD, k) for k in range(1, 8)]
    terms = lax.all_to_all(terms, SEQ + ("rep",), 0, 0, tiled=True)
    (d_inputs,) = products_call(
        inputs_kernel, (place,), (*home, partial), weights, (1, 2), (BF,),
        [pltpu.VMEM((HEADS, BLOCK, 128), BF)],
    )
    summed = small_call(gather_kernel, [terms], (4, rows, HEADS * HEAD_DIM), F32)
    return (output[None], d_inputs[None], summed)


def solution(mesh):
    replicas = mesh.devices.shape[1]
    grid = Mesh(mesh.devices.reshape(2, 2, 2, 2, 2, replicas), SEQ + ("rep",))
    return jax.shard_map(
        body,
        mesh=grid,
        in_specs=(
            P("rep", SEQ, None),
            P("rep", SEQ, None),
            P(),
            P("rep", None, None),
            P("rep", None),
        ),
        out_specs=(
            P("rep", SEQ, None),
            P("rep", SEQ, None),
            P(None, SEQ + ("rep",), None),
        ),
        check_vma=False,
    )
```

profile of v0, /device:TPU:97, one launch (start us, length us, event | category | flops | bytes accessed | tf_op | source)
XLA Modules:
  0.0 132.5 jit_solution(8250218474134136749)
XLA Ops:
  0.7 5.2 %project.1 = (bf16[32,128,128]{2,1,0:T(8,128)(2,1)}, bf16[8,128,128]{2,1,0:T(8,128)(2,1)}, bf16[2,1024,128]{2,1,0:T(8,128)(2,1)}) custom-call(bf16[128,1024]{1,0:T(8,128)(2,1)} %bitcast.10, bf16[128,1024]{1,0:T(8,128)(2,1)} %bitcast.11, bf16[4,1024,512]{2,1,0:T(8,128)(2,1)} %refs_10_.1), custom_call_target="tpu_custom_call" | custom-call | tf_op jit(solution)/shard_map/project/pallas_call | solution.py:71
  5.9 24.8 %all_to_all.20.kvs = bf16[32,128,128]{2,1,0:T(8,128)(2,1)S(1)} all-to-all(bf16[32,128,128]{2,1,0:T(8,128)(2,1)} %get-tuple-element.30), channel_id=1, replica_groups=mesh['y_high'=2,'y_low'=2,'x_high'=2,'x_low'=2,'core'=2,'rep'=8] {'y_hig..., dimensions={0} | all-to-all | bytes 2097152 | tf_op jit(solution)/shard_map/all_to_all | solution.py:359
  30.7 3.7 %all-to-all-start.1 = ((bf16[8,128,128]{2,1,0:T(8,128)(2,1)}), bf16[8,128,128]{2,1,0:T(8,128)(2,1)S(1)}, u32[]{:S(2)}, u32[]{:S(2)}) async-start(bf16[8,128,128]{2,1,0:T(8,128)(2,1)} %get-tuple-element.32), calls=%async_computation.1 | async-start | bytes 524288 | tf_op jit(solution)/shard_map/all_to_all | solution.py:355
  34.4 0.1 copy.8
  34.5 2.9 %collective-permute-start = (bf16[2,1024,128]{2,1,0:T(8,128)(2,1)}, bf16[2,1024,128]{2,1,0:T(8,128)(2,1)S(1)}, u32[]{:S(2)}, u32[]{:S(2)}) collective-permute-start(bf16[2,1024,128]{2,1,0:T(8,128)(2,1)} %get-tuple-element.41.refs_0_), channel_id=1, source_target_pairs={{0,32},{8,40},{32,0},{40,8},{128,160},{136,168},{160,128},{168,136... | collective-permute-start | bytes 1572872 | tf_op jit(solution)/shard_map/ppermute | solution.py:346
  37.4 2.7 %collective-permute-start.1 = (bf16[2,1024,128]{2,1,0:T(8,128)(2,1)}, bf16[2,1024,128]{2,1,0:T(8,128)(2,1)S(1)}, u32[]{:S(2)}, u32[]{:S(2)}) collective-permute-start(bf16[2,1024,128]{2,1,0:T(8,128)(2,1)} %get-tuple-element.41.refs_0_), channel_id=1, source_target_pairs={{0,128},{8,136},{32,160},{40,168},{128,0},{136,8},{160,32},{168,40... | collective-permute-start | bytes 1572872 | tf_op jit(solution)/shard_map/ppermute | solution.py:346
  40.1 0.1 collective-permute-start.2
  40.2 3.0 %all-to-all-done.1.qd_ref = bf16[8,128,128]{2,1,0:T(8,128)(2,1)S(1)} async-done(((bf16[8,128,128]{2,1,0:T(8,128)(2,1)}), bf16[8,128,128]{2,1,0:T(8,128)(2,1)S(1)}, u32[]{:S(2)}, u32[]{:S(2)}) %all-to-all-start.1) | async-done | bytes 262176 | tf_op jit(solution)/shard_map/all_to_all | solution.py:355
  43.1 25.9 %attend.1 = (bf16[8,128,128]{2,1,0:T(8,128)(2,1)}, f32[8,128,128]{2,1,0:T(8,128)S(1)}, bf16[8,128,128]{2,1,0:T(8,128)(2,1)}, bf16[8,128,128]{2,1,0:T(8,128)(2,1)}, bf16[8,128,128]{2,1,0:T(8,128)(2,1)}) custom-call(s32[32,27]{1,0:T(8,128)S(1)} %bitcast.8, s32[32]{0:T(128)S(1)} %bitcast.9, s32[1]{0:T(128)} %bitcast.4.group_ref, ...), custom_call_target="tpu_custom_call" | custom-call | flops 30000001024 | bytes 4000000 | tf_op jit(solution)/shard_map/attend/pallas_call | solution.py:200
  69.0 0.8 copy-done.5
  69.8 0.0 collective-permute-done.refs_1_
  69.8 0.0 collective-permute-done.1.refs_2_
  69.8 0.0 collective-permute-done.2.refs_3_
  69.8 1.9 %collective-permute-start.6 = (bf16[2,1024,128]{2,1,0:T(8,128)(2,1)S(1)}, bf16[2,1024,128]{2,1,0:T(8,128)(2,1)S(1)}, u32[]{:S(2)}, u32[]{:S(2)}) collective-permute-start(bf16[2,1024,128]{2,1,0:T(8,128)(2,1)S(1)} %copy-done.1), channel_id=1, source_target_pairs={{0,8},{8,0},{32,40},{40,32},{128,136},{136,128},{160,168},{168,160... | collective-permute-start | bytes 1572872 | tf_op jit(solution)/shard_map/ppermute | solution.py:346
  71.7 0.1 collective-permute-start.7
  71.8 0.4 collective-permute-start.8
  72.2 0.1 collective-permute-start.9
  72.3 4.5 %collective-permute-start.3 = (bf16[8,128,128]{2,1,0:T(8,128)(2,1)}, bf16[8,128,128]{2,1,0:T(8,128)(2,1)}, u32[]{:S(2)}, u32[]{:S(2)}) collective-permute-start(bf16[8,128,128]{2,1,0:T(8,128)(2,1)} %get-tuple-element.38), channel_id=1, source_target_pairs={{0,16},{16,0},{64,80},{80,64},{1,17},{17,1},{65,81},{81,65},{2,18}... | collective-permute-start | bytes 786440 | tf_op jit(solution)/shard_map/ppermute | solution.py:346
  76.8 0.0 collective-permute-done.6.refs_4_
  76.8 0.0 collective-permute-start.4
  76.8 0.0 collective-permute-done.7.refs_5_
  76.8 2.1 %collective-permute-start.5 = (bf16[8,128,128]{2,1,0:T(8,128)(2,1)}, bf16[8,128,128]{2,1,0:T(8,128)(2,1)}, u32[]{:S(2)}, u32[]{:S(2)}) collective-permute-start(bf16[8,128,128]{2,1,0:T(8,128)(2,1)} %get-tuple-element.40), channel_id=1, source_target_pairs={{0,80},{16,64},{64,16},{80,0},{1,81},{17,65},{65,17},{81,1},{2,82}... | collective-permute-start | bytes 786440 | tf_op jit(solution)/shard_map/ppermute | solution.py:346
  78.9 4.9 %all-to-all-start.2 = ((bf16[8,128,128]{2,1,0:T(8,128)(2,1)}), bf16[8,128,128]{2,1,0:T(8,128)(2,1)S(1)}, u32[]{:S(2)}, u32[]{:S(2)}) async-start(bf16[8,128,128]{2,1,0:T(8,128)(2,1)} %get-tuple-element.35.y_ref), calls=%async_computation.2 | async-start | bytes 524288 | tf_op jit(solution)/shard_map/all_to_all | solution.py:355
  83.8 0.0 collective-permute-done.8.refs_6_
  83.8 2.6 %shard_map.77.first_ref = f32[1024,128]{1,0:T(8,128)S(1)} custom-call(s32[1]{0:T(128)} %bitcast.6.place_ref, bf16[8,128,128]{2,1,0:T(8,128)(2,1)} %get-tuple-element.35.y_ref, bf16[2,1024,128]{2,1,0:T(8,128)(2,1)S(1)} %copy-done.1, bf16[2,1024,128]{2,1,0:T(8,128)(2,1)S(1)} %collective-permute-done.refs_1_, ...), custom_call_target="tpu_custom_call" | custom-call | flops 2000000000 | bytes 4000000 | tf_op jit(solution)/shard_map/pallas_call | solution.py:257
  86.4 0.0 collective-permute-done.3.part1
  86.4 4.6 %collective-permute-done.4.part2 = bf16[8,128,128]{2,1,0:T(8,128)(2,1)} collective-permute-done((bf16[8,128,128]{2,1,0:T(8,128)(2,1)}, bf16[8,128,128]{2,1,0:T(8,128)(2,1)}, u32[]{:S(2)}, u32[]{:S(2)}) %collective-permute-start.4) | collective-permute-done | bytes 262176 | tf_op jit(solution)/shard_map/ppermute | solution.py:346
  91.0 1.0 copy-done.3
  92.0 3.1 %shard_map.78 = (bf16[256,8,128]{2,1,0:T(8,128)(2,1)}, bf16[128,128]{1,0:T(8,128)(2,1)S(1)}, bf16[128,128]{1,0:T(8,128)(2,1)S(1)}, bf16[128,128]{1,0:T(8,128)(2,...) custom-call(s32[1]{0:T(128)} %bitcast.6.place_ref, ...), custom_call_target="tpu_custom_call" | custom-call | flops 2000000000 | bytes 4000000 | tf_op jit(solution)/shard_map/pallas_call | solution.py:257
  95.2 0.0 all-to-all-done.2.y_ref
  95.2 15.5 %all-to-all-start.3 = ((bf16[256,8,128]{2,1,0:T(8,128)(2,1)}), bf16[256,8,128]{2,1,0:T(8,128)(2,1)S(1)}, u32[]{:S(2)}, u32[]{:S(2)}) async-start(bf16[256,8,128]{2,1,0:T(8,128)(2,1)} %get-tuple-element.54), calls=%async_computation.3 | async-start | bytes 1048576 | tf_op jit(solution)/shard_map/all_to_all | solution.py:381
  110.7 0.5 collective-permute-start.10
  111.1 2.7 %collective-permute-start.11 = (bf16[128,128]{1,0:T(8,128)(2,1)S(1)}, bf16[128,128]{1,0:T(8,128)(2,1)S(1)}, u32[]{:S(2)}, u32[]{:S(2)}) collective-permute-start(bf16[128,128]{1,0:T(8,128)(2,1)S(1)} %get-tuple-element.47), channel_id=1, source_target_pairs={{0,32},{8,40},{32,0},{40,8},{128,160},{136,168},{160,128},{168,136... | collective-permute-start | bytes 98312 | tf_op jit(solution)/shard_map/ppermute | solution.py:346
  113.9 0.5 collective-permute-start.12
  114.4 2.8 %collective-permute-start.13 = (bf16[128,128]{1,0:T(8,128)(2,1)S(1)}, bf16[128,128]{1,0:T(8,128)(2,1)S(1)}, u32[]{:S(2)}, u32[]{:S(2)}) collective-permute-start(bf16[128,128]{1,0:T(8,128)(2,1)S(1)} %get-tuple-element.49), channel_id=1, source_target_pairs={{0,128},{8,136},{32,160},{40,168},{128,0},{136,8},{160,32},{168,40... | collective-permute-start | bytes 98312 | tf_op jit(solution)/shard_map/ppermute | solution.py:346
  117.2 0.4 collective-permute-start.14
  117.7 0.0 collective-permute-done.10.refs_1_
  117.7 5.3 %collective-permute-start.15 = (bf16[128,128]{1,0:T(8,128)(2,1)S(1)}, bf16[128,128]{1,0:T(8,128)(2,1)S(1)}, u32[]{:S(2)}, u32[]{:S(2)}) collective-permute-start(bf16[128,128]{1,0:T(8,128)(2,1)S(1)} %get-tuple-element.51), channel_id=1, source_target_pairs={{0,160},{8,168},{32,128},{40,136},{128,32},{136,40},{160,0},{168,8... | collective-permute-start | bytes 98312 | tf_op jit(solution)/shard_map/ppermute | solution.py:346
  122.9 0.4 collective-permute-start.16
  123.3 2.2 %copy-done = bf16[4,1024,512]{2,1,0:T(8,128)(2,1)S(1)} copy-done((bf16[4,1024,512]{2,1,0:T(8,128)(2,1)S(1)}, bf16[4,1024,512]{2,1,0:T(8,128)(2,1)}, u32[]{:S(2)}) %copy-start) | copy-done | bytes 4194328
  125.5 1.2 shard_map.76
  126.7 0.0 collective-permute-done.12.refs_3_
  126.7 0.0 collective-permute-done.13.refs_4_
  126.7 0.0 collective-permute-done.15.refs_6_
  126.7 3.5 %collective-permute-done.16.refs_7_ = bf16[128,128]{1,0:T(8,128)(2,1)S(1)} collective-permute-done((bf16[128,128]{1,0:T(8,128)(2,1)S(1)}, bf16[128,128]{1,0:T(8,128)(2,1)S(1)}, u32[]{:S(2)}, u32[]{:S(2)}) %collective-permute-start.16) | collective-permute-done | bytes 32800 | tf_op jit(solution)/shard_map/ppermute | solution.py:346
  130.2 1.5 %shard_map.79 = bf16[128,1024]{1,0:T(8,128)(2,1)} custom-call(s32[1]{0:T(128)} %bitcast.6.place_ref, bf16[128,128]{1,0:T(8,128)(2,1)S(1)} %get-tuple-element.45.refs_0_, bf16[128,128]{1,0:T(8,128)(2,1)S(1)} %collective-permute-done.10.refs_1_, bf16[128,128]{1,0:T(8,128)(2,1)S(1)} %collective-permute-done.11.refs_2_, ...), custom_call_target="tpu_custom_call" | custom-call | flops 500000000 | bytes 4000000 | tf_op jit(solution)/shard_map/pallas_call | solution.py:322
  131.8 0.0 all-to-all-done.3.in_ref
  131.8 0.8 shard_map.80
  (17 shorter events, 0.0 us)
Async XLA Ops:
  0.6 33.8 %copy-start.7 = (s32[1,32,27]{1,0,2:T(1,128)S(1)}, s32[1,32,27]{1,0,2:T(1,128)}, u32[]{:S(2)}) copy-start(s32[1,32,27]{1,0,2:T(1,128)} %param.8) | copy-start | bytes 10372
  0.6 42.5 %copy-start.4 = (s32[1,32]{1,0:T(1,128)S(1)}, s32[1,32]{1,0:T(1,128)}, u32[]{:S(2)}) copy-start(s32[1,32]{1,0:T(1,128)} %param.9) | copy-start | bytes 388
  30.7 12.4 %all-to-all-start.1 = ((bf16[8,128,128]{2,1,0:T(8,128)(2,1)}), bf16[8,128,128]{2,1,0:T(8,128)(2,1)S(1)}, u32[]{:S(2)}, u32[]{:S(2)}) async-start(bf16[8,128,128]{2,1,0:T(8,128)(2,1)} %get-tuple-element.32), calls=%async_computation.1 | async-start | bytes 524288 | tf_op jit(solution)/shard_map/all_to_all | solution.py:355
  34.5 35.3 %collective-permute-start = (bf16[2,1024,128]{2,1,0:T(8,128)(2,1)}, bf16[2,1024,128]{2,1,0:T(8,128)(2,1)S(1)}, u32[]{:S(2)}, u32[]{:S(2)}) collective-permute-start(bf16[2,1024,128]{2,1,0:T(8,128)(2,1)} %get-tuple-element.41.refs_0_), channel_id=1, source_target_pairs={{0,32},{8,40},{32,0},{40,8},{128,160},{136,168},{160,128},{168,136... | collective-permute-start | bytes 1572872 | tf_op jit(solution)/shard_map/ppermute | solution.py:346
  37.4 32.4 %collective-permute-start.1 = (bf16[2,1024,128]{2,1,0:T(8,128)(2,1)}, bf16[2,1024,128]{2,1,0:T(8,128)(2,1)S(1)}, u32[]{:S(2)}, u32[]{:S(2)}) collective-permute-start(bf16[2,1024,128]{2,1,0:T(8,128)(2,1)} %get-tuple-element.41.refs_0_), channel_id=1, source_target_pairs={{0,128},{8,136},{32,160},{40,168},{128,0},{136,8},{160,32},{168,40... | collective-permute-start | bytes 1572872 | tf_op jit(solution)/shard_map/ppermute | solution.py:346
  40.1 29.7 %collective-permute-start.2 = (bf16[2,1024,128]{2,1,0:T(8,128)(2,1)}, bf16[2,1024,128]{2,1,0:T(8,128)(2,1)S(1)}, u32[]{:S(2)}, u32[]{:S(2)}) collective-permute-start(bf16[2,1024,128]{2,1,0:T(8,128)(2,1)} %get-tuple-element.41.refs_0_), channel_id=1, source_target_pairs={{0,160},{8,168},{32,128},{40,136},{128,32},{136,40},{160,0},{168,8... | collective-permute-start | bytes 1572872 | tf_op jit(solution)/shard_map/ppermute | solution.py:346
  43.1 26.7 %copy-start.1 = (bf16[2,1024,128]{2,1,0:T(8,128)(2,1)S(1)}, bf16[2,1024,128]{2,1,0:T(8,128)(2,1)}, u32[]{:S(2)}) copy-start(bf16[2,1024,128]{2,1,0:T(8,128)(2,1)} %get-tuple-element.41.refs_0_) | copy-start | bytes 1572868
  69.0 0.8 copy-start.5
  69.8 7.0 %collective-permute-start.6 = (bf16[2,1024,128]{2,1,0:T(8,128)(2,1)S(1)}, bf16[2,1024,128]{2,1,0:T(8,128)(2,1)S(1)}, u32[]{:S(2)}, u32[]{:S(2)}) collective-permute-start(bf16[2,1024,128]{2,1,0:T(8,128)(2,1)S(1)} %copy-done.1), channel_id=1, source_target_pairs={{0,8},{8,0},{32,40},{40,32},{128,136},{136,128},{160,168},{168,160... | collective-permute-start | bytes 1572872 | tf_op jit(solution)/shard_map/ppermute | solution.py:346
  71.7 5.1 %collective-permute-start.7 = (bf16[2,1024,128]{2,1,0:T(8,128)(2,1)S(1)}, bf16[2,1024,128]{2,1,0:T(8,128)(2,1)S(1)}, u32[]{:S(2)}, u32[]{:S(2)}) collective-permute-start(bf16[2,1024,128]{2,1,0:T(8,128)(2,1)S(1)} %collective-permute-done.refs_1_), channel_id=1, source_target_pairs={{0,8},{8,0},{32,40},{40,32},{128,136},{136,128},{160,168},{168,160... | collective-permute-start | bytes 1572872 | tf_op jit(solution)/shard_map/ppermute | solution.py:346
  71.8 12.0 %collective-permute-start.8 = (bf16[2,1024,128]{2,1,0:T(8,128)(2,1)S(1)}, bf16[2,1024,128]{2,1,0:T(8,128)(2,1)}, u32[]{:S(2)}, u32[]{:S(2)}) collective-permute-start(bf16[2,1024,128]{2,1,0:T(8,128)(2,1)S(1)} %collective-permute-done.1.refs_2_), channel_id=1, source_target_pairs={{0,8},{8,0},{32,40},{40,32},{128,136},{136,128},{160,168},{168,160... | collective-permute-start | bytes 1572872 | tf_op jit(solution)/shard_map/ppermute | solution.py:346
  72.2 11.6 %collective-permute-start.9 = (bf16[2,1024,128]{2,1,0:T(8,128)(2,1)S(1)}, bf16[2,1024,128]{2,1,0:T(8,128)(2,1)}, u32[]{:S(2)}, u32[]{:S(2)}) collective-permute-start(bf16[2,1024,128]{2,1,0:T(8,128)(2,1)S(1)} %collective-permute-done.2.refs_3_), channel_id=1, source_target_pairs={{0,8},{8,0},{32,40},{40,32},{128,136},{136,128},{160,168},{168,160... | collective-permute-start | bytes 1572872 | tf_op jit(solution)/shard_map/ppermute | solution.py:346
  72.3 14.0 %collective-permute-start.3 = (bf16[8,128,128]{2,1,0:T(8,128)(2,1)}, bf16[8,128,128]{2,1,0:T(8,128)(2,1)}, u32[]{:S(2)}, u32[]{:S(2)}) collective-permute-start(bf16[8,128,128]{2,1,0:T(8,128)(2,1)} %get-tuple-element.38), channel_id=1, source_target_pairs={{0,16},{16,0},{64,80},{80,64},{1,17},{17,1},{65,81},{81,65},{2,18}... | collective-permute-start | bytes 786440 | tf_op jit(solution)/shard_map/ppermute | solution.py:346
  76.8 14.2 %collective-permute-start.4 = (bf16[8,128,128]{2,1,0:T(8,128)(2,1)}, bf16[8,128,128]{2,1,0:T(8,128)(2,1)}, u32[]{:S(2)}, u32[]{:S(2)}) collective-permute-start(bf16[8,128,128]{2,1,0:T(8,128)(2,1)} %get-tuple-element.39), channel_id=1, source_target_pairs={{0,64},{16,80},{64,0},{80,16},{1,65},{17,81},{65,1},{81,17},{2,66}... | collective-permute-start | bytes 786440 | tf_op jit(solution)/shard_map/ppermute | solution.py:346
  76.8 14.2 %copy-start.2 = (bf16[2,1024,128]{2,1,0:T(8,128)(2,1)}, bf16[2,1024,128]{2,1,0:T(8,128)(2,1)S(1)}, u32[]{:S(2)}) copy-start(bf16[2,1024,128]{2,1,0:T(8,128)(2,1)S(1)} %collective-permute-done.7.refs_5_) | copy-start | bytes 1572868
  76.8 14.1 %collective-permute-start.5 = (bf16[8,128,128]{2,1,0:T(8,128)(2,1)}, bf16[8,128,128]{2,1,0:T(8,128)(2,1)}, u32[]{:S(2)}, u32[]{:S(2)}) collective-permute-start(bf16[8,128,128]{2,1,0:T(8,128)(2,1)} %get-tuple-element.40), channel_id=1, source_target_pairs={{0,80},{16,64},{64,16},{80,0},{1,81},{17,65},{65,17},{81,1},{2,82}... | collective-permute-start | bytes 786440 | tf_op jit(solution)/shard_map/ppermute | solution.py:346
  78.9 16.2 %all-to-all-start.2 = ((bf16[8,128,128]{2,1,0:T(8,128)(2,1)}), bf16[8,128,128]{2,1,0:T(8,128)(2,1)S(1)}, u32[]{:S(2)}, u32[]{:S(2)}) async-start(bf16[8,128,128]{2,1,0:T(8,128)(2,1)} %get-tuple-element.35.y_ref), calls=%async_computation.2 | async-start | bytes 524288 | tf_op jit(solution)/shard_map/all_to_all | solution.py:355
  83.8 7.2 %copy-start.6 = (f32[8,128,128]{2,1,0:T(8,128)S(1)}, f32[8,128,128]{2,1,0:T(8,128)}, u32[]{:S(2)}) copy-start(f32[8,128,128]{2,1,0:T(8,128)} %copy-done.5) | copy-start | bytes 1572868
  91.0 1.0 copy-start.3
  95.2 36.6 %all-to-all-start.3 = ((bf16[256,8,128]{2,1,0:T(8,128)(2,1)}), bf16[256,8,128]{2,1,0:T(8,128)(2,1)S(1)}, u32[]{:S(2)}, u32[]{:S(2)}) async-start(bf16[256,8,128]{2,1,0:T(8,128)(2,1)} %get-tuple-element.54), calls=%async_computation.3 | async-start | bytes 1048576 | tf_op jit(solution)/shard_map/all_to_all | solution.py:381
  110.7 7.0 %collective-permute-start.10 = (bf16[128,128]{1,0:T(8,128)(2,1)S(1)}, bf16[128,128]{1,0:T(8,128)(2,1)S(1)}, u32[]{:S(2)}, u32[]{:S(2)}) collective-permute-start(bf16[128,128]{1,0:T(8,128)(2,1)S(1)} %get-tuple-element.46), channel_id=1, source_target_pairs={{0,8},{8,0},{32,40},{40,32},{128,136},{136,128},{160,168},{168,160... | collective-permute-start | bytes 98312 | tf_op jit(solution)/shard_map/ppermute | solution.py:346
  111.1 11.8 %collective-permute-start.11 = (bf16[128,128]{1,0:T(8,128)(2,1)S(1)}, bf16[128,128]{1,0:T(8,128)(2,1)S(1)}, u32[]{:S(2)}, u32[]{:S(2)}) collective-permute-start(bf16[128,128]{1,0:T(8,128)(2,1)S(1)} %get-tuple-element.47), channel_id=1, source_target_pairs={{0,32},{8,40},{32,0},{40,8},{128,160},{136,168},{160,128},{168,136... | collective-permute-start | bytes 98312 | tf_op jit(solution)/shard_map/ppermute | solution.py:346
  113.9 12.9 %collective-permute-start.12 = (bf16[128,128]{1,0:T(8,128)(2,1)S(1)}, bf16[128,128]{1,0:T(8,128)(2,1)S(1)}, u32[]{:S(2)}, u32[]{:S(2)}) collective-permute-start(bf16[128,128]{1,0:T(8,128)(2,1)S(1)} %get-tuple-element.48), channel_id=1, source_target_pairs={{0,40},{8,32},{32,8},{40,0},{128,168},{136,160},{160,136},{168,128... | collective-permute-start | bytes 98312 | tf_op jit(solution)/shard_map/ppermute | solution.py:346
  114.4 12.3 %collective-permute-start.13 = (bf16[128,128]{1,0:T(8,128)(2,1)S(1)}, bf16[128,128]{1,0:T(8,128)(2,1)S(1)}, u32[]{:S(2)}, u32[]{:S(2)}) collective-permute-start(bf16[128,128]{1,0:T(8,128)(2,1)S(1)} %get-tuple-element.49), channel_id=1, source_target_pairs={{0,128},{8,136},{32,160},{40,168},{128,0},{136,8},{160,32},{168,40... | collective-permute-start | bytes 98312 | tf_op jit(solution)/shard_map/ppermute | solution.py:346
  117.2 9.5 %collective-permute-start.14 = (bf16[128,128]{1,0:T(8,128)(2,1)S(1)}, bf16[128,128]{1,0:T(8,128)(2,1)S(1)}, u32[]{:S(2)}, u32[]{:S(2)}) collective-permute-start(bf16[128,128]{1,0:T(8,128)(2,1)S(1)} %get-tuple-element.50), channel_id=1, source_target_pairs={{0,136},{8,128},{32,168},{40,160},{128,8},{136,0},{160,40},{168,32... | collective-permute-start | bytes 98312 | tf_op jit(solution)/shard_map/ppermute | solution.py:346
  117.7 9.1 %collective-permute-start.15 = (bf16[128,128]{1,0:T(8,128)(2,1)S(1)}, bf16[128,128]{1,0:T(8,128)(2,1)S(1)}, u32[]{:S(2)}, u32[]{:S(2)}) collective-permute-start(bf16[128,128]{1,0:T(8,128)(2,1)S(1)} %get-tuple-element.51), channel_id=1, source_target_pairs={{0,160},{8,168},{32,128},{40,136},{128,32},{136,40},{160,0},{168,8... | collective-permute-start | bytes 98312 | tf_op jit(solution)/shard_map/ppermute | solution.py:346
  122.9 7.3 %collective-permute-start.16 = (bf16[128,128]{1,0:T(8,128)(2,1)S(1)}, bf16[128,128]{1,0:T(8,128)(2,1)S(1)}, u32[]{:S(2)}, u32[]{:S(2)}) collective-permute-start(bf16[128,128]{1,0:T(8,128)(2,1)S(1)} %get-tuple-element.52), channel_id=1, source_target_pairs={{0,168},{8,160},{32,136},{40,128},{128,40},{136,32},{160,8},{168,0... | collective-permute-start | bytes 98312 | tf_op jit(solution)/shard_map/ppermute | solution.py:346
  123.3 2.2 %copy-start = (bf16[4,1024,512]{2,1,0:T(8,128)(2,1)S(1)}, bf16[4,1024,512]{2,1,0:T(8,128)(2,1)}, u32[]{:S(2)}) copy-start(bf16[4,1024,512]{2,1,0:T(8,128)(2,1)} %refs_10_.1) | copy-start | bytes 12582916
where the time goes:
time: 135 us; the launch traced here: 133 us
  starting transfers between devices  51.5 us (38%)
  Pallas kernels  40.3 us (30%)
  blocking collectives  24.8 us (18%)
  waiting for transfers between devices  11.1 us (8%)
  local copies, waits for them, and re-layouts  4.12 us (3%)
    ppermute x17, starting transfers between devices, across(): return lax.ppermute(array, axes, [(i, i ^ flip) for i in range(size)])  27.4 us
    pallas_call x1, Pallas kernels, attend(): pl.pallas_call(attend_kernel, grid_spec=pltpu.PrefetchScalarGridSpec(num_...  25.9 us
    all_to_all x1, blocking collectives, body(): kv = lax.all_to_all(kv, SEQ, 0, 0, tiled=True)  24.8 us
    all_to_all x1, starting transfers between devices, body(): terms = lax.all_to_all(terms, SEQ + ('rep',), 0, 0, tiled=True)  15.5 us
    all_to_all x2, starting transfers between devices, body(): swap = lambda array: lax.all_to_all(array, HEAD, 0, 0, tiled=True)  8.56 us
    ppermute x17, waiting for transfers between devices, across(): return lax.ppermute(array, axes, [(i, i ^ flip) for i in range(size)])  8.11 us
    pallas_call x2, Pallas kernels, grads_call(): pl.pallas_call(kernel, in_specs=[pl.BlockSpec(memory_space=pltpu.SMEM)] +...  5.71 us
    pallas_call x1, Pallas kernels, project(): pl.pallas_call(project_kernel, grid=(4,), in_specs=[pl.BlockSpec((rows, w...  5.25 us
  transfers between devices with their start and end apart: 20, of which 3 were waited for; matrix products, arithmetic and copies ran while one was open for 0% of the time, Pallas kernels for 26%

commit v1 on v0

--- a/solution.py
+++ b/solution.py
@@ -33,8 +33,12 @@
     return [pl.BlockSpec(memory_space=pltpu.VMEM) for _ in range(count)]
 
 
+def hbm(count):
+    return [pl.BlockSpec(memory_space=pltpu.HBM) for _ in range(count)]
+
+
 def position(high, low):
-    return (high // 4) * 16 + (low // 2) * 8 + (high // 2 % 2) * 4 + (low % 2) * 2 + high % 2
+    return low * 8 + high
 
 
 def project_kernel(tok_ref, cot_ref, w_ref, kv_ref, qd_ref, xt_ref, rows):
@@ -50,9 +54,7 @@
         for head in range(HEADS):
             cols = slice(head * HEAD_DIM, (head + 1) * HEAD_DIM)
             scaled = (rows[0, :, cols].astype(F32) * 0.125).astype(BF)
-            pair = jnp.concatenate([rows[1, :, cols], rows[2, :, cols]], axis=1)
-            for low in range(4):
-                kv_ref[position(head, low)] = pair
+            kv_ref[head] = jnp.concatenate([rows[1, :, cols], rows[2, :, cols]], axis=1)
             qd_ref[head] = jnp.concatenate([scaled, rows[3, :, cols]], axis=1)
 
     @pl.when(step == 0)
@@ -77,12 +79,12 @@
             pl.BlockSpec((1, width, HEADS * HEAD_DIM), lambda step: (step, 0, 0)),
         ],
         out_specs=[
-            pl.BlockSpec((32, rows, 128), whole3),
+            pl.BlockSpec((HEADS, rows, 128), whole3),
             pl.BlockSpec((HEADS, rows, 128), whole3),
             pl.BlockSpec((2, width, rows), whole3),
         ],
         out_shape=[
-            jax.ShapeDtypeStruct((32, rows, 128), BF),
+            jax.ShapeDtypeStruct((HEADS, rows, 128), BF),
             jax.ShapeDtypeStruct((HEADS, rows, 128), BF),
             jax.ShapeDtypeStruct((2, width, rows), BF),
         ],
@@ -95,9 +97,9 @@
 
 def attend_kernel(
     lists_ref, counts_ref, group_ref,
-    qd_ref, kvs,
+    qd_ref, kv0, kv1, kv2, kv3,
     y_ref, out0, out1, out2, out3,
-    kvt, acc, s_scr, p_scr, places,
+    kvs, kvt, acc, s_scr, p_scr, places, sems,
 ):
     step = pl.program_id(0)
     group = group_ref[0]
@@ -105,16 +107,25 @@
 
     @pl.when(step == 0)
     def _():
-        for idx in range(32):
-            kvt[idx] = kvs[idx].T
+        copies = [
+            pltpu.make_async_copy(ref, kvs.at[pl.ds(8 * part, 8)], sems.at[part])
+            for part, ref in enumerate((kv0, kv1, kv2, kv3))
+        ]
+        for copy in copies:
+            copy.start()
         acc[...] = jnp.zeros_like(acc)
+        for part, copy in enumerate(copies):
+            copy.wait()
+            for idx in range(8 * part, 8 * part + 8):
+                kvt[idx] = kvs[idx].T
 
     count = counts_ref[block]
     trips = (count + GROUP - 1) // GROUP
 
     def place(slot):
         raw = lists_ref[block, jnp.minimum(slot, MAXN - 1)]
-        where = jnp.where(slot < count, raw, block)
+        raw = jnp.where(slot < count, raw, block)
+        where = raw ^ (group * 8)
         places[slot] = where
         return where
 
@@ -189,10 +200,10 @@
     def _():
         for part, ref in enumerate((out0, out1, out2, out3)):
             for idx in range(8):
-                ref[idx] = acc[position(idx, group ^ part)].astype(ref.dtype)
-
-
-def attend(lists, counts, group, qd, kv):
+                ref[idx] = acc[8 * part + idx].astype(ref.dtype)
+
+
+def attend(lists, counts, group, qd, kvs):
     whole3 = lambda step, *_: (0, 0, 0)
     piece = pl.BlockSpec((8, 128, 128), whole3)
     each = pl.BlockSpec((1, 128, 128), lambda step, *_: (step, 0, 0))
@@ -202,14 +213,16 @@
         grid_spec=pltpu.PrefetchScalarGridSpec(
             num_scalar_prefetch=3,
             grid=(8,),
-            in_specs=[each, pl.BlockSpec((32, 128, 128), whole3)],
+            in_specs=[each] + hbm(4),
             out_specs=[each] + [piece] * 4,
             scratch_shapes=[
+                pltpu.VMEM((32, 128, 128), BF),
                 pltpu.VMEM((32, 128, 128), BF),
                 pltpu.VMEM((32, 128, 128), F32),
                 pltpu.VMEM((SLOTS * 128, 128), F32),
                 pltpu.VMEM((SLOTS * 128, 128), F32),
                 pltpu.SMEM((SLOTS,), jnp.int32),
+                pltpu.SemaphoreType.DMA((4,)),
             ],
         ),
         out_shape=[shape(BF), shape(F32), shape(BF), shape(BF), shape(BF)],
@@ -219,7 +232,7 @@
         compiler_params=grant(28),
         interpret=INTERPRET,
         name="attend",
-    )(lists, counts, group, qd, kv)
+    )(lists, counts, group, qd, *kvs)
 
 
 def ordered(y_ref, place):
@@ -235,17 +248,22 @@
     out_ref[...] = jnp.where(left, tok, cot)
 
 
-def second_grads_kernel(place_ref, part0, part1, part2, part3, first_ref, *refs):
-    xs, out_ref, mine_refs, y_ref = refs[:8], refs[8], refs[9:17], refs[17]
-    y_ref[...] = (
-        part0[...]
-        + part1[...].astype(F32)
-        + part2[...].astype(F32)
-        + part3[...].astype(F32)
-    ).astype(BF)
+def second_grads_kernel(place_ref, own, part1, part2, part3, first_ref, *refs):
+    xs, (out_ref, keep_ref, send_ref, y_ref, base, landed, sems) = refs[:8], refs[8:]
+    copies = [pltpu.make_async_copy(own, base, sems.at[0])] + [
+        pltpu.make_async_copy(part, landed.at[k], sems.at[k + 1])
+        for k, part in enumerate((part1, part2, part3))
+    ]
+    for copy in copies:
+        copy.start()
+    for copy in copies:
+        copy.wait()
+    y_ref[...] = (base[...] + jnp.sum(landed[...].astype(F32), axis=0)).astype(BF)
+    chip, core = place_ref[0] // 2, lax.rem(place_ref[0], 2)
+    for k in range(4):
+        keep_ref[k] = y_ref[(chip ^ k) * 2 + core]
+        send_ref[k] = y_ref[(chip ^ k) * 2 + 1 - core]
     y = ordered(y_ref, place_ref[0])
-    for k, ref in enumerate(mine_refs):
-        ref[...] = y_ref[place_ref[0] ^ k]
     second = dot(jnp.concatenate([x[0] for x in xs], axis=1), y)
     rows = out_ref.shape[1] // 2
     for index in range(out_ref.shape[0]):
@@ -253,10 +271,16 @@
         out_ref[index] = jnp.concatenate([first_ref[mine], second[mine]], axis=0).astype(BF)
 
 
-def grads_call(kernel, place, operands, outs, scratch=()):
+def pack_kernel(keep_ref, got_ref, *outs):
+    for k, ref in enumerate(outs):
+        ref[0] = keep_ref[k + 1]
+        ref[1] = got_ref[k + 1]
+
+
+def grads_call(kernel, place, specs, operands, outs, scratch=()):
     return pl.pallas_call(
         kernel,
-        in_specs=[pl.BlockSpec(memory_space=pltpu.SMEM)] + vmem(len(operands)),
+        in_specs=[pl.BlockSpec(memory_space=pltpu.SMEM)] + specs,
         out_specs=vmem(len(outs)),
         out_shape=outs,
         scratch_shapes=list(scratch),
@@ -284,12 +308,12 @@
         out_ref[far] = jnp.concatenate([p[mine, HEAD_DIM:] for p in parts], axis=1)
 
 
-def small_call(kernel, operands, shape, dtype):
+def small_call(kernel, operands, outs):
     return pl.pallas_call(
         kernel,
         in_specs=vmem(len(operands)),
-        out_specs=pl.BlockSpec(memory_space=pltpu.VMEM),
-        out_shape=jax.ShapeDtypeStruct(shape, dtype),
+        out_specs=vmem(len(outs)),
+        out_shape=outs,
         compiler_params=grant(4),
         interpret=INTERPRET,
     )(*operands)
@@ -307,10 +331,14 @@
     part_ref[...] = dot_t(dq, wq_ref[0])
 
 
-def inputs_kernel(place_ref, *refs):
-    pieces, (part_ref, wk_ref, wv_ref, out_ref, heads) = refs[:8], refs[8:]
-    for k, piece in enumerate(pieces):
-        heads[place_ref[0] ^ k] = piece[...]
+def inputs_kernel(place_ref, keep_ref, got_ref, *refs):
+    pairs, (part_ref, wk_ref, wv_ref, out_ref, heads) = refs[:3], refs[3:]
+    place = place_ref[0]
+    heads[place] = keep_ref[0]
+    heads[place ^ 1] = got_ref[0]
+    for k, pair in enumerate(pairs):
+        heads[place ^ (2 * k + 2)] = pair[0]
+        heads[place ^ (2 * k + 3)] = pair[1]
     dk, dv = halves([heads[head] for head in range(HEADS)])
     out_ref[...] = (part_ref[...] + dot_t(dk, wk_ref[0]) + dot_t(dv, wv_ref[0])).astype(BF)
 
@@ -336,60 +364,67 @@
     )(*place, *arrays, *[weights for _ in picks])
 
 
-ROW = ("y_low", "x_low")
-HEAD = ("y_high", "x_high", "core")
-SEQ = ("y_high", "y_low", "x_high", "x_low", "core")
+ROW = ("row",)
+HEAD = ("head",)
+SEQ = ROW + HEAD
 
 
 def across(array, axes, flip):
-    size = 1 << len(axes)
-    return lax.ppermute(array, axes, [(i, i ^ flip) for i in range(size)])
+    return lax.ppermute(array, axes, [(i, i ^ flip) for i in range(lax.axis_size(axes))])
 
 
 def body(tokens, cotangent, weights, neighbour_lists, neighbour_counts):
     width = tokens.shape[2]
-    replicas = lax.axis_size("rep")
-    rows = width // (32 * replicas)
+    rows = width // (32 * lax.axis_size("rep"))
     group = lax.axis_index(ROW).astype(jnp.int32).reshape(1)
     place = lax.axis_index(HEAD).astype(jnp.int32).reshape(1)
     swap = lambda array: lax.all_to_all(array, HEAD, 0, 0, tiled=True)
-
     kv, qd, xt = project(tokens[0], cotangent[0], weights)
+    kv = swap(kv)
+    qd, xt, kv = lax.optimization_barrier((qd, xt, kv))
+    kvs = [kv] + [across(kv, ROW, k) for k in (1, 2, 3)]
     qd = swap(qd)
-    kv = lax.all_to_all(kv, SEQ, 0, 0, tiled=True)
-    xt, kv = lax.optimization_barrier((xt, kv))
     xs = [xt] + [across(xt, HEAD, k) for k in (2, 4, 6)]
-    y, *parts = attend(neighbour_lists[0], neighbour_counts[0], group, qd, kv)
+    y, *parts = attend(neighbour_lists[0], neighbour_counts[0], group, qd, kvs)
     xs, y = lax.optimization_barrier((xs, y))
     xs = xs + [across(x, HEAD, 1) for x in xs]
     parts = [parts[0]] + [across(parts[k], ROW, k) for k in (1, 2, 3)]
     home = swap(y)
     (first,) = grads_call(
-        first_grads_kernel, place, [y, *xs],
+        first_grads_kernel, place, vmem(9), [y, *xs],
         [jax.ShapeDtypeStruct((width, 128), F32)],
     )
     output, partial = products_call(output_kernel, (), (home,), weights, (0, 3), (BF, F32))
-    terms, *y2 = grads_call(
-        second_grads_kernel, place, [*parts, first, *xs],
+    pieces = lambda count: jax.ShapeDtypeStruct((count, 128, 128), BF)
+    terms, keep, send = grads_call(
+        second_grads_kernel, place, hbm(4) + vmem(9),
+        [*parts, first, *xs],
+        [jax.ShapeDtypeStruct((width // rows, 2 * rows, 128), BF), pieces(4), pieces(4)],
         [
-            jax.ShapeDtypeStruct((width // rows, 2 * rows, 128), BF),
-        ]
-        + [jax.ShapeDtypeStruct((128, 128), BF)] * 8,
-        [pltpu.VMEM((8, 128, 128), BF)],
-    )
-    home = y2[:1] + [across(y2[k], HEAD, k) for k in range(1, 8)]
+            pltpu.VMEM((8, 128, 128), BF),
+            pltpu.VMEM((8, 128, 128), F32),
+            pltpu.VMEM((3, 8, 128, 128), BF),
+            pltpu.SemaphoreType.DMA((4,)),
+        ],
+    )
     terms = lax.all_to_all(terms, SEQ + ("rep",), 0, 0, tiled=True)
+    got = across(send, HEAD, 1)
+    pairs = small_call(pack_kernel, [keep, got], [pieces(2)] * 3)
+    pairs = [across(pair, HEAD, 2 * k + 2) for k, pair in enumerate(pairs)]
     (d_inputs,) = products_call(
-        inputs_kernel, (place,), (*home, partial), weights, (1, 2), (BF,),
-        [pltpu.VMEM((HEADS, BLOCK, 128), BF)],
-    )
-    summed = small_call(gather_kernel, [terms], (4, rows, HEADS * HEAD_DIM), F32)
+        inputs_kernel, (place,), (keep, got, *pairs, partial), weights, (1, 2),
+        (BF,), [pltpu.VMEM((HEADS, BLOCK, 128), BF)],
+    )
+    (summed,) = small_call(
+        gather_kernel, [terms],
+        [jax.ShapeDtypeStruct((4, rows, HEADS * HEAD_DIM), F32)],
+    )
     return (output[None], d_inputs[None], summed)
 
 
 def solution(mesh):
     replicas = mesh.devices.shape[1]
-    grid = Mesh(mesh.devices.reshape(2, 2, 2, 2, 2, replicas), SEQ + ("rep",))
+    grid = Mesh(mesh.devices.reshape(4, 8, replicas), SEQ + ("rep",))
     return jax.shard_map(
         body,
         mesh=grid,

time: 135 us -> 125 us (0.926)
  the two profiles are of different devices: /device:TPU:97 before, /device:TPU:1 now
where the time goes in v1:
time: 125 us
  starting transfers between devices  44.9 us (36%)
  Pallas kernels  40.4 us (32%)
  waiting for transfers between devices  21.8 us (17%)
  blocking collectives  13 us (10%)
  local copies, waits for them, and re-layouts  3.72 us (3%)
    pallas_call x1, Pallas kernels, attend(): pl.pallas_call(attend_kernel, grid_spec=pltpu.PrefetchScalarGridSpec(num_...  25.2 us
    ppermute x17, starting transfers between devices, across(): lax.ppermute(array, axes, [(i, i ^ flip) for i in range(lax.axis_size(axe...  21.6 us
    all_to_all x1, starting transfers between devices, body(): terms = lax.all_to_all(terms, SEQ + ('rep',), 0, 0, tiled=True)  14.1 us
    all_to_all x1, blocking collectives, body(): swap = lambda array: lax.all_to_all(array, HEAD, 0, 0, tiled=True)  13 us
    ppermute x17, waiting for transfers between devices, across(): lax.ppermute(array, axes, [(i, i ^ flip) for i in range(lax.axis_size(axe...  12.6 us
    all_to_all x2, starting transfers between devices, body(): swap = lambda array: lax.all_to_all(array, HEAD, 0, 0, tiled=True)  9.16 us
    pallas_call x2, Pallas kernels, grads_call(): pl.pallas_call(kernel, in_specs=[pl.BlockSpec(memory_space=pltpu.SMEM)] +...  6.69 us
    all_to_all x1, waiting for transfers between devices, body(): terms = lax.all_to_all(terms, SEQ + ('rep',), 0, 0, tiled=True)  6.43 us
  transfers between devices with their start and end apart: 20, of which 8 were waited for; matrix products, arithmetic and copies ran while one was open for 0% of the time, Pallas kernels for 28%

profile of v1, /device:TPU:1, one launch (start us, length us, event | category | flops | bytes accessed | tf_op | source)
XLA Modules:
  0.0 124.6 jit_solution(7698403700033317440)
XLA Ops:
  0.7 5.0 %project.1 = (bf16[8,128,128]{2,1,0:T(8,128)(2,1)}, bf16[8,128,128]{2,1,0:T(8,128)(2,1)}, bf16[2,1024,128]{2,1,0:T(8,128)(2,1)}) custom-call(bf16[128,1024]{1,0:T(8,128)(2,1)} %bitcast.10, bf16[128,1024]{1,0:T(8,128)(2,1)} %bitcast.11, bf16[4,1024,512]{2,1,0:T(8,128)(2,1)} %refs_5_.1), custom_call_target="tpu_custom_call" | custom-call | tf_op jit(solution)/shard_map/project/pallas_call | solution.py:73
  5.6 13.0 %all_to_all.20.kv0 = bf16[8,128,128]{2,1,0:T(8,128)(2,1)S(1)} all-to-all(bf16[8,128,128]{2,1,0:T(8,128)(2,1)} %get-tuple-element.29), channel_id=1, replica_groups=mesh['row'=4,'head'=8,'rep'=8] {'head'}, dimensions={0} | all-to-all | bytes 524288 | tf_op jit(solution)/shard_map/all_to_all | solution.py:381
  18.6 0.6 collective-permute-start.3
  19.2 2.6 %collective-permute-start.4 = (bf16[8,128,128]{2,1,0:T(8,128)(2,1)S(1)}, bf16[8,128,128]{2,1,0:T(8,128)(2,1)S(1)}, u32[]{:S(2)}, u32[]{:S(2)}) collective-permute-start(bf16[8,128,128]{2,1,0:T(8,128)(2,1)S(1)} %all_to_all.20.kv0), channel_id=1, source_target_pairs={{0,128},{64,192},{128,0},{192,64},{1,129},{65,193},{129,1},{193,65... | collective-permute-start | bytes 786440 | tf_op jit(solution)/shard_map/ppermute | solution.py:373
  21.8 0.7 collective-permute-start.5
  22.5 5.2 %all-to-all-start.1 = ((bf16[8,128,128]{2,1,0:T(8,128)(2,1)}), bf16[8,128,128]{2,1,0:T(8,128)(2,1)S(1)}, u32[]{:S(2)}, u32[]{:S(2)}) async-start(bf16[8,128,128]{2,1,0:T(8,128)(2,1)} %get-tuple-element.31), calls=%async_computation.1 | async-start | bytes 524288 | tf_op jit(solution)/shard_map/all_to_all | solution.py:381
  27.7 0.1 copy.8
  27.7 1.4 %collective-permute-start = (bf16[2,1024,128]{2,1,0:T(8,128)(2,1)}, bf16[2,1024,128]{2,1,0:T(8,128)(2,1)S(1)}, u32[]{:S(2)}, u32[]{:S(2)}) collective-permute-start(bf16[2,1024,128]{2,1,0:T(8,128)(2,1)} %get-tuple-element.40.refs_0_), channel_id=1, source_target_pairs={{0,16},{8,24},{16,0},{24,8},{32,48},{40,56},{48,32},{56,40},{1,17}... | collective-permute-start | bytes 1572872 | tf_op jit(solution)/shard_map/ppermute | solution.py:373
  29.1 2.4 %collective-permute-start.1 = (bf16[2,1024,128]{2,1,0:T(8,128)(2,1)}, bf16[2,1024,128]{2,1,0:T(8,128)(2,1)S(1)}, u32[]{:S(2)}, u32[]{:S(2)}) collective-permute-start(bf16[2,1024,128]{2,1,0:T(8,128)(2,1)} %get-tuple-element.40.refs_0_), channel_id=1, source_target_pairs={{0,32},{8,40},{16,48},{24,56},{32,0},{40,8},{48,16},{56,24},{1,33}... | collective-permute-start | bytes 1572872 | tf_op jit(solution)/shard_map/ppermute | solution.py:373
  31.6 0.1 collective-permute-start.2
  31.6 2.7 %all-to-all-done.1.qd_ref = bf16[8,128,128]{2,1,0:T(8,128)(2,1)S(1)} async-done(((bf16[8,128,128]{2,1,0:T(8,128)(2,1)}), bf16[8,128,128]{2,1,0:T(8,128)(2,1)S(1)}, u32[]{:S(2)}, u32[]{:S(2)}) %all-to-all-start.1) | async-done | bytes 262176 | tf_op jit(solution)/shard_map/all_to_all | solution.py:381
  34.4 0.8 collective-permute-done.5.kv3
  35.2 25.2 %attend.1 = (bf16[8,128,128]{2,1,0:T(8,128)(2,1)}, f32[8,128,128]{2,1,0:T(8,128)S(1)}, bf16[8,128,128]{2,1,0:T(8,128)(2,1)}, bf16[8,128,128]{2,1,0:T(8,128)(2,1)}, bf16[8,128,128]{2,1,0:T(8,128)(2,1)}) custom-call(s32[32,27]{1,0:T(8,128)S(1)} %bitcast.8, s32[32]{0:T(128)S(1)} %bitcast.9, s32[1]{0:T(128)} %bitcast.4.group_ref, ...), custom_call_target="tpu_custom_call" | custom-call | flops 30000001024 | bytes 4000000 | tf_op jit(solution)/shard_map/attend/pallas_call | solution.py:211
  60.5 0.8 copy-done.4
  61.3 0.0 collective-permute-done.refs_1_
  61.3 0.0 collective-permute-done.1.refs_2_
  61.3 0.0 collective-permute-done.2.refs_3_
  61.3 2.2 %collective-permute-start.10 = (bf16[2,1024,128]{2,1,0:T(8,128)(2,1)S(1)}, bf16[2,1024,128]{2,1,0:T(8,128)(2,1)S(1)}, u32[]{:S(2)}, u32[]{:S(2)}) collective-permute-start(bf16[2,1024,128]{2,1,0:T(8,128)(2,1)S(1)} %collective-permute-done.refs_1_), channel_id=1, source_target_pairs={{0,8},{8,0},{16,24},{24,16},{32,40},{40,32},{48,56},{56,48},{1,9},... | collective-permute-start | bytes 1572872 | tf_op jit(solution)/shard_map/ppermute | solution.py:373
  63.5 0.1 collective-permute-start.11
  63.6 0.4 collective-permute-start.12
  64.0 0.1 collective-permute-start.9
  64.1 0.0 collective-permute-start.6
  64.1 0.9 collective-permute-done.10.refs_5_
  65.0 4.4 %collective-permute-start.7 = (bf16[8,128,128]{2,1,0:T(8,128)(2,1)}, bf16[8,128,128]{2,1,0:T(8,128)(2,1)}, u32[]{:S(2)}, u32[]{:S(2)}) collective-permute-start(bf16[8,128,128]{2,1,0:T(8,128)(2,1)} %get-tuple-element.38), channel_id=1, source_target_pairs={{0,128},{64,192},{128,0},{192,64},{1,129},{65,193},{129,1},{193,65... | collective-permute-start | bytes 786440 | tf_op jit(solution)/shard_map/ppermute | solution.py:373
  69.5 0.0 collective-permute-done.11.refs_6_
  69.5 0.5 collective-permute-start.8
  69.9 4.0 %all-to-all-start.2 = ((bf16[8,128,128]{2,1,0:T(8,128)(2,1)}), bf16[8,128,128]{2,1,0:T(8,128)(2,1)S(1)}, u32[]{:S(2)}, u32[]{:S(2)}) async-start(bf16[8,128,128]{2,1,0:T(8,128)(2,1)} %get-tuple-element.34.y_ref), calls=%async_computation.2 | async-start | bytes 524288 | tf_op jit(solution)/shard_map/all_to_all | solution.py:381
  73.9 0.0 collective-permute-done.9.refs_4_
  73.9 2.6 %shard_map.77.first_ref = f32[1024,128]{1,0:T(8,128)S(1)} custom-call(s32[1]{0:T(128)} %bitcast.6.place_ref, bf16[8,128,128]{2,1,0:T(8,128)(2,1)} %get-tuple-element.34.y_ref, bf16[2,1024,128]{2,1,0:T(8,128)(2,1)S(1)} %copy-done.1, bf16[2,1024,128]{2,1,0:T(8,128)(2,1)S(1)} %collective-permute-done.refs_1_, ...), custom_call_target="tpu_custom_call" | custom-call | flops 2000000000 | bytes 4000000 | tf_op jit(solution)/shard_map/pallas_call | solution.py:281
  76.5 4.9 %collective-permute-done.7.part2 = bf16[8,128,128]{2,1,0:T(8,128)(2,1)} collective-permute-done((bf16[8,128,128]{2,1,0:T(8,128)(2,1)}, bf16[8,128,128]{2,1,0:T(8,128)(2,1)}, u32[]{:S(2)}, u32[]{:S(2)}) %collective-permute-start.7) | collective-permute-done | bytes 262176 | tf_op jit(solution)/shard_map/ppermute | solution.py:373
  81.4 2.1 %collective-permute-done.8.part3 = bf16[8,128,128]{2,1,0:T(8,128)(2,1)} collective-permute-done((bf16[8,128,128]{2,1,0:T(8,128)(2,1)}, bf16[8,128,128]{2,1,0:T(8,128)(2,1)}, u32[]{:S(2)}, u32[]{:S(2)}) %collective-permute-start.8) | collective-permute-done | bytes 262176 | tf_op jit(solution)/shard_map/ppermute | solution.py:373
  83.5 4.1 %shard_map.78 = (bf16[256,8,128]{2,1,0:T(8,128)(2,1)}, bf16[4,128,128]{2,1,0:T(8,128)(2,1)S(1)}, bf16[4,128,128]{2,1,0:T(8,128)(2,1)S(1)}) custom-call(s32[1]{0:T(128)} %bitcast.6.place_ref, f32[8,128,128]{2,1,0:T(8,128)S(1)} %copy-done.5, bf16[8,128,128]{2,1,0:T(8,128)(2,1)} %collective-permute-done.6.part1, ...), custom_call_target="tpu_custom_call" | custom-call | flops 2000000000 | bytes 4000000 | tf_op jit(solution)/shard_map/pallas_call | solution.py:281
  87.6 0.0 copy-start.2
  87.6 0.6 copy-done.2
  88.3 0.0 all-to-all-done.2.y_ref
  88.3 14.1 %all-to-all-start.3 = ((bf16[256,8,128]{2,1,0:T(8,128)(2,1)}), bf16[256,8,128]{2,1,0:T(8,128)(2,1)S(1)}, u32[]{:S(2)}, u32[]{:S(2)}) async-start(bf16[256,8,128]{2,1,0:T(8,128)(2,1)} %get-tuple-element.50), calls=%async_computation.3 | async-start | bytes 1048576 | tf_op jit(solution)/shard_map/all_to_all | solution.py:410
  102.4 2.2 %collective-permute-start.13 = (bf16[4,128,128]{2,1,0:T(8,128)(2,1)}, bf16[4,128,128]{2,1,0:T(8,128)(2,1)S(1)}, u32[]{:S(2)}, u32[]{:S(2)}) collective-permute-start(bf16[4,128,128]{2,1,0:T(8,128)(2,1)} %copy-done.2), channel_id=1, source_target_pairs={{0,8},{8,0},{16,24},{24,16},{32,40},{40,32},{48,56},{56,48},{1,9},... | collective-permute-start | bytes 393224 | tf_op jit(solution)/shard_map/ppermute | solution.py:373
  104.6 1.2 collective-permute-done.13.got_ref
  105.8 0.1 collective-permute-start.14
  105.9 2.0 %collective-permute-start.15 = (bf16[2,128,128]{2,1,0:T(8,128)(2,1)S(1)}, bf16[2,128,128]{2,1,0:T(8,128)(2,1)S(1)}, u32[]{:S(2)}, u32[]{:S(2)}) collective-permute-start(bf16[2,128,128]{2,1,0:T(8,128)(2,1)S(1)} %get-tuple-element.47), channel_id=1, source_target_pairs={{0,32},{8,40},{16,48},{24,56},{32,0},{40,8},{48,16},{56,24},{1,33}... | collective-permute-start | bytes 196616 | tf_op jit(solution)/shard_map/ppermute | solution.py:373
  107.9 1.9 %collective-permute-start.16 = (bf16[2,128,128]{2,1,0:T(8,128)(2,1)S(1)}, bf16[2,128,128]{2,1,0:T(8,128)(2,1)S(1)}, u32[]{:S(2)}, u32[]{:S(2)}) collective-permute-start(bf16[2,128,128]{2,1,0:T(8,128)(2,1)S(1)} %get-tuple-element.48), channel_id=1, source_target_pairs={{0,48},{8,56},{16,32},{24,40},{32,16},{40,24},{48,0},{56,8},{1,49}... | collective-permute-start | bytes 196616 | tf_op jit(solution)/shard_map/ppermute | solution.py:373
  109.8 2.2 %copy-done = bf16[4,1024,512]{2,1,0:T(8,128)(2,1)S(1)} copy-done((bf16[4,1024,512]{2,1,0:T(8,128)(2,1)S(1)}, bf16[4,1024,512]{2,1,0:T(8,128)(2,1)}, u32[]{:S(2)}) %copy-start) | copy-done | bytes 4194328
  111.9 1.2 shard_map.76
  113.2 0.0 collective-permute-done.15.refs_1_
  113.2 2.6 %collective-permute-done.16.refs_2_ = bf16[2,128,128]{2,1,0:T(8,128)(2,1)S(1)} collective-permute-done((bf16[2,128,128]{2,1,0:T(8,128)(2,1)S(1)}, bf16[2,128,128]{2,1,0:T(8,128)(2,1)S(1)}, u32[]{:S(2)}, u32[]{:S(2)}) %collective-permute-start.16) | collective-permute-done | bytes 65568 | tf_op jit(solution)/shard_map/ppermute | solution.py:373
  115.8 1.5 %shard_map.80 = bf16[128,1024]{1,0:T(8,128)(2,1)} custom-call(s32[1]{0:T(128)} %bitcast.6.place_ref, bf16[4,128,128]{2,1,0:T(8,128)(2,1)S(1)} %get-tuple-element.44.keep_ref, bf16[4,128,128]{2,1,0:T(8,128)(2,1)S(1)} %collective-permute-done.13.got_ref, bf16[2,128,128]{2,1,0:T(8,128)(2,1)S(1)} %collective-permute-done.14.refs_0_, ...), custom_call_target="tpu_custom_call" | custom-call | flops 500000000 | bytes 4000000 | tf_op jit(solution)/shard_map/pallas_call | solution.py:350
  117.4 6.4 %all-to-all-done.3.in_ref = bf16[256,8,128]{2,1,0:T(8,128)(2,1)S(1)} async-done(((bf16[256,8,128]{2,1,0:T(8,128)(2,1)}), bf16[256,8,128]{2,1,0:T(8,128)(2,1)S(1)}, u32[]{:S(2)}, u32[]{:S(2)}) %all-to-all-start.3) | async-done | bytes 524320 | tf_op jit(solution)/shard_map/all_to_all | solution.py:410
  123.8 0.8 shard_map.81
  (16 shorter events, 0.0 us)
Async XLA Ops:
  0.6 27.0 %copy-start.6 = (s32[1,32,27]{1,0,2:T(1,128)S(1)}, s32[1,32,27]{1,0,2:T(1,128)}, u32[]{:S(2)}) copy-start(s32[1,32,27]{1,0,2:T(1,128)} %param.8) | copy-start | bytes 10372
  0.6 34.6 %copy-start.3 = (s32[1,32]{1,0:T(1,128)S(1)}, s32[1,32]{1,0:T(1,128)}, u32[]{:S(2)}) copy-start(s32[1,32]{1,0:T(1,128)} %param.9) | copy-start | bytes 388
  18.6 12.9 %collective-permute-start.3 = (bf16[8,128,128]{2,1,0:T(8,128)(2,1)S(1)}, bf16[8,128,128]{2,1,0:T(8,128)(2,1)S(1)}, u32[]{:S(2)}, u32[]{:S(2)}) collective-permute-start(bf16[8,128,128]{2,1,0:T(8,128)(2,1)S(1)} %all_to_all.20.kv0), channel_id=1, source_target_pairs={{0,64},{64,0},{128,192},{192,128},{1,65},{65,1},{129,193},{193,129... | collective-permute-start | bytes 786440 | tf_op jit(solution)/shard_map/ppermute | solution.py:373
  19.2 15.2 %collective-permute-start.4 = (bf16[8,128,128]{2,1,0:T(8,128)(2,1)S(1)}, bf16[8,128,128]{2,1,0:T(8,128)(2,1)S(1)}, u32[]{:S(2)}, u32[]{:S(2)}) collective-permute-start(bf16[8,128,128]{2,1,0:T(8,128)(2,1)S(1)} %all_to_all.20.kv0), channel_id=1, source_target_pairs={{0,128},{64,192},{128,0},{192,64},{1,129},{65,193},{129,1},{193,65... | collective-permute-start | bytes 786440 | tf_op jit(solution)/shard_map/ppermute | solution.py:373
  21.8 13.4 %collective-permute-start.5 = (bf16[8,128,128]{2,1,0:T(8,128)(2,1)S(1)}, bf16[8,128,128]{2,1,0:T(8,128)(2,1)S(1)}, u32[]{:S(2)}, u32[]{:S(2)}) collective-permute-start(bf16[8,128,128]{2,1,0:T(8,128)(2,1)S(1)} %all_to_all.20.kv0), channel_id=1, source_target_pairs={{0,192},{64,128},{128,64},{192,0},{1,193},{65,129},{129,65},{193,1... | collective-permute-start | bytes 786440 | tf_op jit(solution)/shard_map/ppermute | solution.py:373
  22.5 11.9 %all-to-all-start.1 = ((bf16[8,128,128]{2,1,0:T(8,128)(2,1)}), bf16[8,128,128]{2,1,0:T(8,128)(2,1)S(1)}, u32[]{:S(2)}, u32[]{:S(2)}) async-start(bf16[8,128,128]{2,1,0:T(8,128)(2,1)} %get-tuple-element.31), calls=%async_computation.1 | async-start | bytes 524288 | tf_op jit(solution)/shard_map/all_to_all | solution.py:381
  27.7 33.5 %collective-permute-start = (bf16[2,1024,128]{2,1,0:T(8,128)(2,1)}, bf16[2,1024,128]{2,1,0:T(8,128)(2,1)S(1)}, u32[]{:S(2)}, u32[]{:S(2)}) collective-permute-start(bf16[2,1024,128]{2,1,0:T(8,128)(2,1)} %get-tuple-element.40.refs_0_), channel_id=1, source_target_pairs={{0,16},{8,24},{16,0},{24,8},{32,48},{40,56},{48,32},{56,40},{1,17}... | collective-permute-start | bytes 1572872 | tf_op jit(solution)/shard_map/ppermute | solution.py:373
  29.1 32.1 %collective-permute-start.1 = (bf16[2,1024,128]{2,1,0:T(8,128)(2,1)}, bf16[2,1024,128]{2,1,0:T(8,128)(2,1)S(1)}, u32[]{:S(2)}, u32[]{:S(2)}) collective-permute-start(bf16[2,1024,128]{2,1,0:T(8,128)(2,1)} %get-tuple-element.40.refs_0_), channel_id=1, source_target_pairs={{0,32},{8,40},{16,48},{24,56},{32,0},{40,8},{48,16},{56,24},{1,33}... | collective-permute-start | bytes 1572872 | tf_op jit(solution)/shard_map/ppermute | solution.py:373
  31.6 29.7 %collective-permute-start.2 = (bf16[2,1024,128]{2,1,0:T(8,128)(2,1)}, bf16[2,1024,128]{2,1,0:T(8,128)(2,1)S(1)}, u32[]{:S(2)}, u32[]{:S(2)}) collective-permute-start(bf16[2,1024,128]{2,1,0:T(8,128)(2,1)} %get-tuple-element.40.refs_0_), channel_id=1, source_target_pairs={{0,48},{8,56},{16,32},{24,40},{32,16},{40,24},{48,0},{56,8},{1,49}... | collective-permute-start | bytes 1572872 | tf_op jit(solution)/shard_map/ppermute | solution.py:373
  35.2 28.8 %copy-start.1 = (bf16[2,1024,128]{2,1,0:T(8,128)(2,1)S(1)}, bf16[2,1024,128]{2,1,0:T(8,128)(2,1)}, u32[]{:S(2)}) copy-start(bf16[2,1024,128]{2,1,0:T(8,128)(2,1)} %get-tuple-element.40.refs_0_) | copy-start | bytes 1572868
  60.5 0.8 copy-start.4
  61.3 3.8 %collective-permute-start.10 = (bf16[2,1024,128]{2,1,0:T(8,128)(2,1)S(1)}, bf16[2,1024,128]{2,1,0:T(8,128)(2,1)S(1)}, u32[]{:S(2)}, u32[]{:S(2)}) collective-permute-start(bf16[2,1024,128]{2,1,0:T(8,128)(2,1)S(1)} %collective-permute-done.refs_1_), channel_id=1, source_target_pairs={{0,8},{8,0},{16,24},{24,16},{32,40},{40,32},{48,56},{56,48},{1,9},... | collective-permute-start | bytes 1572872 | tf_op jit(solution)/shard_map/ppermute | solution.py:373
  63.5 6.0 %collective-permute-start.11 = (bf16[2,1024,128]{2,1,0:T(8,128)(2,1)S(1)}, bf16[2,1024,128]{2,1,0:T(8,128)(2,1)S(1)}, u32[]{:S(2)}, u32[]{:S(2)}) collective-permute-start(bf16[2,1024,128]{2,1,0:T(8,128)(2,1)S(1)} %collective-permute-done.1.refs_2_), channel_id=1, source_target_pairs={{0,8},{8,0},{16,24},{24,16},{32,40},{40,32},{48,56},{56,48},{1,9},... | collective-permute-start | bytes 1572872 | tf_op jit(solution)/shard_map/ppermute | solution.py:373
  63.6 10.3 %collective-permute-start.12 = (bf16[2,1024,128]{2,1,0:T(8,128)(2,1)S(1)}, bf16[2,1024,128]{2,1,0:T(8,128)(2,1)}, u32[]{:S(2)}, u32[]{:S(2)}) collective-permute-start(bf16[2,1024,128]{2,1,0:T(8,128)(2,1)S(1)} %collective-permute-done.2.refs_3_), channel_id=1, source_target_pairs={{0,8},{8,0},{16,24},{24,16},{32,40},{40,32},{48,56},{56,48},{1,9},... | collective-permute-start | bytes 1572872 | tf_op jit(solution)/shard_map/ppermute | solution.py:373
  64.0 9.9 %collective-permute-start.9 = (bf16[2,1024,128]{2,1,0:T(8,128)(2,1)S(1)}, bf16[2,1024,128]{2,1,0:T(8,128)(2,1)}, u32[]{:S(2)}, u32[]{:S(2)}) collective-permute-start(bf16[2,1024,128]{2,1,0:T(8,128)(2,1)S(1)} %copy-done.1), channel_id=1, source_target_pairs={{0,8},{8,0},{16,24},{24,16},{32,40},{40,32},{48,56},{56,48},{1,9},... | collective-permute-start | bytes 1572872 | tf_op jit(solution)/shard_map/ppermute | solution.py:373
  64.1 12.4 %collective-permute-start.6 = (bf16[8,128,128]{2,1,0:T(8,128)(2,1)}, bf16[8,128,128]{2,1,0:T(8,128)(2,1)}, u32[]{:S(2)}, u32[]{:S(2)}) collective-permute-start(bf16[8,128,128]{2,1,0:T(8,128)(2,1)} %get-tuple-element.37), channel_id=1, source_target_pairs={{0,64},{64,0},{128,192},{192,128},{1,65},{65,1},{129,193},{193,129... | collective-permute-start | bytes 786440 | tf_op jit(solution)/shard_map/ppermute | solution.py:373
  65.0 16.4 %collective-permute-start.7 = (bf16[8,128,128]{2,1,0:T(8,128)(2,1)}, bf16[8,128,128]{2,1,0:T(8,128)(2,1)}, u32[]{:S(2)}, u32[]{:S(2)}) collective-permute-start(bf16[8,128,128]{2,1,0:T(8,128)(2,1)} %get-tuple-element.38), channel_id=1, source_target_pairs={{0,128},{64,192},{128,0},{192,64},{1,129},{65,193},{129,1},{193,65... | collective-permute-start | bytes 786440 | tf_op jit(solution)/shard_map/ppermute | solution.py:373
  69.5 14.0 %collective-permute-start.8 = (bf16[8,128,128]{2,1,0:T(8,128)(2,1)}, bf16[8,128,128]{2,1,0:T(8,128)(2,1)}, u32[]{:S(2)}, u32[]{:S(2)}) collective-permute-start(bf16[8,128,128]{2,1,0:T(8,128)(2,1)} %get-tuple-element.39), channel_id=1, source_target_pairs={{0,192},{64,128},{128,64},{192,0},{1,193},{65,129},{129,65},{193,1... | collective-permute-start | bytes 786440 | tf_op jit(solution)/shard_map/ppermute | solution.py:373
  69.9 18.3 %all-to-all-start.2 = ((bf16[8,128,128]{2,1,0:T(8,128)(2,1)}), bf16[8,128,128]{2,1,0:T(8,128)(2,1)S(1)}, u32[]{:S(2)}, u32[]{:S(2)}) async-start(bf16[8,128,128]{2,1,0:T(8,128)(2,1)} %get-tuple-element.34.y_ref), calls=%async_computation.2 | async-start | bytes 524288 | tf_op jit(solution)/shard_map/all_to_all | solution.py:381
  73.9 9.6 %copy-start.5 = (f32[8,128,128]{2,1,0:T(8,128)S(1)}, f32[8,128,128]{2,1,0:T(8,128)}, u32[]{:S(2)}) copy-start(f32[8,128,128]{2,1,0:T(8,128)} %copy-done.4) | copy-start | bytes 1572868
  87.6 0.7 copy-start.2
  88.3 35.5 %all-to-all-start.3 = ((bf16[256,8,128]{2,1,0:T(8,128)(2,1)}), bf16[256,8,128]{2,1,0:T(8,128)(2,1)S(1)}, u32[]{:S(2)}, u32[]{:S(2)}) async-start(bf16[256,8,128]{2,1,0:T(8,128)(2,1)} %get-tuple-element.50), calls=%async_computation.3 | async-start | bytes 1048576 | tf_op jit(solution)/shard_map/all_to_all | solution.py:410
  102.4 3.4 %collective-permute-start.13 = (bf16[4,128,128]{2,1,0:T(8,128)(2,1)}, bf16[4,128,128]{2,1,0:T(8,128)(2,1)S(1)}, u32[]{:S(2)}, u32[]{:S(2)}) collective-permute-start(bf16[4,128,128]{2,1,0:T(8,128)(2,1)} %copy-done.2), channel_id=1, source_target_pairs={{0,8},{8,0},{16,24},{24,16},{32,40},{40,32},{48,56},{56,48},{1,9},... | collective-permute-start | bytes 393224 | tf_op jit(solution)/shard_map/ppermute | solution.py:373
  105.8 7.4 %collective-permute-start.14 = (bf16[2,128,128]{2,1,0:T(8,128)(2,1)S(1)}, bf16[2,128,128]{2,1,0:T(8,128)(2,1)S(1)}, u32[]{:S(2)}, u32[]{:S(2)}) collective-permute-start(bf16[2,128,128]{2,1,0:T(8,128)(2,1)S(1)} %get-tuple-element.46), channel_id=1, source_target_pairs={{0,16},{8,24},{16,0},{24,8},{32,48},{40,56},{48,32},{56,40},{1,17}... | collective-permute-start | bytes 196616 | tf_op jit(solution)/shard_map/ppermute | solution.py:373
  105.9 7.3 %collective-permute-start.15 = (bf16[2,128,128]{2,1,0:T(8,128)(2,1)S(1)}, bf16[2,128,128]{2,1,0:T(8,128)(2,1)S(1)}, u32[]{:S(2)}, u32[]{:S(2)}) collective-permute-start(bf16[2,128,128]{2,1,0:T(8,128)(2,1)S(1)} %get-tuple-element.47), channel_id=1, source_target_pairs={{0,32},{8,40},{16,48},{24,56},{32,0},{40,8},{48,16},{56,24},{1,33}... | collective-permute-start | bytes 196616 | tf_op jit(solution)/shard_map/ppermute | solution.py:373
  107.9 7.9 %collective-permute-start.16 = (bf16[2,128,128]{2,1,0:T(8,128)(2,1)S(1)}, bf16[2,128,128]{2,1,0:T(8,128)(2,1)S(1)}, u32[]{:S(2)}, u32[]{:S(2)}) collective-permute-start(bf16[2,128,128]{2,1,0:T(8,128)(2,1)S(1)} %get-tuple-element.48), channel_id=1, source_target_pairs={{0,48},{8,56},{16,32},{24,40},{32,16},{40,24},{48,0},{56,8},{1,49}... | collective-permute-start | bytes 196616 | tf_op jit(solution)/shard_map/ppermute | solution.py:373
  109.7 2.2 %copy-start = (bf16[4,1024,512]{2,1,0:T(8,128)(2,1)S(1)}, bf16[4,1024,512]{2,1,0:T(8,128)(2,1)}, u32[]{:S(2)}) copy-start(bf16[4,1024,512]{2,1,0:T(8,128)(2,1)} %refs_5_.1) | copy-start | bytes 12582916

commit v2 on v1

--- a/solution.py
+++ b/solution.py
@@ -10,7 +10,7 @@
 HEAD_DIM = 64
 BLOCK = 128
 MAXN = 27
-GROUP = 4
+LARGE, SMALL = 8, 4
 SLOTS = 28
 BF = jnp.bfloat16
 F32 = jnp.float32
@@ -99,7 +99,7 @@
     lists_ref, counts_ref, group_ref,
     qd_ref, kv0, kv1, kv2, kv3,
     y_ref, out0, out1, out2, out3,
-    kvs, kvt, acc, s_scr, p_scr, places, sems,
+    kvs, kvt, acc, s_scr, p_scr, ds_scr, n_scr, w_in, w_back, places, sems,
 ):
     step = pl.program_id(0)
     group = group_ref[0]
@@ -120,7 +120,14 @@
                 kvt[idx] = kvs[idx].T
 
     count = counts_ref[block]
-    trips = (count + GROUP - 1) // GROUP
+    large = (count + SMALL - 1) // LARGE
+    small = (count - large * LARGE + SMALL - 1) // SMALL
+
+    def sweep(visit, carry):
+        carry = lax.fori_loop(0, large, lambda i, c: visit(LARGE, i * LARGE, c), carry)
+        return lax.fori_loop(
+            0, small, lambda i, c: visit(SMALL, large * LARGE + i * SMALL, c), carry
+        )
 
     def place(slot):
         raw = lists_ref[block, jnp.minimum(slot, MAXN - 1)]
@@ -134,66 +141,60 @@
     upper = lax.broadcasted_iota(jnp.int32, (128, 128), 0) < HEAD_DIM
     left = lax.broadcasted_iota(jnp.int32, (128, 128), 1) < HEAD_DIM
     zero = jnp.zeros((128, 128), BF)
-    w_in = jnp.concatenate([jnp.where(upper, qdt, zero), jnp.where(upper, zero, qdt)], axis=1)
-    w_back = jnp.concatenate([jnp.where(left, qd, zero), jnp.where(left, zero, qd)], axis=0)
-    span = GROUP * 128
-
-    def scores(trip, top):
-        stack = jnp.concatenate(
-            [kvs[place(trip * GROUP + i)] for i in range(GROUP)], axis=0
-        )
-        both = dot(stack, w_in)
-        base = pl.multiple_of(trip * span, span)
-        s_scr[pl.ds(base, span), :] = both[:, :128]
-        p_scr[pl.ds(base, span), :] = both[:, 128:]
-        return jnp.maximum(top, jnp.max(both[:, :128].reshape(span // 8, 8, 128), axis=0))
-
-    top = lax.fori_loop(0, trips, scores, jnp.full((8, 128), -3e38, F32))
+    w_in[:, :128] = jnp.where(upper, qdt, zero)
+    w_in[:, 128:] = jnp.where(upper, zero, qdt)
+    w_back[:128] = jnp.where(left, qd, zero)
+    w_back[128:] = jnp.where(left, zero, qd)
+
+    def rows_of(slot, size):
+        return pl.ds(pl.multiple_of(slot * 128, 128), size * 128)
+
+    def scores(size, slot, top):
+        stack = jnp.concatenate([kvs[place(slot + i)] for i in range(size)], axis=0)
+        both = dot(stack, w_in[...])
+        s_scr[rows_of(slot, size), :] = both[:, :128]
+        p_scr[rows_of(slot, size), :] = both[:, 128:]
+        return jnp.maximum(top, jnp.max(both[:, :128].reshape(size * 16, 8, 128), axis=0))
+
+    top = sweep(scores, jnp.full((8, 128), -3e38, F32))
     row_max = jnp.max(top, axis=0, keepdims=True)
 
-    def mix(trip, carry):
+    def mix(size, slot, carry):
         total, mixed = carry
-        base = pl.multiple_of(trip * span, span)
         parts, values = [], []
-        for i in range(GROUP):
-            slot = trip * GROUP + i
-            shift = jnp.where(slot < count, row_max, 1e30)
-            e = jnp.exp(s_scr[pl.ds(base + i * 128, 128), :] - shift)
-            s_scr[pl.ds(base + i * 128, 128), :] = e
+        for i in range(size):
+            shift = jnp.where(slot + i < count, row_max, 1e30)
+            e = jnp.exp(s_scr[rows_of(slot + i, 1), :] - shift)
+            s_scr[rows_of(slot + i, 1), :] = e
             total = total + jnp.sum(e.reshape(16, 8, 128), axis=0)
             parts.append(e.astype(BF))
-            values.append(kvt[places[slot], HEAD_DIM:, :])
+            values.append(kvt[places[slot + i], HEAD_DIM:, :])
         mixed = mixed + dot(jnp.concatenate(values, axis=1), jnp.concatenate(parts, axis=0))
         return total, mixed
 
-    total, mixed = lax.fori_loop(
-        0, trips, mix, (jnp.zeros((8, 128), F32), jnp.zeros((HEAD_DIM, 128), F32))
-    )
+    total, mixed = sweep(mix, (jnp.zeros((8, 128), F32), jnp.zeros((HEAD_DIM, 128), F32)))
     inverse = 1.0 / jnp.sum(total, axis=0, keepdims=True)
     attended = (mixed * inverse).astype(BF)
     delta = jnp.sum(
         qdt[HEAD_DIM:, :].astype(F32) * attended.astype(F32), axis=0, keepdims=True
     )
 
-    def back(trip, dq):
-        base = pl.multiple_of(trip * span, span)
-        dss, pairs, keys, targets = [], [], [], []
-        for i in range(GROUP):
-            rows = pl.ds(base + i * 128, 128)
+    def back(size, slot, dq):
+        keys = []
+        for i in range(size):
+            rows, here = rows_of(slot + i, 1), slice(i * 128, (i + 1) * 128)
             normed = s_scr[rows, :] * inverse
-            ds = (normed * (p_scr[rows, :] - delta)).astype(BF)
-            dss.append(ds)
-            pairs.append(jnp.concatenate([ds, normed.astype(BF)], axis=1))
-            where = places[trip * GROUP + i]
-            targets.append(where)
-            keys.append(kvt[where, :HEAD_DIM, :])
-        dq = dq + dot(jnp.concatenate(keys, axis=1), jnp.concatenate(dss, axis=0))
-        grads = dot(jnp.concatenate(pairs, axis=0), w_back)
-        for i in range(GROUP):
-            acc[targets[i]] += grads[i * 128 : (i + 1) * 128]
+            ds_scr[here, :] = (normed * (p_scr[rows, :] - delta)).astype(BF)
+            n_scr[here, :] = normed.astype(BF)
+            keys.append(kvt[places[slot + i], :HEAD_DIM, :])
+        span = slice(0, size * 128)
+        dq = dq + dot(jnp.concatenate(keys, axis=1), ds_scr[span, :])
+        grads = dot(jnp.concatenate([ds_scr[span, :], n_scr[span, :]], axis=1), w_back[...])
+        for i in range(size):
+            acc[places[slot + i]] += grads[i * 128 : (i + 1) * 128]
         return dq
 
-    dq = lax.fori_loop(0, trips, back, jnp.zeros((HEAD_DIM, 128), F32))
+    dq = sweep(back, jnp.zeros((HEAD_DIM, 128), F32))
     y_ref[0] = jnp.concatenate([dq * 0.125, attended.astype(F32)], axis=0).T.astype(BF)
 
     @pl.when(step == 7)
@@ -221,6 +222,10 @@
                 pltpu.VMEM((32, 128, 128), F32),
                 pltpu.VMEM((SLOTS * 128, 128), F32),
                 pltpu.VMEM((SLOTS * 128, 128), F32),
+                pltpu.VMEM((LARGE * 128, 128), BF),
+                pltpu.VMEM((LARGE * 128, 128), BF),
+                pltpu.VMEM((128, 256), BF),
+                pltpu.VMEM((256, 128), BF),
                 pltpu.SMEM((SLOTS,), jnp.int32),
                 pltpu.SemaphoreType.DMA((4,)),
             ],

time: 125 us -> 119 us (0.952)
  Pallas kernels: 40.4 us -> 35.9 us
  starting transfers between devices: 44.9 us -> 43.3 us
    pallas_call x1, Pallas kernels: 25.2 us -> 20.7 us  [attend(): pl.pallas_call(attend_kernel, grid_spec=pltpu.PrefetchScalarGridSpec(num_...]
    ppermute x17, starting transfers between devices: 21.6 us -> 20 us  [across(): lax.ppermute(array, axes, [(i, i ^ flip) for i in range(lax.axis_size(axe...]
  transfers between devices with their start and end apart: 20 -> 20, of which waited for: 8 -> 8; matrix products, arithmetic and copies ran while one was open for 0% -> 0% of each run, Pallas kernels for 28% -> 26%
where the time goes in v2:
time: 119 us; the launch traced here: 118 us
  starting transfers between devices  43.3 us (36%)
  Pallas kernels  35.9 us (30%)
  waiting for transfers between devices  21.6 us (18%)
  blocking collectives  13 us (11%)
  local copies, waits for them, and re-layouts  3.72 us (3%)
    pallas_call x1, Pallas kernels, attend(): pl.pallas_call(attend_kernel, grid_spec=pltpu.PrefetchScalarGridSpec(num_...  20.7 us
    ppermute x17, starting transfers between devices, across(): lax.ppermute(array, axes, [(i, i ^ flip) for i in range(lax.axis_size(axe...  20 us
    all_to_all x1, starting transfers between devices, body(): terms = lax.all_to_all(terms, SEQ + ('rep',), 0, 0, tiled=True)  13.9 us
    all_to_all x1, blocking collectives, body(): swap = lambda array: lax.all_to_all(array, HEAD, 0, 0, tiled=True)  13 us
    ppermute x17, waiting for transfers between devices, across(): lax.ppermute(array, axes, [(i, i ^ flip) for i in range(lax.axis_size(axe...  12.4 us
    all_to_all x2, starting transfers between devices, body(): swap = lambda array: lax.all_to_all(array, HEAD, 0, 0, tiled=True)  9.42 us
    pallas_call x2, Pallas kernels, grads_call(): pl.pallas_call(kernel, in_specs=[pl.BlockSpec(memory_space=pltpu.SMEM)] +...  6.69 us
    all_to_all x1, waiting for transfers between devices, body(): terms = lax.all_to_all(terms, SEQ + ('rep',), 0, 0, tiled=True)  6.43 us
  transfers between devices with their start and end apart: 20, of which 8 were waited for; matrix products, arithmetic and copies ran while one was open for 0% of the time, Pallas kernels for 26%

profile of v2, /device:TPU:1, one launch (start us, length us, event | category | flops | bytes accessed | tf_op | source)
XLA Modules:
  0.0 118.2 jit_solution(6306392813219801443)
XLA Ops:
  0.7 5.0 %project.1 = (bf16[8,128,128]{2,1,0:T(8,128)(2,1)}, bf16[8,128,128]{2,1,0:T(8,128)(2,1)}, bf16[2,1024,128]{2,1,0:T(8,128)(2,1)}) custom-call(bf16[128,1024]{1,0:T(8,128)(2,1)} %bitcast.10, bf16[128,1024]{1,0:T(8,128)(2,1)} %bitcast.11, bf16[4,1024,512]{2,1,0:T(8,128)(2,1)} %refs_5_.1), custom_call_target="tpu_custom_call" | custom-call | tf_op jit(solution)/shard_map/project/pallas_call | solution.py:73
  5.6 13.0 %all_to_all.20.kv0 = bf16[8,128,128]{2,1,0:T(8,128)(2,1)S(1)} all-to-all(bf16[8,128,128]{2,1,0:T(8,128)(2,1)} %get-tuple-element.29), channel_id=1, replica_groups=mesh['row'=4,'head'=8,'rep'=8] {'head'}, dimensions={0} | all-to-all | bytes 524288 | tf_op jit(solution)/shard_map/all_to_all | solution.py:386
  18.6 0.6 collective-permute-start.3
  19.2 2.6 %collective-permute-start.4 = (bf16[8,128,128]{2,1,0:T(8,128)(2,1)S(1)}, bf16[8,128,128]{2,1,0:T(8,128)(2,1)S(1)}, u32[]{:S(2)}, u32[]{:S(2)}) collective-permute-start(bf16[8,128,128]{2,1,0:T(8,128)(2,1)S(1)} %all_to_all.20.kv0), channel_id=1, source_target_pairs={{0,128},{64,192},{128,0},{192,64},{1,129},{65,193},{129,1},{193,65... | collective-permute-start | bytes 786440 | tf_op jit(solution)/shard_map/ppermute | solution.py:378
  21.8 0.7 collective-permute-start.5
  22.5 5.2 %all-to-all-start.1 = ((bf16[8,128,128]{2,1,0:T(8,128)(2,1)}), bf16[8,128,128]{2,1,0:T(8,128)(2,1)S(1)}, u32[]{:S(2)}, u32[]{:S(2)}) async-start(bf16[8,128,128]{2,1,0:T(8,128)(2,1)} %get-tuple-element.31), calls=%async_computation.1 | async-start | bytes 524288 | tf_op jit(solution)/shard_map/all_to_all | solution.py:386
  27.7 0.1 copy.8
  27.7 1.4 %collective-permute-start = (bf16[2,1024,128]{2,1,0:T(8,128)(2,1)}, bf16[2,1024,128]{2,1,0:T(8,128)(2,1)S(1)}, u32[]{:S(2)}, u32[]{:S(2)}) collective-permute-start(bf16[2,1024,128]{2,1,0:T(8,128)(2,1)} %get-tuple-element.40.refs_0_), channel_id=1, source_target_pairs={{0,16},{8,24},{16,0},{24,8},{32,48},{40,56},{48,32},{56,40},{1,17}... | collective-permute-start | bytes 1572872 | tf_op jit(solution)/shard_map/ppermute | solution.py:378
  29.1 2.4 %collective-permute-start.1 = (bf16[2,1024,128]{2,1,0:T(8,128)(2,1)}, bf16[2,1024,128]{2,1,0:T(8,128)(2,1)S(1)}, u32[]{:S(2)}, u32[]{:S(2)}) collective-permute-start(bf16[2,1024,128]{2,1,0:T(8,128)(2,1)} %get-tuple-element.40.refs_0_), channel_id=1, source_target_pairs={{0,32},{8,40},{16,48},{24,56},{32,0},{40,8},{48,16},{56,24},{1,33}... | collective-permute-start | bytes 1572872 | tf_op jit(solution)/shard_map/ppermute | solution.py:378
  31.6 0.1 collective-permute-start.2
  31.6 2.7 %all-to-all-done.1.qd_ref = bf16[8,128,128]{2,1,0:T(8,128)(2,1)S(1)} async-done(((bf16[8,128,128]{2,1,0:T(8,128)(2,1)}), bf16[8,128,128]{2,1,0:T(8,128)(2,1)S(1)}, u32[]{:S(2)}, u32[]{:S(2)}) %all-to-all-start.1) | async-done | bytes 262176 | tf_op jit(solution)/shard_map/all_to_all | solution.py:386
  34.4 0.8 collective-permute-done.5.kv3
  35.2 20.7 %attend.1 = (bf16[8,128,128]{2,1,0:T(8,128)(2,1)}, f32[8,128,128]{2,1,0:T(8,128)S(1)}, bf16[8,128,128]{2,1,0:T(8,128)(2,1)}, bf16[8,128,128]{2,1,0:T(8,128)(2,1)}, bf16[8,128,128]{2,1,0:T(8,128)(2,1)}) custom-call(s32[32,27]{1,0:T(8,128)S(1)} %bitcast.8, s32[32]{0:T(128)S(1)} %bitcast.9, s32[1]{0:T(128)} %bitcast.4.group_ref, ...), custom_call_target="tpu_custom_call" | custom-call | flops 30000001024 | bytes 4000000 | tf_op jit(solution)/shard_map/attend/pallas_call | solution.py:212
  55.9 0.8 copy-done.4
  56.7 0.0 collective-permute-done.refs_1_
  56.7 0.0 collective-permute-done.1.refs_2_
  56.8 0.0 collective-permute-done.2.refs_3_
  56.8 2.2 %collective-permute-start.10 = (bf16[2,1024,128]{2,1,0:T(8,128)(2,1)S(1)}, bf16[2,1024,128]{2,1,0:T(8,128)(2,1)S(1)}, u32[]{:S(2)}, u32[]{:S(2)}) collective-permute-start(bf16[2,1024,128]{2,1,0:T(8,128)(2,1)S(1)} %collective-permute-done.refs_1_), channel_id=1, source_target_pairs={{0,8},{8,0},{16,24},{24,16},{32,40},{40,32},{48,56},{56,48},{1,9},... | collective-permute-start | bytes 1572872 | tf_op jit(solution)/shard_map/ppermute | solution.py:378
  58.9 0.1 collective-permute-start.11
  59.0 0.4 collective-permute-start.12
  59.5 0.1 collective-permute-start.9
  59.6 0.0 collective-permute-start.6
  59.6 0.9 collective-permute-done.10.refs_5_
  60.5 2.8 %collective-permute-start.7 = (bf16[8,128,128]{2,1,0:T(8,128)(2,1)}, bf16[8,128,128]{2,1,0:T(8,128)(2,1)}, u32[]{:S(2)}, u32[]{:S(2)}) collective-permute-start(bf16[8,128,128]{2,1,0:T(8,128)(2,1)} %get-tuple-element.38), channel_id=1, source_target_pairs={{0,128},{64,192},{128,0},{192,64},{1,129},{65,193},{129,1},{193,65... | collective-permute-start | bytes 786440 | tf_op jit(solution)/shard_map/ppermute | solution.py:378
  63.3 0.0 collective-permute-done.11.refs_6_
  63.3 0.5 collective-permute-start.8
  63.8 4.2 %all-to-all-start.2 = ((bf16[8,128,128]{2,1,0:T(8,128)(2,1)}), bf16[8,128,128]{2,1,0:T(8,128)(2,1)S(1)}, u32[]{:S(2)}, u32[]{:S(2)}) async-start(bf16[8,128,128]{2,1,0:T(8,128)(2,1)} %get-tuple-element.34.y_ref), calls=%async_computation.2 | async-start | bytes 524288 | tf_op jit(solution)/shard_map/all_to_all | solution.py:386
  68.0 0.0 collective-permute-done.9.refs_4_
  68.0 2.6 %shard_map.77.first_ref = f32[1024,128]{1,0:T(8,128)S(1)} custom-call(s32[1]{0:T(128)} %bitcast.6.place_ref, bf16[8,128,128]{2,1,0:T(8,128)(2,1)} %get-tuple-element.34.y_ref, bf16[2,1024,128]{2,1,0:T(8,128)(2,1)S(1)} %copy-done.1, bf16[2,1024,128]{2,1,0:T(8,128)(2,1)S(1)} %collective-permute-done.refs_1_, ...), custom_call_target="tpu_custom_call" | custom-call | flops 2000000000 | bytes 4000000 | tf_op jit(solution)/shard_map/pallas_call | solution.py:286
  70.6 0.0 collective-permute-done.6.part1
  70.6 4.6 %collective-permute-done.7.part2 = bf16[8,128,128]{2,1,0:T(8,128)(2,1)} collective-permute-done((bf16[8,128,128]{2,1,0:T(8,128)(2,1)}, bf16[8,128,128]{2,1,0:T(8,128)(2,1)}, u32[]{:S(2)}, u32[]{:S(2)}) %collective-permute-start.7) | collective-permute-done | bytes 262176 | tf_op jit(solution)/shard_map/ppermute | solution.py:378
  75.2 2.1 %collective-permute-done.8.part3 = bf16[8,128,128]{2,1,0:T(8,128)(2,1)} collective-permute-done((bf16[8,128,128]{2,1,0:T(8,128)(2,1)}, bf16[8,128,128]{2,1,0:T(8,128)(2,1)}, u32[]{:S(2)}, u32[]{:S(2)}) %collective-permute-start.8) | collective-permute-done | bytes 262176 | tf_op jit(solution)/shard_map/ppermute | solution.py:378
  77.3 4.1 %shard_map.78 = (bf16[256,8,128]{2,1,0:T(8,128)(2,1)}, bf16[4,128,128]{2,1,0:T(8,128)(2,1)S(1)}, bf16[4,128,128]{2,1,0:T(8,128)(2,1)S(1)}) custom-call(s32[1]{0:T(128)} %bitcast.6.place_ref, f32[8,128,128]{2,1,0:T(8,128)S(1)} %copy-done.5, bf16[8,128,128]{2,1,0:T(8,128)(2,1)} %collective-permute-done.6.part1, ...), custom_call_target="tpu_custom_call" | custom-call | flops 2000000000 | bytes 4000000 | tf_op jit(solution)/shard_map/pallas_call | solution.py:286
  81.4 0.0 copy-start.2
  81.5 0.6 copy-done.2
  82.1 13.9 %all-to-all-start.3 = ((bf16[256,8,128]{2,1,0:T(8,128)(2,1)}), bf16[256,8,128]{2,1,0:T(8,128)(2,1)S(1)}, u32[]{:S(2)}, u32[]{:S(2)}) async-start(bf16[256,8,128]{2,1,0:T(8,128)(2,1)} %get-tuple-element.50), calls=%async_computation.3 | async-start | bytes 1048576 | tf_op jit(solution)/shard_map/all_to_all | solution.py:415
  96.0 2.2 %collective-permute-start.13 = (bf16[4,128,128]{2,1,0:T(8,128)(2,1)}, bf16[4,128,128]{2,1,0:T(8,128)(2,1)S(1)}, u32[]{:S(2)}, u32[]{:S(2)}) collective-permute-start(bf16[4,128,128]{2,1,0:T(8,128)(2,1)} %copy-done.2), channel_id=1, source_target_pairs={{0,8},{8,0},{16,24},{24,16},{32,40},{40,32},{48,56},{56,48},{1,9},... | collective-permute-start | bytes 393224 | tf_op jit(solution)/shard_map/ppermute | solution.py:378
  98.2 1.2 %collective-permute-done.13.got_ref = bf16[4,128,128]{2,1,0:T(8,128)(2,1)S(1)} collective-permute-done((bf16[4,128,128]{2,1,0:T(8,128)(2,1)}, bf16[4,128,128]{2,1,0:T(8,128)(2,1)S(1)}, u32[]{:S(2)}, u32[]{:S(2)}) %collective-permute-start.13) | collective-permute-done | bytes 131104 | tf_op jit(solution)/shard_map/ppermute | solution.py:378
  99.4 0.1 collective-permute-start.14
  99.5 2.0 %collective-permute-start.15 = (bf16[2,128,128]{2,1,0:T(8,128)(2,1)S(1)}, bf16[2,128,128]{2,1,0:T(8,128)(2,1)S(1)}, u32[]{:S(2)}, u32[]{:S(2)}) collective-permute-start(bf16[2,128,128]{2,1,0:T(8,128)(2,1)S(1)} %get-tuple-element.47), channel_id=1, source_target_pairs={{0,32},{8,40},{16,48},{24,56},{32,0},{40,8},{48,16},{56,24},{1,33}... | collective-permute-start | bytes 196616 | tf_op jit(solution)/shard_map/ppermute | solution.py:378
  101.5 1.9 %collective-permute-start.16 = (bf16[2,128,128]{2,1,0:T(8,128)(2,1)S(1)}, bf16[2,128,128]{2,1,0:T(8,128)(2,1)S(1)}, u32[]{:S(2)}, u32[]{:S(2)}) collective-permute-start(bf16[2,128,128]{2,1,0:T(8,128)(2,1)S(1)} %get-tuple-element.48), channel_id=1, source_target_pairs={{0,48},{8,56},{16,32},{24,40},{32,16},{40,24},{48,0},{56,8},{1,49}... | collective-permute-start | bytes 196616 | tf_op jit(solution)/shard_map/ppermute | solution.py:378
  103.4 2.2 %copy-done = bf16[4,1024,512]{2,1,0:T(8,128)(2,1)S(1)} copy-done((bf16[4,1024,512]{2,1,0:T(8,128)(2,1)S(1)}, bf16[4,1024,512]{2,1,0:T(8,128)(2,1)}, u32[]{:S(2)}) %copy-start) | copy-done | bytes 4194328
  105.6 1.2 %shard_map.76 = (bf16[128,1024]{1,0:T(8,128)(2,1)}, f32[128,1024]{1,0:T(8,128)S(1)}) custom-call(bf16[8,128,128]{2,1,0:T(8,128)(2,1)S(1)} %all-to-all-done.2.y_ref, bf16[4,1024,512]{2,1,0:T(8,128)(2,1)S(1)} %copy-done, bf16[4,1024,512]{2,1,0:T(8,128)(2,1)S(1)} %copy-done), custom_call_target="tpu_custom_call" | custom-call | flops 500000000 | bytes 4000000 | tf_op jit(solution)/shard_map/pallas_call | solution.py:355
  106.8 0.0 collective-permute-done.15.refs_1_
  106.8 2.6 %collective-permute-done.16.refs_2_ = bf16[2,128,128]{2,1,0:T(8,128)(2,1)S(1)} collective-permute-done((bf16[2,128,128]{2,1,0:T(8,128)(2,1)S(1)}, bf16[2,128,128]{2,1,0:T(8,128)(2,1)S(1)}, u32[]{:S(2)}, u32[]{:S(2)}) %collective-permute-start.16) | collective-permute-done | bytes 65568 | tf_op jit(solution)/shard_map/ppermute | solution.py:378
  109.5 1.5 %shard_map.80 = bf16[128,1024]{1,0:T(8,128)(2,1)} custom-call(s32[1]{0:T(128)} %bitcast.6.place_ref, bf16[4,128,128]{2,1,0:T(8,128)(2,1)S(1)} %get-tuple-element.44.keep_ref, bf16[4,128,128]{2,1,0:T(8,128)(2,1)S(1)} %collective-permute-done.13.got_ref, bf16[2,128,128]{2,1,0:T(8,128)(2,1)S(1)} %collective-permute-done.14.refs_0_, ...), custom_call_target="tpu_custom_call" | custom-call | flops 500000000 | bytes 4000000 | tf_op jit(solution)/shard_map/pallas_call | solution.py:355
  111.0 6.4 %all-to-all-done.3.in_ref = bf16[256,8,128]{2,1,0:T(8,128)(2,1)S(1)} async-done(((bf16[256,8,128]{2,1,0:T(8,128)(2,1)}), bf16[256,8,128]{2,1,0:T(8,128)(2,1)S(1)}, u32[]{:S(2)}, u32[]{:S(2)}) %all-to-all-start.3) | async-done | bytes 524320 | tf_op jit(solution)/shard_map/all_to_all | solution.py:415
  117.4 0.8 shard_map.81
  (16 shorter events, 0.0 us)
Async XLA Ops:
  0.6 27.0 %copy-start.6 = (s32[1,32,27]{1,0,2:T(1,128)S(1)}, s32[1,32,27]{1,0,2:T(1,128)}, u32[]{:S(2)}) copy-start(s32[1,32,27]{1,0,2:T(1,128)} %param.8) | copy-start | bytes 10372
  0.6 34.6 %copy-start.3 = (s32[1,32]{1,0:T(1,128)S(1)}, s32[1,32]{1,0:T(1,128)}, u32[]{:S(2)}) copy-start(s32[1,32]{1,0:T(1,128)} %param.9) | copy-start | bytes 388
  18.6 12.9 %collective-permute-start.3 = (bf16[8,128,128]{2,1,0:T(8,128)(2,1)S(1)}, bf16[8,128,128]{2,1,0:T(8,128)(2,1)S(1)}, u32[]{:S(2)}, u32[]{:S(2)}) collective-permute-start(bf16[8,128,128]{2,1,0:T(8,128)(2,1)S(1)} %all_to_all.20.kv0), channel_id=1, source_target_pairs={{0,64},{64,0},{128,192},{192,128},{1,65},{65,1},{129,193},{193,129... | collective-permute-start | bytes 786440 | tf_op jit(solution)/shard_map/ppermute | solution.py:378
  19.2 15.2 %collective-permute-start.4 = (bf16[8,128,128]{2,1,0:T(8,128)(2,1)S(1)}, bf16[8,128,128]{2,1,0:T(8,128)(2,1)S(1)}, u32[]{:S(2)}, u32[]{:S(2)}) collective-permute-start(bf16[8,128,128]{2,1,0:T(8,128)(2,1)S(1)} %all_to_all.20.kv0), channel_id=1, source_target_pairs={{0,128},{64,192},{128,0},{192,64},{1,129},{65,193},{129,1},{193,65... | collective-permute-start | bytes 786440 | tf_op jit(solution)/shard_map/ppermute | solution.py:378
  21.8 13.4 %collective-permute-start.5 = (bf16[8,128,128]{2,1,0:T(8,128)(2,1)S(1)}, bf16[8,128,128]{2,1,0:T(8,128)(2,1)S(1)}, u32[]{:S(2)}, u32[]{:S(2)}) collective-permute-start(bf16[8,128,128]{2,1,0:T(8,128)(2,1)S(1)} %all_to_all.20.kv0), channel_id=1, source_target_pairs={{0,192},{64,128},{128,64},{192,0},{1,193},{65,129},{129,65},{193,1... | collective-permute-start | bytes 786440 | tf_op jit(solution)/shard_map/ppermute | solution.py:378
  22.5 11.9 %all-to-all-start.1 = ((bf16[8,128,128]{2,1,0:T(8,128)(2,1)}), bf16[8,128,128]{2,1,0:T(8,128)(2,1)S(1)}, u32[]{:S(2)}, u32[]{:S(2)}) async-start(bf16[8,128,128]{2,1,0:T(8,128)(2,1)} %get-tuple-element.31), calls=%async_computation.1 | async-start | bytes 524288 | tf_op jit(solution)/shard_map/all_to_all | solution.py:386
  27.7 29.0 %collective-permute-start = (bf16[2,1024,128]{2,1,0:T(8,128)(2,1)}, bf16[2,1024,128]{2,1,0:T(8,128)(2,1)S(1)}, u32[]{:S(2)}, u32[]{:S(2)}) collective-permute-start(bf16[2,1024,128]{2,1,0:T(8,128)(2,1)} %get-tuple-element.40.refs_0_), channel_id=1, source_target_pairs={{0,16},{8,24},{16,0},{24,8},{32,48},{40,56},{48,32},{56,40},{1,17}... | collective-permute-start | bytes 1572872 | tf_op jit(solution)/shard_map/ppermute | solution.py:378
  29.1 27.6 %collective-permute-start.1 = (bf16[2,1024,128]{2,1,0:T(8,128)(2,1)}, bf16[2,1024,128]{2,1,0:T(8,128)(2,1)S(1)}, u32[]{:S(2)}, u32[]{:S(2)}) collective-permute-start(bf16[2,1024,128]{2,1,0:T(8,128)(2,1)} %get-tuple-element.40.refs_0_), channel_id=1, source_target_pairs={{0,32},{8,40},{16,48},{24,56},{32,0},{40,8},{48,16},{56,24},{1,33}... | collective-permute-start | bytes 1572872 | tf_op jit(solution)/shard_map/ppermute | solution.py:378
  31.6 25.2 %collective-permute-start.2 = (bf16[2,1024,128]{2,1,0:T(8,128)(2,1)}, bf16[2,1024,128]{2,1,0:T(8,128)(2,1)S(1)}, u32[]{:S(2)}, u32[]{:S(2)}) collective-permute-start(bf16[2,1024,128]{2,1,0:T(8,128)(2,1)} %get-tuple-element.40.refs_0_), channel_id=1, source_target_pairs={{0,48},{8,56},{16,32},{24,40},{32,16},{40,24},{48,0},{56,8},{1,49}... | collective-permute-start | bytes 1572872 | tf_op jit(solution)/shard_map/ppermute | solution.py:378
  35.2 24.2 %copy-start.1 = (bf16[2,1024,128]{2,1,0:T(8,128)(2,1)S(1)}, bf16[2,1024,128]{2,1,0:T(8,128)(2,1)}, u32[]{:S(2)}) copy-start(bf16[2,1024,128]{2,1,0:T(8,128)(2,1)} %get-tuple-element.40.refs_0_) | copy-start | bytes 1572868
  55.9 0.8 copy-start.4
  56.8 3.7 %collective-permute-start.10 = (bf16[2,1024,128]{2,1,0:T(8,128)(2,1)S(1)}, bf16[2,1024,128]{2,1,0:T(8,128)(2,1)S(1)}, u32[]{:S(2)}, u32[]{:S(2)}) collective-permute-start(bf16[2,1024,128]{2,1,0:T(8,128)(2,1)S(1)} %collective-permute-done.refs_1_), channel_id=1, source_target_pairs={{0,8},{8,0},{16,24},{24,16},{32,40},{40,32},{48,56},{56,48},{1,9},... | collective-permute-start | bytes 1572872 | tf_op jit(solution)/shard_map/ppermute | solution.py:378
  58.9 4.3 %collective-permute-start.11 = (bf16[2,1024,128]{2,1,0:T(8,128)(2,1)S(1)}, bf16[2,1024,128]{2,1,0:T(8,128)(2,1)S(1)}, u32[]{:S(2)}, u32[]{:S(2)}) collective-permute-start(bf16[2,1024,128]{2,1,0:T(8,128)(2,1)S(1)} %collective-permute-done.1.refs_2_), channel_id=1, source_target_pairs={{0,8},{8,0},{16,24},{24,16},{32,40},{40,32},{48,56},{56,48},{1,9},... | collective-permute-start | bytes 1572872 | tf_op jit(solution)/shard_map/ppermute | solution.py:378
  59.0 9.0 %collective-permute-start.12 = (bf16[2,1024,128]{2,1,0:T(8,128)(2,1)S(1)}, bf16[2,1024,128]{2,1,0:T(8,128)(2,1)}, u32[]{:S(2)}, u32[]{:S(2)}) collective-permute-start(bf16[2,1024,128]{2,1,0:T(8,128)(2,1)S(1)} %collective-permute-done.2.refs_3_), channel_id=1, source_target_pairs={{0,8},{8,0},{16,24},{24,16},{32,40},{40,32},{48,56},{56,48},{1,9},... | collective-permute-start | bytes 1572872 | tf_op jit(solution)/shard_map/ppermute | solution.py:378
  59.5 8.5 %collective-permute-start.9 = (bf16[2,1024,128]{2,1,0:T(8,128)(2,1)S(1)}, bf16[2,1024,128]{2,1,0:T(8,128)(2,1)}, u32[]{:S(2)}, u32[]{:S(2)}) collective-permute-start(bf16[2,1024,128]{2,1,0:T(8,128)(2,1)S(1)} %copy-done.1), channel_id=1, source_target_pairs={{0,8},{8,0},{16,24},{24,16},{32,40},{40,32},{48,56},{56,48},{1,9},... | collective-permute-start | bytes 1572872 | tf_op jit(solution)/shard_map/ppermute | solution.py:378
  59.6 11.0 %collective-permute-start.6 = (bf16[8,128,128]{2,1,0:T(8,128)(2,1)}, bf16[8,128,128]{2,1,0:T(8,128)(2,1)}, u32[]{:S(2)}, u32[]{:S(2)}) collective-permute-start(bf16[8,128,128]{2,1,0:T(8,128)(2,1)} %get-tuple-element.37), channel_id=1, source_target_pairs={{0,64},{64,0},{128,192},{192,128},{1,65},{65,1},{129,193},{193,129... | collective-permute-start | bytes 786440 | tf_op jit(solution)/shard_map/ppermute | solution.py:378
  60.5 14.8 %collective-permute-start.7 = (bf16[8,128,128]{2,1,0:T(8,128)(2,1)}, bf16[8,128,128]{2,1,0:T(8,128)(2,1)}, u32[]{:S(2)}, u32[]{:S(2)}) collective-permute-start(bf16[8,128,128]{2,1,0:T(8,128)(2,1)} %get-tuple-element.38), channel_id=1, source_target_pairs={{0,128},{64,192},{128,0},{192,64},{1,129},{65,193},{129,1},{193,65... | collective-permute-start | bytes 786440 | tf_op jit(solution)/shard_map/ppermute | solution.py:378
  63.3 14.0 %collective-permute-start.8 = (bf16[8,128,128]{2,1,0:T(8,128)(2,1)}, bf16[8,128,128]{2,1,0:T(8,128)(2,1)}, u32[]{:S(2)}, u32[]{:S(2)}) collective-permute-start(bf16[8,128,128]{2,1,0:T(8,128)(2,1)} %get-tuple-element.39), channel_id=1, source_target_pairs={{0,192},{64,128},{128,64},{192,0},{1,193},{65,129},{129,65},{193,1... | collective-permute-start | bytes 786440 | tf_op jit(solution)/shard_map/ppermute | solution.py:378
  63.8 18.3 %all-to-all-start.2 = ((bf16[8,128,128]{2,1,0:T(8,128)(2,1)}), bf16[8,128,128]{2,1,0:T(8,128)(2,1)S(1)}, u32[]{:S(2)}, u32[]{:S(2)}) async-start(bf16[8,128,128]{2,1,0:T(8,128)(2,1)} %get-tuple-element.34.y_ref), calls=%async_computation.2 | async-start | bytes 524288 | tf_op jit(solution)/shard_map/all_to_all | solution.py:386
  68.0 9.3 %copy-start.5 = (f32[8,128,128]{2,1,0:T(8,128)S(1)}, f32[8,128,128]{2,1,0:T(8,128)}, u32[]{:S(2)}) copy-start(f32[8,128,128]{2,1,0:T(8,128)} %copy-done.4) | copy-start | bytes 1572868
  81.4 0.7 copy-start.2
  82.1 35.3 %all-to-all-start.3 = ((bf16[256,8,128]{2,1,0:T(8,128)(2,1)}), bf16[256,8,128]{2,1,0:T(8,128)(2,1)S(1)}, u32[]{:S(2)}, u32[]{:S(2)}) async-start(bf16[256,8,128]{2,1,0:T(8,128)(2,1)} %get-tuple-element.50), calls=%async_computation.3 | async-start | bytes 1048576 | tf_op jit(solution)/shard_map/all_to_all | solution.py:415
  96.0 3.4 %collective-permute-start.13 = (bf16[4,128,128]{2,1,0:T(8,128)(2,1)}, bf16[4,128,128]{2,1,0:T(8,128)(2,1)S(1)}, u32[]{:S(2)}, u32[]{:S(2)}) collective-permute-start(bf16[4,128,128]{2,1,0:T(8,128)(2,1)} %copy-done.2), channel_id=1, source_target_pairs={{0,8},{8,0},{16,24},{24,16},{32,40},{40,32},{48,56},{56,48},{1,9},... | collective-permute-start | bytes 393224 | tf_op jit(solution)/shard_map/ppermute | solution.py:378
  99.4 7.4 %collective-permute-start.14 = (bf16[2,128,128]{2,1,0:T(8,128)(2,1)S(1)}, bf16[2,128,128]{2,1,0:T(8,128)(2,1)S(1)}, u32[]{:S(2)}, u32[]{:S(2)}) collective-permute-start(bf16[2,128,128]{2,1,0:T(8,128)(2,1)S(1)} %get-tuple-element.46), channel_id=1, source_target_pairs={{0,16},{8,24},{16,0},{24,8},{32,48},{40,56},{48,32},{56,40},{1,17}... | collective-permute-start | bytes 196616 | tf_op jit(solution)/shard_map/ppermute | solution.py:378
  99.5 7.3 %collective-permute-start.15 = (bf16[2,128,128]{2,1,0:T(8,128)(2,1)S(1)}, bf16[2,128,128]{2,1,0:T(8,128)(2,1)S(1)}, u32[]{:S(2)}, u32[]{:S(2)}) collective-permute-start(bf16[2,128,128]{2,1,0:T(8,128)(2,1)S(1)} %get-tuple-element.47), channel_id=1, source_target_pairs={{0,32},{8,40},{16,48},{24,56},{32,0},{40,8},{48,16},{56,24},{1,33}... | collective-permute-start | bytes 196616 | tf_op jit(solution)/shard_map/ppermute | solution.py:378
  101.5 7.9 %collective-permute-start.16 = (bf16[2,128,128]{2,1,0:T(8,128)(2,1)S(1)}, bf16[2,128,128]{2,1,0:T(8,128)(2,1)S(1)}, u32[]{:S(2)}, u32[]{:S(2)}) collective-permute-start(bf16[2,128,128]{2,1,0:T(8,128)(2,1)S(1)} %get-tuple-element.48), channel_id=1, source_target_pairs={{0,48},{8,56},{16,32},{24,40},{32,16},{40,24},{48,0},{56,8},{1,49}... | collective-permute-start | bytes 196616 | tf_op jit(solution)/shard_map/ppermute | solution.py:378
  103.4 2.2 %copy-start = (bf16[4,1024,512]{2,1,0:T(8,128)(2,1)S(1)}, bf16[4,1024,512]{2,1,0:T(8,128)(2,1)}, u32[]{:S(2)}) copy-start(bf16[4,1024,512]{2,1,0:T(8,128)(2,1)} %refs_5_.1) | copy-start | bytes 12582916

commit v3 on v2

--- a/solution.py
+++ b/solution.py
@@ -41,58 +41,53 @@
     return low * 8 + high
 
 
-def project_kernel(tok_ref, cot_ref, w_ref, kv_ref, qd_ref, xt_ref, rows):
+def by_head(rows, out_ref):
+    for head in range(HEADS):
+        cols = slice(head * HEAD_DIM, (head + 1) * HEAD_DIM)
+        out_ref[head] = jnp.concatenate([rows[0, :, cols], rows[1, :, cols]], axis=1)
+
+
+def keys_kernel(tok_ref, w_ref, kv_ref, rows):
     step = pl.program_id(0)
-
-    @pl.when(step < 3)
+    rows[step] = dot(tok_ref[...], w_ref[0]).astype(BF)
+
+    @pl.when(step == 1)
     def _():
-        rows[step] = dot(tok_ref[...], w_ref[0]).astype(BF)
-
-    @pl.when(step == 3)
-    def _():
-        rows[3] = dot(cot_ref[...], w_ref[0]).astype(BF)
-        for head in range(HEADS):
-            cols = slice(head * HEAD_DIM, (head + 1) * HEAD_DIM)
-            scaled = (rows[0, :, cols].astype(F32) * 0.125).astype(BF)
-            kv_ref[head] = jnp.concatenate([rows[1, :, cols], rows[2, :, cols]], axis=1)
-            qd_ref[head] = jnp.concatenate([scaled, rows[3, :, cols]], axis=1)
+        by_head(rows, kv_ref)
+
+
+def queries_kernel(tok_ref, cot_ref, w_ref, qd_ref, xt_ref, rows):
+    step = pl.program_id(0)
 
     @pl.when(step == 0)
     def _():
+        queries = dot(tok_ref[...], w_ref[0]).astype(BF)
+        rows[0] = (queries.astype(F32) * 0.125).astype(BF)
         xt_ref[0] = tok_ref[...].T
 
     @pl.when(step == 1)
     def _():
+        rows[1] = dot(cot_ref[...], w_ref[0]).astype(BF)
         xt_ref[1] = cot_ref[...].T
-
-
-def project(tok, cot, weights):
-    rows, width = tok.shape
-    whole = lambda step: (0, 0)
-    whole3 = lambda step: (0, 0, 0)
+        by_head(rows, qd_ref)
+
+
+def project(kernel, arrays, weights, pick, outs):
+    rows, width = arrays[0].shape
     return pl.pallas_call(
-        project_kernel,
-        grid=(4,),
-        in_specs=[
-            pl.BlockSpec((rows, width), whole),
-            pl.BlockSpec((rows, width), whole),
-            pl.BlockSpec((1, width, HEADS * HEAD_DIM), lambda step: (step, 0, 0)),
-        ],
-        out_specs=[
-            pl.BlockSpec((HEADS, rows, 128), whole3),
-            pl.BlockSpec((HEADS, rows, 128), whole3),
-            pl.BlockSpec((2, width, rows), whole3),
-        ],
-        out_shape=[
-            jax.ShapeDtypeStruct((HEADS, rows, 128), BF),
-            jax.ShapeDtypeStruct((HEADS, rows, 128), BF),
-            jax.ShapeDtypeStruct((2, width, rows), BF),
-        ],
-        scratch_shapes=[pltpu.VMEM((4, rows, HEADS * HEAD_DIM), BF)],
+        kernel,
+        grid=(2,),
+        in_specs=[pl.BlockSpec((rows, width), lambda step: (0, 0)) for _ in arrays]
+        + [pl.BlockSpec((1, width, HEADS * HEAD_DIM), lambda step: (pick(step), 0, 0))],
+        out_specs=[pl.BlockSpec(out, lambda step: (0, 0, 0)) for out in outs],
+        out_shape=[jax.ShapeDtypeStruct(out, BF) for out in outs],
+        scratch_shapes=[pltpu.VMEM((2, rows, HEADS * HEAD_DIM), BF)],
+        cost_estimate=pl.CostEstimate(
+            flops=1_000_000_000, bytes_accessed=4_000_000, transcendentals=0
+        ),
         compiler_params=grant(56),
         interpret=INTERPRET,
-        name="project",
-    )(tok, cot, weights)
+    )(*arrays, weights)
 
 
 def attend_kernel(
@@ -244,17 +239,26 @@
     return jnp.concatenate([y_ref[place ^ k] for k in (0, 2, 4, 6, 1, 3, 5, 7)], axis=0)
 
 
-def first_grads_kernel(place_ref, y_ref, *refs):
-    xs, out_ref = refs[:8], refs[8]
+def deal(grads, group, scratch, outs):
+    scratch[...] = grads
+    size = outs[0].shape[0]
+    for k, ref in enumerate(outs):
+        rows = pl.ds(pl.multiple_of((group ^ k) * size, size), size)
+        ref[...] = scratch[rows, :].astype(ref.dtype)
+
+
+def first_grads_kernel(group_ref, place_ref, y_ref, *refs):
+    xs, outs, scratch = refs[:8], refs[8:12], refs[12]
     y = ordered(y_ref, place_ref[0])
     tok = dot(jnp.concatenate([x[0] for x in xs], axis=1), y)
     cot = dot(jnp.concatenate([x[1] for x in xs], axis=1), y)
     left = lax.broadcasted_iota(jnp.int32, tok.shape, 1) < HEAD_DIM
-    out_ref[...] = jnp.where(left, tok, cot)
-
-
-def second_grads_kernel(place_ref, own, part1, part2, part3, first_ref, *refs):
-    xs, (out_ref, keep_ref, send_ref, y_ref, base, landed, sems) = refs[:8], refs[8:]
+    deal(jnp.where(left, tok, cot), group_ref[0], scratch, outs)
+
+
+def second_grads_kernel(group_ref, place_ref, own, part1, part2, part3, *refs):
+    xs, outs = refs[:8], refs[8:12]
+    keep_ref, send_ref, scratch, y_ref, base, landed, sems = refs[12:]
     copies = [pltpu.make_async_copy(own, base, sems.at[0])] + [
         pltpu.make_async_copy(part, landed.at[k], sems.at[k + 1])
         for k, part in enumerate((part1, part2, part3))
@@ -269,11 +273,17 @@
         keep_ref[k] = y_ref[(chip ^ k) * 2 + core]
         send_ref[k] = y_ref[(chip ^ k) * 2 + 1 - core]
     y = ordered(y_ref, place_ref[0])
-    second = dot(jnp.concatenate([x[0] for x in xs], axis=1), y)
+    grads = dot(jnp.concatenate([x[0] for x in xs], axis=1), y)
+    deal(grads, group_ref[0], scratch, outs)
+
+
+def pair_kernel(*refs):
+    total = lambda four: four[0][...] + sum(ref[...].astype(F32) for ref in four[1:])
+    first, second, out_ref = total(refs[0:4]), total(refs[4:8]), refs[8]
     rows = out_ref.shape[1] // 2
     for index in range(out_ref.shape[0]):
         mine = slice(index * rows, (index + 1) * rows)
-        out_ref[index] = jnp.concatenate([first_ref[mine], second[mine]], axis=0).astype(BF)
+        out_ref[index] = jnp.concatenate([first[mine], second[mine]], axis=0).astype(BF)
 
 
 def pack_kernel(keep_ref, got_ref, *outs):
@@ -282,31 +292,29 @@
         ref[1] = got_ref[k + 1]
 
 
-def grads_call(kernel, place, specs, operands, outs, scratch=()):
+def grads_call(kernel, scalars, specs, operands, width, more=(), scratch=()):
+    quarter = lambda dtype: jax.ShapeDtypeStruct((width // 4, 128), dtype)
+    outs = [quarter(F32)] + [quarter(BF)] * 3 + list(more)
     return pl.pallas_call(
         kernel,
-        in_specs=[pl.BlockSpec(memory_space=pltpu.SMEM)] + specs,
+        in_specs=[pl.BlockSpec(memory_space=pltpu.SMEM) for _ in scalars] + specs,
         out_specs=vmem(len(outs)),
         out_shape=outs,
-        scratch_shapes=list(scratch),
+        scratch_shapes=[pltpu.VMEM((width, 128), F32)] + list(scratch),
         cost_estimate=pl.CostEstimate(
             flops=2_000_000_000, bytes_accessed=4_000_000, transcendentals=0
         ),
         compiler_params=grant(16),
         interpret=INTERPRET,
-    )(place, *operands)
+    )(*scalars, *operands)
 
 
 def gather_kernel(in_ref, out_ref):
-    replicas, rows = in_ref.shape[0] // 32, in_ref.shape[1] // 2
-    parts = []
-    for head in range(HEADS):
-        total = None
-        for low in range(4):
-            start = position(head, low) * replicas
-            term = jnp.sum(in_ref[start : start + replicas].astype(F32), axis=0)
-            total = term if total is None else total + term
-        parts.append(total)
+    replicas, rows = in_ref.shape[0] // HEADS, in_ref.shape[1] // 2
+    parts = [
+        jnp.sum(in_ref[head * replicas : (head + 1) * replicas].astype(F32), axis=0)
+        for head in range(HEADS)
+    ]
     for half, (near, far) in enumerate(((0, 3), (1, 2))):
         mine = slice(half * rows, (half + 1) * rows)
         out_ref[near] = jnp.concatenate([p[mine, :HEAD_DIM] for p in parts], axis=1)
@@ -384,8 +392,14 @@
     group = lax.axis_index(ROW).astype(jnp.int32).reshape(1)
     place = lax.axis_index(HEAD).astype(jnp.int32).reshape(1)
     swap = lambda array: lax.all_to_all(array, HEAD, 0, 0, tiled=True)
-    kv, qd, xt = project(tokens[0], cotangent[0], weights)
+    (kv,) = project(
+        keys_kernel, [tokens[0]], weights, lambda step: step + 1, [(HEADS, BLOCK, 128)]
+    )
     kv = swap(kv)
+    qd, xt = project(
+        queries_kernel, [tokens[0], cotangent[0]], weights,
+        lambda step: 3 * step, [(HEADS, BLOCK, 128), (2, width, BLOCK)],
+    )
     qd, xt, kv = lax.optimization_barrier((qd, xt, kv))
     kvs = [kv] + [across(kv, ROW, k) for k in (1, 2, 3)]
     qd = swap(qd)
@@ -395,16 +409,16 @@
     xs = xs + [across(x, HEAD, 1) for x in xs]
     parts = [parts[0]] + [across(parts[k], ROW, k) for k in (1, 2, 3)]
     home = swap(y)
-    (first,) = grads_call(
-        first_grads_kernel, place, vmem(9), [y, *xs],
-        [jax.ShapeDtypeStruct((width, 128), F32)],
-    )
-    output, partial = products_call(output_kernel, (), (home,), weights, (0, 3), (BF, F32))
+    first = grads_call(first_grads_kernel, (group, place), vmem(9), [y, *xs], width)
+    first = [first[0]] + [across(first[k], ROW, k) for k in (1, 2, 3)]
+    parts, first = lax.optimization_barrier((parts, first))
+    output, partial = products_call(
+        output_kernel, (), (home,), weights, (0, 3), (BF, F32)
+    )
     pieces = lambda count: jax.ShapeDtypeStruct((count, 128, 128), BF)
-    terms, keep, send = grads_call(
-        second_grads_kernel, place, hbm(4) + vmem(9),
-        [*parts, first, *xs],
-        [jax.ShapeDtypeStruct((width // rows, 2 * rows, 128), BF), pieces(4), pieces(4)],
+    *second, keep, send = grads_call(
+        second_grads_kernel, (group, place), hbm(4) + vmem(8),
+        [*parts, *xs], width, [pieces(4), pieces(4)],
         [
             pltpu.VMEM((8, 128, 128), BF),
             pltpu.VMEM((8, 128, 128), F32),
@@ -412,9 +426,15 @@
             pltpu.SemaphoreType.DMA((4,)),
         ],
     )
-    terms = lax.all_to_all(terms, SEQ + ("rep",), 0, 0, tiled=True)
+    second = second[:1] + [across(second[k], ROW, k) for k in (1, 2, 3)]
     got = across(send, HEAD, 1)
     pairs = small_call(pack_kernel, [keep, got], [pieces(2)] * 3)
+    second, pairs = lax.optimization_barrier((second, pairs))
+    (terms,) = small_call(
+        pair_kernel, [*first, *second],
+        [jax.ShapeDtypeStruct((width // 4 // rows, 2 * rows, 128), BF)],
+    )
+    terms = lax.all_to_all(terms, HEAD + ("rep",), 0, 0, tiled=True)
     pairs = [across(pair, HEAD, 2 * k + 2) for k, pair in enumerate(pairs)]
     (d_inputs,) = products_call(
         inputs_kernel, (place,), (keep, got, *pairs, partial), weights, (1, 2),

time: 119 us -> 119 us (level)
  starting transfers between devices: 43.3 us -> 57.7 us
  blocking collectives: 13 us -> 0 us
  waiting for transfers between devices: 21.6 us -> 17.3 us
  local copies, waits for them, and re-layouts: 3.72 us -> 5.16 us
  Pallas kernels: 35.9 us -> 37.3 us
    all_to_all x1 -> x0, blocking collectives: 13 us -> none  [body(): swap = lambda array: lax.all_to_all(array, HEAD, 0, 0, tiled=True)]
    ppermute x17 -> x23, starting transfers between devices: 20 us -> 27.5 us  [across(): lax.ppermute(array, axes, [(i, i ^ flip) for i in range(lax.axis_size(axe...]
    all_to_all x2 -> x3, starting transfers between devices: 9.42 us -> 16.7 us  [body(): swap = lambda array: lax.all_to_all(array, HEAD, 0, 0, tiled=True)]
    all_to_all x1, waiting for transfers between devices: 6.43 us -> 0.01 us  [body(): terms = lax.all_to_all(terms, HEAD + ('rep',), 0, 0, tiled=True)]
    all_to_all x2 -> x3, waiting for transfers between devices: 2.75 us -> 6.24 us  [body(): swap = lambda array: lax.all_to_all(array, HEAD, 0, 0, tiled=True)]
    unnamed x15 -> x17, local copies, waits for them, and re-layouts: 3.72 us -> 5.16 us
    ppermute x17 -> x23, waiting for transfers between devices: 12.4 us -> 11.1 us  [across(): lax.ppermute(array, axes, [(i, i ^ flip) for i in range(lax.axis_size(axe...]
    pallas_call x3 -> x4, Pallas kernels: 11.7 us -> 12.3 us  [the longest x2 6.54 us: grads_call(): pl.pallas_call(kernel, in_specs=[pl.BlockSpec(memory_space=pltpu.SMEM) fo...]
  transfers between devices with their start and end apart: 20 -> 27, of which waited for: 8 -> 10; matrix products, arithmetic and copies ran while one was open for 0% -> 0% of each run, Pallas kernels for 26% -> 29%
where the time goes in v3:
time: 119 us; the launch traced here: 118 us
  starting transfers between devices  57.7 us (48%)
  Pallas kernels  37.3 us (31%)
  waiting for transfers between devices  17.3 us (15%)
  local copies, waits for them, and re-layouts  5.16 us (4%)
    ppermute x23, starting transfers between devices, across(): lax.ppermute(array, axes, [(i, i ^ flip) for i in range(lax.axis_size(axe...  27.5 us
    pallas_call x1, Pallas kernels, attend(): pl.pallas_call(attend_kernel, grid_spec=pltpu.PrefetchScalarGridSpec(num_...  20.7 us
    all_to_all x3, starting transfers between devices, body(): swap = lambda array: lax.all_to_all(array, HEAD, 0, 0, tiled=True)  16.7 us
    all_to_all x1, starting transfers between devices, body(): terms = lax.all_to_all(terms, HEAD + ('rep',), 0, 0, tiled=True)  13.4 us
    ppermute x23, waiting for transfers between devices, across(): lax.ppermute(array, axes, [(i, i ^ flip) for i in range(lax.axis_size(axe...  11.1 us
    pallas_call x2, Pallas kernels, grads_call(): pl.pallas_call(kernel, in_specs=[pl.BlockSpec(memory_space=pltpu.SMEM) fo...  6.54 us
    all_to_all x3, waiting for transfers between devices, body(): swap = lambda array: lax.all_to_all(array, HEAD, 0, 0, tiled=True)  6.24 us
    pallas_call x2, Pallas kernels, project(): pl.pallas_call(kernel, grid=(2,), in_specs=[pl.BlockSpec((rows, width), l...  5.8 us
  transfers between devices with their start and end apart: 27, of which 10 were waited for; matrix products, arithmetic and copies ran while one was open for 0% of the time, Pallas kernels for 29%

profile of v3, /device:TPU:1, one launch (start us, length us, event | category | flops | bytes accessed | tf_op | source)
XLA Modules:
  0.0 118.1 jit_solution(15142576305366452148)
XLA Ops:
  0.7 2.8 %shard_map.77 = bf16[8,128,128]{2,1,0:T(8,128)(2,1)} custom-call(bf16[128,1024]{1,0:T(8,128)(2,1)} %bitcast.10, bf16[4,1024,512]{2,1,0:T(8,128)(2,1)} %refs_5_.1), custom_call_target="tpu_custom_call" | custom-call | flops 1000000000 | bytes 4000000 | tf_op jit(solution)/shard_map/pallas_call | solution.py:77
  3.4 6.5 %all-to-all-start = ((bf16[8,128,128]{2,1,0:T(8,128)(2,1)}), bf16[8,128,128]{2,1,0:T(8,128)(2,1)S(1)}, u32[]{:S(2)}, u32[]{:S(2)}) async-start(bf16[8,128,128]{2,1,0:T(8,128)(2,1)} %shard_map.77), calls=%async_computation | async-start | bytes 524288 | tf_op jit(solution)/shard_map/all_to_all | solution.py:394
  10.0 3.0 %shard_map.76 = (bf16[8,128,128]{2,1,0:T(8,128)(2,1)}, bf16[2,1024,128]{2,1,0:T(8,128)(2,1)}) custom-call(bf16[128,1024]{1,0:T(8,128)(2,1)} %bitcast.11, bf16[128,1024]{1,0:T(8,128)(2,1)} %bitcast.12, bf16[4,1024,512]{2,1,0:T(8,128)(2,1)} %refs_5_.1), custom_call_target="tpu_custom_call" | custom-call | flops 1000000000 | bytes 4000000 | tf_op jit(solution)/shard_map/pallas_call | solution.py:77
  13.0 3.5 %all-to-all-done.kv0 = bf16[8,128,128]{2,1,0:T(8,128)(2,1)S(1)} async-done(((bf16[8,128,128]{2,1,0:T(8,128)(2,1)}), bf16[8,128,128]{2,1,0:T(8,128)(2,1)S(1)}, u32[]{:S(2)}, u32[]{:S(2)}) %all-to-all-start) | async-done | bytes 262176 | tf_op jit(solution)/shard_map/all_to_all | solution.py:394
  16.5 0.5 collective-permute-start.3
  17.0 2.6 %collective-permute-start.4 = (bf16[8,128,128]{2,1,0:T(8,128)(2,1)S(1)}, bf16[8,128,128]{2,1,0:T(8,128)(2,1)S(1)}, u32[]{:S(2)}, u32[]{:S(2)}) collective-permute-start(bf16[8,128,128]{2,1,0:T(8,128)(2,1)S(1)} %all-to-all-done.kv0), channel_id=1, source_target_pairs={{0,128},{64,192},{128,0},{192,64},{1,129},{65,193},{129,1},{193,65... | collective-permute-start | bytes 786440 | tf_op jit(solution)/shard_map/ppermute | solution.py:386
  19.6 0.7 collective-permute-start.5
  20.3 5.2 %all-to-all-start.1 = ((bf16[8,128,128]{2,1,0:T(8,128)(2,1)}), bf16[8,128,128]{2,1,0:T(8,128)(2,1)S(1)}, u32[]{:S(2)}, u32[]{:S(2)}) async-start(bf16[8,128,128]{2,1,0:T(8,128)(2,1)} %get-tuple-element.51), calls=%async_computation.1 | async-start | bytes 524288 | tf_op jit(solution)/shard_map/all_to_all | solution.py:394
  25.5 0.1 copy.8
  25.6 1.4 %collective-permute-start = (bf16[2,1024,128]{2,1,0:T(8,128)(2,1)}, bf16[2,1024,128]{2,1,0:T(8,128)(2,1)S(1)}, u32[]{:S(2)}, u32[]{:S(2)}) collective-permute-start(bf16[2,1024,128]{2,1,0:T(8,128)(2,1)} %get-tuple-element.60.refs_0_), channel_id=1, source_target_pairs={{0,16},{8,24},{16,0},{24,8},{32,48},{40,56},{48,32},{56,40},{1,17}... | collective-permute-start | bytes 1572872 | tf_op jit(solution)/shard_map/ppermute | solution.py:386
  27.0 2.4 %collective-permute-start.1 = (bf16[2,1024,128]{2,1,0:T(8,128)(2,1)}, bf16[2,1024,128]{2,1,0:T(8,128)(2,1)S(1)}, u32[]{:S(2)}, u32[]{:S(2)}) collective-permute-start(bf16[2,1024,128]{2,1,0:T(8,128)(2,1)} %get-tuple-element.60.refs_0_), channel_id=1, source_target_pairs={{0,32},{8,40},{16,48},{24,56},{32,0},{40,8},{48,16},{56,24},{1,33}... | collective-permute-start | bytes 1572872 | tf_op jit(solution)/shard_map/ppermute | solution.py:386
  29.4 0.1 collective-permute-start.2
  29.5 2.7 %all-to-all-done.1.qd_ref = bf16[8,128,128]{2,1,0:T(8,128)(2,1)S(1)} async-done(((bf16[8,128,128]{2,1,0:T(8,128)(2,1)}), bf16[8,128,128]{2,1,0:T(8,128)(2,1)S(1)}, u32[]{:S(2)}, u32[]{:S(2)}) %all-to-all-start.1) | async-done | bytes 262176 | tf_op jit(solution)/shard_map/all_to_all | solution.py:394
  32.2 0.8 collective-permute-done.5.kv3
  33.0 20.7 %attend.1 = (bf16[8,128,128]{2,1,0:T(8,128)(2,1)}, f32[8,128,128]{2,1,0:T(8,128)S(1)}, bf16[8,128,128]{2,1,0:T(8,128)(2,1)}, bf16[8,128,128]{2,1,0:T(8,128)(2,1)}, bf16[8,128,128]{2,1,0:T(8,128)(2,1)}) custom-call(s32[32,27]{1,0:T(8,128)S(1)} %bitcast.8, s32[32]{0:T(128)S(1)} %bitcast.9, s32[1]{0:T(128)} %bitcast.4.group_ref, ...), custom_call_target="tpu_custom_call" | custom-call | flops 30000001024 | bytes 4000000 | tf_op jit(solution)/shard_map/attend/pallas_call | solution.py:207
  53.8 0.8 copy-done.5
  54.6 0.0 collective-permute-done.1.refs_2_
  54.6 2.2 %collective-permute-start.10 = (bf16[2,1024,128]{2,1,0:T(8,128)(2,1)S(1)}, bf16[2,1024,128]{2,1,0:T(8,128)(2,1)S(1)}, u32[]{:S(2)}, u32[]{:S(2)}) collective-permute-start(bf16[2,1024,128]{2,1,0:T(8,128)(2,1)S(1)} %collective-permute-done.refs_1_), channel_id=1, source_target_pairs={{0,8},{8,0},{16,24},{24,16},{32,40},{40,32},{48,56},{56,48},{1,9},... | collective-permute-start | bytes 1572872 | tf_op jit(solution)/shard_map/ppermute | solution.py:386
  56.8 0.1 collective-permute-start.11
  56.9 0.4 collective-permute-start.12
  57.3 0.1 collective-permute-start.9
  57.4 0.9 collective-permute-done.10.refs_5_
  58.3 2.8 %collective-permute-start.7 = (bf16[8,128,128]{2,1,0:T(8,128)(2,1)}, bf16[8,128,128]{2,1,0:T(8,128)(2,1)}, u32[]{:S(2)}, u32[]{:S(2)}) collective-permute-start(bf16[8,128,128]{2,1,0:T(8,128)(2,1)} %get-tuple-element.58), channel_id=1, source_target_pairs={{0,128},{64,192},{128,0},{192,64},{1,129},{65,193},{129,1},{193,65... | collective-permute-start | bytes 786440 | tf_op jit(solution)/shard_map/ppermute | solution.py:386
  61.2 0.5 collective-permute-start.8
  61.6 3.2 %shard_map.79 = (f32[256,128]{1,0:T(8,128)S(1)}, bf16[256,128]{1,0:T(8,128)(2,1)}, bf16[256,128]{1,0:T(8,128)(2,1)}, bf16[256,128]{1,0:T(8,128)(2,1)S(1)}) custom-call(s32[1]{0:T(128)} %bitcast.4.group_ref, s32[1]{0:T(128)} %bitcast.6.place_ref, bf16[8,128,128]{2,1,0:T(8,128)(2,1)} %get-tuple-element.54.y_ref, bf16[2,1024,128]{2,1,0:T(8,128)(2,1)S(1)} %copy-done.1, ...), custom_call_target="tpu_custom_call" | custom-call | flops 2000000000 | bytes 4000000 | tf_op jit(solution)/shard_map/pallas_call | solution.py:298
  64.9 3.3 %collective-permute-start.14 = (bf16[256,128]{1,0:T(8,128)(2,1)}, bf16[256,128]{1,0:T(8,128)(2,1)S(1)}, u32[]{:S(2)}, u32[]{:S(2)}) collective-permute-start(bf16[256,128]{1,0:T(8,128)(2,1)} %get-tuple-element.66), channel_id=1, source_target_pairs={{0,128},{64,192},{128,0},{192,64},{1,129},{65,193},{129,1},{193,65... | collective-permute-start | bytes 196616 | tf_op jit(solution)/shard_map/ppermute | solution.py:386
  68.2 0.5 collective-permute-start.15
  68.7 5.0 %all-to-all-start.2 = ((bf16[8,128,128]{2,1,0:T(8,128)(2,1)}), bf16[8,128,128]{2,1,0:T(8,128)(2,1)S(1)}, u32[]{:S(2)}, u32[]{:S(2)}) async-start(bf16[8,128,128]{2,1,0:T(8,128)(2,1)} %get-tuple-element.54.y_ref), calls=%async_computation.2 | async-start | bytes 524288 | tf_op jit(solution)/shard_map/all_to_all | solution.py:394
  73.8 2.1 %collective-permute-done.8.part3 = bf16[8,128,128]{2,1,0:T(8,128)(2,1)} collective-permute-done((bf16[8,128,128]{2,1,0:T(8,128)(2,1)}, bf16[8,128,128]{2,1,0:T(8,128)(2,1)}, u32[]{:S(2)}, u32[]{:S(2)}) %collective-permute-start.8) | collective-permute-done | bytes 262176 | tf_op jit(solution)/shard_map/ppermute | solution.py:386
  75.9 2.1 %collective-permute-done.15.refs_3_ = bf16[256,128]{1,0:T(8,128)(2,1)S(1)} collective-permute-done((bf16[256,128]{1,0:T(8,128)(2,1)S(1)}, bf16[256,128]{1,0:T(8,128)(2,1)S(1)}, u32[]{:S(2)}, u32[]{:S(2)}) %collective-permute-start.15) | collective-permute-done | bytes 65568 | tf_op jit(solution)/shard_map/ppermute | solution.py:386
  78.0 1.0 copy-done.3
  79.1 1.0 copy-done.6
  80.1 3.3 %shard_map.80 = (f32[256,128]{1,0:T(8,128)S(1)}, bf16[256,128]{1,0:T(8,128)(2,1)S(1)}, bf16[256,128]{1,0:T(8,128)(2,1)S(1)}, bf16[256,128]{1,0:T(8,128)(2,1)S(1)...) custom-call(s32[1]{0:T(128)} %bitcast.4.group_ref, s32[1]{0:T(128)} %bitcast.6.place_ref, ...), custom_call_target="tpu_custom_call" | custom-call | flops 2000000000 | bytes 4000000 | tf_op jit(solution)/shard_map/pallas_call | solution.py:298
  83.4 1.8 %collective-permute-start.16 = (bf16[4,128,128]{2,1,0:T(8,128)(2,1)S(1)}, bf16[4,128,128]{2,1,0:T(8,128)(2,1)S(1)}, u32[]{:S(2)}, u32[]{:S(2)}) collective-permute-start(bf16[4,128,128]{2,1,0:T(8,128)(2,1)S(1)} %get-tuple-element.73), channel_id=1, source_target_pairs={{0,8},{8,0},{16,24},{24,16},{32,40},{40,32},{48,56},{56,48},{1,9},... | collective-permute-start | bytes 393224 | tf_op jit(solution)/shard_map/ppermute | solution.py:386
  85.3 1.7 %collective-permute-start.18 = (bf16[256,128]{1,0:T(8,128)(2,1)S(1)}, bf16[256,128]{1,0:T(8,128)(2,1)S(1)}, u32[]{:S(2)}, u32[]{:S(2)}) collective-permute-start(bf16[256,128]{1,0:T(8,128)(2,1)S(1)} %get-tuple-element.76), channel_id=1, source_target_pairs={{0,128},{64,192},{128,0},{192,64},{1,129},{65,193},{129,1},{193,65... | collective-permute-start | bytes 196616 | tf_op jit(solution)/shard_map/ppermute | solution.py:386
  86.9 2.2 %collective-permute-start.19 = (bf16[256,128]{1,0:T(8,128)(2,1)S(1)}, bf16[256,128]{1,0:T(8,128)(2,1)S(1)}, u32[]{:S(2)}, u32[]{:S(2)}) collective-permute-start(bf16[256,128]{1,0:T(8,128)(2,1)S(1)} %get-tuple-element.77), channel_id=1, source_target_pairs={{0,192},{64,128},{128,64},{192,0},{1,193},{65,129},{129,65},{193,1... | collective-permute-start | bytes 196616 | tf_op jit(solution)/shard_map/ppermute | solution.py:386
  89.1 1.3 %collective-permute-done.18.refs_6_ = bf16[256,128]{1,0:T(8,128)(2,1)S(1)} collective-permute-done((bf16[256,128]{1,0:T(8,128)(2,1)S(1)}, bf16[256,128]{1,0:T(8,128)(2,1)S(1)}, u32[]{:S(2)}, u32[]{:S(2)}) %collective-permute-start.18) | collective-permute-done | bytes 65568 | tf_op jit(solution)/shard_map/ppermute | solution.py:386
  90.4 1.0 collective-permute-done.19.refs_7_
  91.4 0.7 shard_map.83
  92.1 13.4 %all-to-all-start.3 = ((bf16[64,8,128]{2,1,0:T(8,128)(2,1)}), bf16[64,8,128]{2,1,0:T(8,128)(2,1)S(1)}, u32[]{:S(2)}, u32[]{:S(2)}) async-start(bf16[64,8,128]{2,1,0:T(8,128)(2,1)} %shard_map.83), calls=%async_computation.3 | async-start | bytes 262144 | tf_op jit(solution)/shard_map/all_to_all | solution.py:437
  105.6 1.5 %collective-permute-start.20 = (bf16[2,128,128]{2,1,0:T(8,128)(2,1)S(1)}, bf16[2,128,128]{2,1,0:T(8,128)(2,1)S(1)}, u32[]{:S(2)}, u32[]{:S(2)}) collective-permute-start(bf16[2,128,128]{2,1,0:T(8,128)(2,1)S(1)} %get-tuple-element.81), channel_id=1, source_target_pairs={{0,16},{8,24},{16,0},{24,8},{32,48},{40,56},{48,32},{56,40},{1,17}... | collective-permute-start | bytes 196616 | tf_op jit(solution)/shard_map/ppermute | solution.py:386
  107.0 2.6 %collective-permute-start.21 = (bf16[2,128,128]{2,1,0:T(8,128)(2,1)S(1)}, bf16[2,128,128]{2,1,0:T(8,128)(2,1)S(1)}, u32[]{:S(2)}, u32[]{:S(2)}) collective-permute-start(bf16[2,128,128]{2,1,0:T(8,128)(2,1)S(1)} %get-tuple-element.82), channel_id=1, source_target_pairs={{0,32},{8,40},{16,48},{24,56},{32,0},{40,8},{48,16},{56,24},{1,33}... | collective-permute-start | bytes 196616 | tf_op jit(solution)/shard_map/ppermute | solution.py:386
  109.7 2.2 %copy-done = bf16[4,1024,512]{2,1,0:T(8,128)(2,1)S(1)} copy-done((bf16[4,1024,512]{2,1,0:T(8,128)(2,1)S(1)}, bf16[4,1024,512]{2,1,0:T(8,128)(2,1)}, u32[]{:S(2)}) %copy-start) | copy-done | bytes 4194328
  111.8 1.2 %shard_map.78 = (bf16[128,1024]{1,0:T(8,128)(2,1)}, f32[128,1024]{1,0:T(8,128)S(1)}) custom-call(bf16[8,128,128]{2,1,0:T(8,128)(2,1)S(1)} %all-to-all-done.2.y_ref, bf16[4,1024,512]{2,1,0:T(8,128)(2,1)S(1)} %copy-done, bf16[4,1024,512]{2,1,0:T(8,128)(2,1)S(1)} %copy-done), custom_call_target="tpu_custom_call" | custom-call | flops 500000000 | bytes 4000000 | tf_op jit(solution)/shard_map/pallas_call | solution.py:363
  113.1 0.7 collective-permute-done.21.refs_1_
  113.8 2.1 %collective-permute-done.22.refs_2_ = bf16[2,128,128]{2,1,0:T(8,128)(2,1)S(1)} collective-permute-done((bf16[2,128,128]{2,1,0:T(8,128)(2,1)S(1)}, bf16[2,128,128]{2,1,0:T(8,128)(2,1)S(1)}, u32[]{:S(2)}, u32[]{:S(2)}) %collective-permute-start.22) | collective-permute-done | bytes 65568 | tf_op jit(solution)/shard_map/ppermute | solution.py:386
  115.9 1.5 %shard_map.82 = bf16[128,1024]{1,0:T(8,128)(2,1)} custom-call(s32[1]{0:T(128)} %bitcast.6.place_ref, bf16[4,128,128]{2,1,0:T(8,128)(2,1)S(1)} %get-tuple-element.72.keep_ref, bf16[4,128,128]{2,1,0:T(8,128)(2,1)S(1)} %collective-permute-done.16.got_ref, bf16[2,128,128]{2,1,0:T(8,128)(2,1)S(1)} %collective-permute-done.20.refs_0_, ...), custom_call_target="tpu_custom_call" | custom-call | flops 500000000 | bytes 4000000 | tf_op jit(solution)/shard_map/pallas_call | solution.py:363
  117.4 0.7 shard_map.84
  (33 shorter events, 0.1 us)
Async XLA Ops:
  0.6 24.9 %copy-start.7 = (s32[1,32,27]{1,0,2:T(1,128)S(1)}, s32[1,32,27]{1,0,2:T(1,128)}, u32[]{:S(2)}) copy-start(s32[1,32,27]{1,0,2:T(1,128)} %param.8) | copy-start | bytes 10372
  0.6 32.4 %copy-start.4 = (s32[1,32]{1,0:T(1,128)S(1)}, s32[1,32]{1,0:T(1,128)}, u32[]{:S(2)}) copy-start(s32[1,32]{1,0:T(1,128)} %param.9) | copy-start | bytes 388
  3.4 13.0 %all-to-all-start = ((bf16[8,128,128]{2,1,0:T(8,128)(2,1)}), bf16[8,128,128]{2,1,0:T(8,128)(2,1)S(1)}, u32[]{:S(2)}, u32[]{:S(2)}) async-start(bf16[8,128,128]{2,1,0:T(8,128)(2,1)} %shard_map.77), calls=%async_computation | async-start | bytes 524288 | tf_op jit(solution)/shard_map/all_to_all | solution.py:394
  16.5 12.9 %collective-permute-start.3 = (bf16[8,128,128]{2,1,0:T(8,128)(2,1)S(1)}, bf16[8,128,128]{2,1,0:T(8,128)(2,1)S(1)}, u32[]{:S(2)}, u32[]{:S(2)}) collective-permute-start(bf16[8,128,128]{2,1,0:T(8,128)(2,1)S(1)} %all-to-all-done.kv0), channel_id=1, source_target_pairs={{0,64},{64,0},{128,192},{192,128},{1,65},{65,1},{129,193},{193,129... | collective-permute-start | bytes 786440 | tf_op jit(solution)/shard_map/ppermute | solution.py:386
  17.0 15.2 %collective-permute-start.4 = (bf16[8,128,128]{2,1,0:T(8,128)(2,1)S(1)}, bf16[8,128,128]{2,1,0:T(8,128)(2,1)S(1)}, u32[]{:S(2)}, u32[]{:S(2)}) collective-permute-start(bf16[8,128,128]{2,1,0:T(8,128)(2,1)S(1)} %all-to-all-done.kv0), channel_id=1, source_target_pairs={{0,128},{64,192},{128,0},{192,64},{1,129},{65,193},{129,1},{193,65... | collective-permute-start | bytes 786440 | tf_op jit(solution)/shard_map/ppermute | solution.py:386
  19.6 13.4 %collective-permute-start.5 = (bf16[8,128,128]{2,1,0:T(8,128)(2,1)S(1)}, bf16[8,128,128]{2,1,0:T(8,128)(2,1)S(1)}, u32[]{:S(2)}, u32[]{:S(2)}) collective-permute-start(bf16[8,128,128]{2,1,0:T(8,128)(2,1)S(1)} %all-to-all-done.kv0), channel_id=1, source_target_pairs={{0,192},{64,128},{128,64},{192,0},{1,193},{65,129},{129,65},{193,1... | collective-permute-start | bytes 786440 | tf_op jit(solution)/shard_map/ppermute | solution.py:386
  20.3 11.9 %all-to-all-start.1 = ((bf16[8,128,128]{2,1,0:T(8,128)(2,1)}), bf16[8,128,128]{2,1,0:T(8,128)(2,1)S(1)}, u32[]{:S(2)}, u32[]{:S(2)}) async-start(bf16[8,128,128]{2,1,0:T(8,128)(2,1)} %get-tuple-element.51), calls=%async_computation.1 | async-start | bytes 524288 | tf_op jit(solution)/shard_map/all_to_all | solution.py:394
  25.6 29.0 %collective-permute-start = (bf16[2,1024,128]{2,1,0:T(8,128)(2,1)}, bf16[2,1024,128]{2,1,0:T(8,128)(2,1)S(1)}, u32[]{:S(2)}, u32[]{:S(2)}) collective-permute-start(bf16[2,1024,128]{2,1,0:T(8,128)(2,1)} %get-tuple-element.60.refs_0_), channel_id=1, source_target_pairs={{0,16},{8,24},{16,0},{24,8},{32,48},{40,56},{48,32},{56,40},{1,17}... | collective-permute-start | bytes 1572872 | tf_op jit(solution)/shard_map/ppermute | solution.py:386
  27.0 27.6 %collective-permute-start.1 = (bf16[2,1024,128]{2,1,0:T(8,128)(2,1)}, bf16[2,1024,128]{2,1,0:T(8,128)(2,1)S(1)}, u32[]{:S(2)}, u32[]{:S(2)}) collective-permute-start(bf16[2,1024,128]{2,1,0:T(8,128)(2,1)} %get-tuple-element.60.refs_0_), channel_id=1, source_target_pairs={{0,32},{8,40},{16,48},{24,56},{32,0},{40,8},{48,16},{56,24},{1,33}... | collective-permute-start | bytes 1572872 | tf_op jit(solution)/shard_map/ppermute | solution.py:386
  29.4 25.2 %collective-permute-start.2 = (bf16[2,1024,128]{2,1,0:T(8,128)(2,1)}, bf16[2,1024,128]{2,1,0:T(8,128)(2,1)S(1)}, u32[]{:S(2)}, u32[]{:S(2)}) collective-permute-start(bf16[2,1024,128]{2,1,0:T(8,128)(2,1)} %get-tuple-element.60.refs_0_), channel_id=1, source_target_pairs={{0,48},{8,56},{16,32},{24,40},{32,16},{40,24},{48,0},{56,8},{1,49}... | collective-permute-start | bytes 1572872 | tf_op jit(solution)/shard_map/ppermute | solution.py:386
  33.0 24.3 %copy-start.1 = (bf16[2,1024,128]{2,1,0:T(8,128)(2,1)S(1)}, bf16[2,1024,128]{2,1,0:T(8,128)(2,1)}, u32[]{:S(2)}) copy-start(bf16[2,1024,128]{2,1,0:T(8,128)(2,1)} %get-tuple-element.60.refs_0_) | copy-start | bytes 1572868
  53.8 0.8 copy-start.5
  54.6 3.7 %collective-permute-start.10 = (bf16[2,1024,128]{2,1,0:T(8,128)(2,1)S(1)}, bf16[2,1024,128]{2,1,0:T(8,128)(2,1)S(1)}, u32[]{:S(2)}, u32[]{:S(2)}) collective-permute-start(bf16[2,1024,128]{2,1,0:T(8,128)(2,1)S(1)} %collective-permute-done.refs_1_), channel_id=1, source_target_pairs={{0,8},{8,0},{16,24},{24,16},{32,40},{40,32},{48,56},{56,48},{1,9},... | collective-permute-start | bytes 1572872 | tf_op jit(solution)/shard_map/ppermute | solution.py:386
  56.8 4.4 %collective-permute-start.11 = (bf16[2,1024,128]{2,1,0:T(8,128)(2,1)S(1)}, bf16[2,1024,128]{2,1,0:T(8,128)(2,1)S(1)}, u32[]{:S(2)}, u32[]{:S(2)}) collective-permute-start(bf16[2,1024,128]{2,1,0:T(8,128)(2,1)S(1)} %collective-permute-done.1.refs_2_), channel_id=1, source_target_pairs={{0,8},{8,0},{16,24},{24,16},{32,40},{40,32},{48,56},{56,48},{1,9},... | collective-permute-start | bytes 1572872 | tf_op jit(solution)/shard_map/ppermute | solution.py:386
  56.9 4.8 %collective-permute-start.12 = (bf16[2,1024,128]{2,1,0:T(8,128)(2,1)S(1)}, bf16[2,1024,128]{2,1,0:T(8,128)(2,1)}, u32[]{:S(2)}, u32[]{:S(2)}) collective-permute-start(bf16[2,1024,128]{2,1,0:T(8,128)(2,1)S(1)} %collective-permute-done.2.refs_3_), channel_id=1, source_target_pairs={{0,8},{8,0},{16,24},{24,16},{32,40},{40,32},{48,56},{56,48},{1,9},... | collective-permute-start | bytes 1572872 | tf_op jit(solution)/shard_map/ppermute | solution.py:386
  57.3 4.3 %collective-permute-start.9 = (bf16[2,1024,128]{2,1,0:T(8,128)(2,1)S(1)}, bf16[2,1024,128]{2,1,0:T(8,128)(2,1)}, u32[]{:S(2)}, u32[]{:S(2)}) collective-permute-start(bf16[2,1024,128]{2,1,0:T(8,128)(2,1)S(1)} %copy-done.1), channel_id=1, source_target_pairs={{0,8},{8,0},{16,24},{24,16},{32,40},{40,32},{48,56},{56,48},{1,9},... | collective-permute-start | bytes 1572872 | tf_op jit(solution)/shard_map/ppermute | solution.py:386
  57.4 10.8 %collective-permute-start.6 = (bf16[8,128,128]{2,1,0:T(8,128)(2,1)}, bf16[8,128,128]{2,1,0:T(8,128)(2,1)}, u32[]{:S(2)}, u32[]{:S(2)}) collective-permute-start(bf16[8,128,128]{2,1,0:T(8,128)(2,1)} %get-tuple-element.57), channel_id=1, source_target_pairs={{0,64},{64,0},{128,192},{192,128},{1,65},{65,1},{129,193},{193,129... | collective-permute-start | bytes 786440 | tf_op jit(solution)/shard_map/ppermute | solution.py:386
  58.3 15.4 %collective-permute-start.7 = (bf16[8,128,128]{2,1,0:T(8,128)(2,1)}, bf16[8,128,128]{2,1,0:T(8,128)(2,1)}, u32[]{:S(2)}, u32[]{:S(2)}) collective-permute-start(bf16[8,128,128]{2,1,0:T(8,128)(2,1)} %get-tuple-element.58), channel_id=1, source_target_pairs={{0,128},{64,192},{128,0},{192,64},{1,129},{65,193},{129,1},{193,65... | collective-permute-start | bytes 786440 | tf_op jit(solution)/shard_map/ppermute | solution.py:386
  61.2 7.6 %copy-start.2 = (bf16[2,1024,128]{2,1,0:T(8,128)(2,1)}, bf16[2,1024,128]{2,1,0:T(8,128)(2,1)S(1)}, u32[]{:S(2)}) copy-start(bf16[2,1024,128]{2,1,0:T(8,128)(2,1)S(1)} %collective-permute-done.11.refs_6_) | copy-start | bytes 1572868
  61.2 14.7 %collective-permute-start.8 = (bf16[8,128,128]{2,1,0:T(8,128)(2,1)}, bf16[8,128,128]{2,1,0:T(8,128)(2,1)}, u32[]{:S(2)}, u32[]{:S(2)}) collective-permute-start(bf16[8,128,128]{2,1,0:T(8,128)(2,1)} %get-tuple-element.59), channel_id=1, source_target_pairs={{0,192},{64,128},{128,64},{192,0},{1,193},{65,129},{129,65},{193,1... | collective-permute-start | bytes 786440 | tf_op jit(solution)/shard_map/ppermute | solution.py:386
  64.8 11.0 %collective-permute-start.13 = (bf16[256,128]{1,0:T(8,128)(2,1)}, bf16[256,128]{1,0:T(8,128)(2,1)S(1)}, u32[]{:S(2)}, u32[]{:S(2)}) collective-permute-start(bf16[256,128]{1,0:T(8,128)(2,1)} %get-tuple-element.65), channel_id=1, source_target_pairs={{0,64},{64,0},{128,192},{192,128},{1,65},{65,1},{129,193},{193,129... | collective-permute-start | bytes 196616 | tf_op jit(solution)/shard_map/ppermute | solution.py:386
  64.9 11.0 %collective-permute-start.14 = (bf16[256,128]{1,0:T(8,128)(2,1)}, bf16[256,128]{1,0:T(8,128)(2,1)S(1)}, u32[]{:S(2)}, u32[]{:S(2)}) collective-permute-start(bf16[256,128]{1,0:T(8,128)(2,1)} %get-tuple-element.66), channel_id=1, source_target_pairs={{0,128},{64,192},{128,0},{192,64},{1,129},{65,193},{129,1},{193,65... | collective-permute-start | bytes 196616 | tf_op jit(solution)/shard_map/ppermute | solution.py:386
  68.2 9.8 %collective-permute-start.15 = (bf16[256,128]{1,0:T(8,128)(2,1)S(1)}, bf16[256,128]{1,0:T(8,128)(2,1)S(1)}, u32[]{:S(2)}, u32[]{:S(2)}) collective-permute-start(bf16[256,128]{1,0:T(8,128)(2,1)S(1)} %get-tuple-element.67), channel_id=1, source_target_pairs={{0,192},{64,128},{128,64},{192,0},{1,193},{65,129},{129,65},{193,1... | collective-permute-start | bytes 196616 | tf_op jit(solution)/shard_map/ppermute | solution.py:386
  68.7 23.4 %all-to-all-start.2 = ((bf16[8,128,128]{2,1,0:T(8,128)(2,1)}), bf16[8,128,128]{2,1,0:T(8,128)(2,1)S(1)}, u32[]{:S(2)}, u32[]{:S(2)}) async-start(bf16[8,128,128]{2,1,0:T(8,128)(2,1)} %get-tuple-element.54.y_ref), calls=%async_computation.2 | async-start | bytes 524288 | tf_op jit(solution)/shard_map/all_to_all | solution.py:394
  78.0 1.0 copy-start.3
  79.0 1.0 copy-start.6
  83.4 5.7 %collective-permute-start.16 = (bf16[4,128,128]{2,1,0:T(8,128)(2,1)S(1)}, bf16[4,128,128]{2,1,0:T(8,128)(2,1)S(1)}, u32[]{:S(2)}, u32[]{:S(2)}) collective-permute-start(bf16[4,128,128]{2,1,0:T(8,128)(2,1)S(1)} %get-tuple-element.73), channel_id=1, source_target_pairs={{0,8},{8,0},{16,24},{24,16},{32,40},{40,32},{48,56},{56,48},{1,9},... | collective-permute-start | bytes 393224 | tf_op jit(solution)/shard_map/ppermute | solution.py:386
  85.3 3.9 %collective-permute-start.17 = (bf16[256,128]{1,0:T(8,128)(2,1)S(1)}, bf16[256,128]{1,0:T(8,128)(2,1)S(1)}, u32[]{:S(2)}, u32[]{:S(2)}) collective-permute-start(bf16[256,128]{1,0:T(8,128)(2,1)S(1)} %get-tuple-element.75), channel_id=1, source_target_pairs={{0,64},{64,0},{128,192},{192,128},{1,65},{65,1},{129,193},{193,129... | collective-permute-start | bytes 196616 | tf_op jit(solution)/shard_map/ppermute | solution.py:386
  85.3 5.2 %collective-permute-start.18 = (bf16[256,128]{1,0:T(8,128)(2,1)S(1)}, bf16[256,128]{1,0:T(8,128)(2,1)S(1)}, u32[]{:S(2)}, u32[]{:S(2)}) collective-permute-start(bf16[256,128]{1,0:T(8,128)(2,1)S(1)} %get-tuple-element.76), channel_id=1, source_target_pairs={{0,128},{64,192},{128,0},{192,64},{1,129},{65,193},{129,1},{193,65... | collective-permute-start | bytes 196616 | tf_op jit(solution)/shard_map/ppermute | solution.py:386
  86.9 4.5 %collective-permute-start.19 = (bf16[256,128]{1,0:T(8,128)(2,1)S(1)}, bf16[256,128]{1,0:T(8,128)(2,1)S(1)}, u32[]{:S(2)}, u32[]{:S(2)}) collective-permute-start(bf16[256,128]{1,0:T(8,128)(2,1)S(1)} %get-tuple-element.77), channel_id=1, source_target_pairs={{0,192},{64,128},{128,64},{192,0},{1,193},{65,129},{129,65},{193,1... | collective-permute-start | bytes 196616 | tf_op jit(solution)/shard_map/ppermute | solution.py:386
  92.1 25.3 %all-to-all-start.3 = ((bf16[64,8,128]{2,1,0:T(8,128)(2,1)}), bf16[64,8,128]{2,1,0:T(8,128)(2,1)S(1)}, u32[]{:S(2)}, u32[]{:S(2)}) async-start(bf16[64,8,128]{2,1,0:T(8,128)(2,1)} %shard_map.83), calls=%async_computation.3 | async-start | bytes 262144 | tf_op jit(solution)/shard_map/all_to_all | solution.py:437
  105.6 7.5 %collective-permute-start.20 = (bf16[2,128,128]{2,1,0:T(8,128)(2,1)S(1)}, bf16[2,128,128]{2,1,0:T(8,128)(2,1)S(1)}, u32[]{:S(2)}, u32[]{:S(2)}) collective-permute-start(bf16[2,128,128]{2,1,0:T(8,128)(2,1)S(1)} %get-tuple-element.81), channel_id=1, source_target_pairs={{0,16},{8,24},{16,0},{24,8},{32,48},{40,56},{48,32},{56,40},{1,17}... | collective-permute-start | bytes 196616 | tf_op jit(solution)/shard_map/ppermute | solution.py:386
  107.0 6.7 %collective-permute-start.21 = (bf16[2,128,128]{2,1,0:T(8,128)(2,1)S(1)}, bf16[2,128,128]{2,1,0:T(8,128)(2,1)S(1)}, u32[]{:S(2)}, u32[]{:S(2)}) collective-permute-start(bf16[2,128,128]{2,1,0:T(8,128)(2,1)S(1)} %get-tuple-element.82), channel_id=1, source_target_pairs={{0,32},{8,40},{16,48},{24,56},{32,0},{40,8},{48,16},{56,24},{1,33}... | collective-permute-start | bytes 196616 | tf_op jit(solution)/shard_map/ppermute | solution.py:386
  109.7 6.2 %collective-permute-start.22 = (bf16[2,128,128]{2,1,0:T(8,128)(2,1)S(1)}, bf16[2,128,128]{2,1,0:T(8,128)(2,1)S(1)}, u32[]{:S(2)}, u32[]{:S(2)}) collective-permute-start(bf16[2,128,128]{2,1,0:T(8,128)(2,1)S(1)} %get-tuple-element.83), channel_id=1, source_target_pairs={{0,48},{8,56},{16,32},{24,40},{32,16},{40,24},{48,0},{56,8},{1,49}... | collective-permute-start | bytes 196616 | tf_op jit(solution)/shard_map/ppermute | solution.py:386
  109.7 2.2 %copy-start = (bf16[4,1024,512]{2,1,0:T(8,128)(2,1)S(1)}, bf16[4,1024,512]{2,1,0:T(8,128)(2,1)}, u32[]{:S(2)}) copy-start(bf16[4,1024,512]{2,1,0:T(8,128)(2,1)} %refs_5_.1) | copy-start | bytes 12582916

commit v4 on v2

--- a/solution.py
+++ b/solution.py
@@ -41,58 +41,53 @@
     return low * 8 + high
 
 
-def project_kernel(tok_ref, cot_ref, w_ref, kv_ref, qd_ref, xt_ref, rows):
+def by_head(rows, out_ref):
+    for head in range(HEADS):
+        cols = slice(head * HEAD_DIM, (head + 1) * HEAD_DIM)
+        out_ref[head] = jnp.concatenate([rows[0, :, cols], rows[1, :, cols]], axis=1)
+
+
+def keys_kernel(tok_ref, w_ref, kv_ref, rows):
     step = pl.program_id(0)
-
-    @pl.when(step < 3)
+    rows[step] = dot(tok_ref[...], w_ref[0]).astype(BF)
+
+    @pl.when(step == 1)
     def _():
-        rows[step] = dot(tok_ref[...], w_ref[0]).astype(BF)
-
-    @pl.when(step == 3)
-    def _():
-        rows[3] = dot(cot_ref[...], w_ref[0]).astype(BF)
-        for head in range(HEADS):
-            cols = slice(head * HEAD_DIM, (head + 1) * HEAD_DIM)
-            scaled = (rows[0, :, cols].astype(F32) * 0.125).astype(BF)
-            kv_ref[head] = jnp.concatenate([rows[1, :, cols], rows[2, :, cols]], axis=1)
-            qd_ref[head] = jnp.concatenate([scaled, rows[3, :, cols]], axis=1)
+        by_head(rows, kv_ref)
+
+
+def queries_kernel(tok_ref, cot_ref, w_ref, qd_ref, xt_ref, rows):
+    step = pl.program_id(0)
 
     @pl.when(step == 0)
     def _():
+        queries = dot(tok_ref[...], w_ref[0]).astype(BF)
+        rows[0] = (queries.astype(F32) * 0.125).astype(BF)
         xt_ref[0] = tok_ref[...].T
 
     @pl.when(step == 1)
     def _():
+        rows[1] = dot(cot_ref[...], w_ref[0]).astype(BF)
         xt_ref[1] = cot_ref[...].T
-
-
-def project(tok, cot, weights):
-    rows, width = tok.shape
-    whole = lambda step: (0, 0)
-    whole3 = lambda step: (0, 0, 0)
+        by_head(rows, qd_ref)
+
+
+def project(kernel, arrays, weights, pick, outs):
+    rows, width = arrays[0].shape
     return pl.pallas_call(
-        project_kernel,
-        grid=(4,),
-        in_specs=[
-            pl.BlockSpec((rows, width), whole),
-            pl.BlockSpec((rows, width), whole),
-            pl.BlockSpec((1, width, HEADS * HEAD_DIM), lambda step: (step, 0, 0)),
-        ],
-        out_specs=[
-            pl.BlockSpec((HEADS, rows, 128), whole3),
-            pl.BlockSpec((HEADS, rows, 128), whole3),
-            pl.BlockSpec((2, width, rows), whole3),
-        ],
-        out_shape=[
-            jax.ShapeDtypeStruct((HEADS, rows, 128), BF),
-            jax.ShapeDtypeStruct((HEADS, rows, 128), BF),
-            jax.ShapeDtypeStruct((2, width, rows), BF),
-        ],
-        scratch_shapes=[pltpu.VMEM((4, rows, HEADS * HEAD_DIM), BF)],
+        kernel,
+        grid=(2,),
+        in_specs=[pl.BlockSpec((rows, width), lambda step: (0, 0)) for _ in arrays]
+        + [pl.BlockSpec((1, width, HEADS * HEAD_DIM), lambda step: (pick(step), 0, 0))],
+        out_specs=[pl.BlockSpec(out, lambda step: (0, 0, 0)) for out in outs],
+        out_shape=[jax.ShapeDtypeStruct(out, BF) for out in outs],
+        scratch_shapes=[pltpu.VMEM((2, rows, HEADS * HEAD_DIM), BF)],
+        cost_estimate=pl.CostEstimate(
+            flops=1_000_000_000, bytes_accessed=4_000_000, transcendentals=0
+        ),
         compiler_params=grant(56),
         interpret=INTERPRET,
-        name="project",
-    )(tok, cot, weights)
+    )(*arrays, weights)
 
 
 def attend_kernel(
@@ -384,8 +379,12 @@
     group = lax.axis_index(ROW).astype(jnp.int32).reshape(1)
     place = lax.axis_index(HEAD).astype(jnp.int32).reshape(1)
     swap = lambda array: lax.all_to_all(array, HEAD, 0, 0, tiled=True)
-    kv, qd, xt = project(tokens[0], cotangent[0], weights)
+    (kv,) = project(keys_kernel, [tokens[0]], weights, lambda step: step + 1, [(HEADS, BLOCK, 128)])
     kv = swap(kv)
+    qd, xt = project(
+        queries_kernel, [tokens[0], cotangent[0]], weights,
+        lambda step: 3 * step, [(HEADS, BLOCK, 128), (2, width, BLOCK)],
+    )
     qd, xt, kv = lax.optimization_barrier((qd, xt, kv))
     kvs = [kv] + [across(kv, ROW, k) for k in (1, 2, 3)]
     qd = swap(qd)

time: 119 us -> 117 us (0.983)
  blocking collectives: 13 us -> 0 us
  starting transfers between devices: 43.3 us -> 49.7 us
  waiting for transfers between devices: 21.6 us -> 25.1 us
    all_to_all x1 -> x0, blocking collectives: 13 us -> none  [body(): swap = lambda array: lax.all_to_all(array, HEAD, 0, 0, tiled=True)]
    all_to_all x2 -> x3, starting transfers between devices: 9.42 us -> 15.9 us  [body(): swap = lambda array: lax.all_to_all(array, HEAD, 0, 0, tiled=True)]
    all_to_all x2 -> x3, waiting for transfers between devices: 2.75 us -> 6.26 us  [body(): swap = lambda array: lax.all_to_all(array, HEAD, 0, 0, tiled=True)]
    pallas_call x1 -> x2, Pallas kernels: 4.98 us -> 5.78 us  [project(): pl.pallas_call(kernel, grid=(2,), in_specs=[pl.BlockSpec((rows, width), l...]
  transfers between devices with their start and end apart: 20 -> 21, of which waited for: 8 -> 10; matrix products, arithmetic and copies ran while one was open for 0% -> 0% of each run, Pallas kernels for 26% -> 29%
where the time goes in v4:
time: 117 us; the launch traced here: 116 us
  starting transfers between devices  49.7 us (42%)
  Pallas kernels  36.7 us (31%)
  waiting for transfers between devices  25.1 us (21%)
  local copies, waits for them, and re-layouts  3.74 us (3%)
    pallas_call x1, Pallas kernels, attend(): pl.pallas_call(attend_kernel, grid_spec=pltpu.PrefetchScalarGridSpec(num_...  20.7 us
    ppermute x17, starting transfers between devices, across(): lax.ppermute(array, axes, [(i, i ^ flip) for i in range(lax.axis_size(axe...  20 us
    all_to_all x3, starting transfers between devices, body(): swap = lambda array: lax.all_to_all(array, HEAD, 0, 0, tiled=True)  15.9 us
    all_to_all x1, starting transfers between devices, body(): terms = lax.all_to_all(terms, SEQ + ('rep',), 0, 0, tiled=True)  13.8 us
    ppermute x17, waiting for transfers between devices, across(): lax.ppermute(array, axes, [(i, i ^ flip) for i in range(lax.axis_size(axe...  12.4 us
    pallas_call x2, Pallas kernels, grads_call(): pl.pallas_call(kernel, in_specs=[pl.BlockSpec(memory_space=pltpu.SMEM)] +...  6.7 us
    all_to_all x1, waiting for transfers between devices, body(): terms = lax.all_to_all(terms, SEQ + ('rep',), 0, 0, tiled=True)  6.43 us
    all_to_all x3, waiting for transfers between devices, body(): swap = lambda array: lax.all_to_all(array, HEAD, 0, 0, tiled=True)  6.26 us
  transfers between devices with their start and end apart: 21, of which 10 were waited for; matrix products, arithmetic and copies ran while one was open for 0% of the time, Pallas kernels for 29%

profile of v4, /device:TPU:1, one launch (start us, length us, event | category | flops | bytes accessed | tf_op | source)
XLA Modules:
  0.0 116.0 jit_solution(4595549602350533938)
XLA Ops:
  0.7 2.8 %shard_map.77 = bf16[8,128,128]{2,1,0:T(8,128)(2,1)} custom-call(bf16[128,1024]{1,0:T(8,128)(2,1)} %bitcast.10, bf16[4,1024,512]{2,1,0:T(8,128)(2,1)} %refs_5_.1), custom_call_target="tpu_custom_call" | custom-call | flops 1000000000 | bytes 4000000 | tf_op jit(solution)/shard_map/pallas_call | solution.py:77
  3.4 6.5 %all-to-all-start = ((bf16[8,128,128]{2,1,0:T(8,128)(2,1)}), bf16[8,128,128]{2,1,0:T(8,128)(2,1)S(1)}, u32[]{:S(2)}, u32[]{:S(2)}) async-start(bf16[8,128,128]{2,1,0:T(8,128)(2,1)} %shard_map.77), calls=%async_computation | async-start | bytes 524288 | tf_op jit(solution)/shard_map/all_to_all | solution.py:381
  10.0 3.0 %shard_map.76 = (bf16[8,128,128]{2,1,0:T(8,128)(2,1)}, bf16[2,1024,128]{2,1,0:T(8,128)(2,1)}) custom-call(bf16[128,1024]{1,0:T(8,128)(2,1)} %bitcast.11, bf16[128,1024]{1,0:T(8,128)(2,1)} %bitcast.12, bf16[4,1024,512]{2,1,0:T(8,128)(2,1)} %refs_5_.1), custom_call_target="tpu_custom_call" | custom-call | flops 1000000000 | bytes 4000000 | tf_op jit(solution)/shard_map/pallas_call | solution.py:77
  12.9 3.5 %all-to-all-done.kv0 = bf16[8,128,128]{2,1,0:T(8,128)(2,1)S(1)} async-done(((bf16[8,128,128]{2,1,0:T(8,128)(2,1)}), bf16[8,128,128]{2,1,0:T(8,128)(2,1)S(1)}, u32[]{:S(2)}, u32[]{:S(2)}) %all-to-all-start) | async-done | bytes 262176 | tf_op jit(solution)/shard_map/all_to_all | solution.py:381
  16.5 0.5 collective-permute-start.3
  17.0 2.6 %collective-permute-start.4 = (bf16[8,128,128]{2,1,0:T(8,128)(2,1)S(1)}, bf16[8,128,128]{2,1,0:T(8,128)(2,1)S(1)}, u32[]{:S(2)}, u32[]{:S(2)}) collective-permute-start(bf16[8,128,128]{2,1,0:T(8,128)(2,1)S(1)} %all-to-all-done.kv0), channel_id=1, source_target_pairs={{0,128},{64,192},{128,0},{192,64},{1,129},{65,193},{129,1},{193,65... | collective-permute-start | bytes 786440 | tf_op jit(solution)/shard_map/ppermute | solution.py:373
  19.6 0.7 collective-permute-start.5
  20.3 5.2 %all-to-all-start.1 = ((bf16[8,128,128]{2,1,0:T(8,128)(2,1)}), bf16[8,128,128]{2,1,0:T(8,128)(2,1)S(1)}, u32[]{:S(2)}, u32[]{:S(2)}) async-start(bf16[8,128,128]{2,1,0:T(8,128)(2,1)} %get-tuple-element.29), calls=%async_computation.1 | async-start | bytes 524288 | tf_op jit(solution)/shard_map/all_to_all | solution.py:381
  25.5 0.1 copy.8
  25.6 1.4 %collective-permute-start = (bf16[2,1024,128]{2,1,0:T(8,128)(2,1)}, bf16[2,1024,128]{2,1,0:T(8,128)(2,1)S(1)}, u32[]{:S(2)}, u32[]{:S(2)}) collective-permute-start(bf16[2,1024,128]{2,1,0:T(8,128)(2,1)} %get-tuple-element.38.refs_0_), channel_id=1, source_target_pairs={{0,16},{8,24},{16,0},{24,8},{32,48},{40,56},{48,32},{56,40},{1,17}... | collective-permute-start | bytes 1572872 | tf_op jit(solution)/shard_map/ppermute | solution.py:373
  27.0 2.4 %collective-permute-start.1 = (bf16[2,1024,128]{2,1,0:T(8,128)(2,1)}, bf16[2,1024,128]{2,1,0:T(8,128)(2,1)S(1)}, u32[]{:S(2)}, u32[]{:S(2)}) collective-permute-start(bf16[2,1024,128]{2,1,0:T(8,128)(2,1)} %get-tuple-element.38.refs_0_), channel_id=1, source_target_pairs={{0,32},{8,40},{16,48},{24,56},{32,0},{40,8},{48,16},{56,24},{1,33}... | collective-permute-start | bytes 1572872 | tf_op jit(solution)/shard_map/ppermute | solution.py:373
  29.4 0.1 collective-permute-start.2
  29.5 2.7 %all-to-all-done.1.qd_ref = bf16[8,128,128]{2,1,0:T(8,128)(2,1)S(1)} async-done(((bf16[8,128,128]{2,1,0:T(8,128)(2,1)}), bf16[8,128,128]{2,1,0:T(8,128)(2,1)S(1)}, u32[]{:S(2)}, u32[]{:S(2)}) %all-to-all-start.1) | async-done | bytes 262176 | tf_op jit(solution)/shard_map/all_to_all | solution.py:381
  32.2 0.0 collective-permute-done.4.kv2
  32.2 0.8 collective-permute-done.5.kv3
  33.0 20.7 %attend.1 = (bf16[8,128,128]{2,1,0:T(8,128)(2,1)}, f32[8,128,128]{2,1,0:T(8,128)S(1)}, bf16[8,128,128]{2,1,0:T(8,128)(2,1)}, bf16[8,128,128]{2,1,0:T(8,128)(2,1)}, bf16[8,128,128]{2,1,0:T(8,128)(2,1)}) custom-call(s32[32,27]{1,0:T(8,128)S(1)} %bitcast.8, s32[32]{0:T(128)S(1)} %bitcast.9, s32[1]{0:T(128)} %bitcast.4.group_ref, ...), custom_call_target="tpu_custom_call" | custom-call | flops 30000001024 | bytes 4000000 | tf_op jit(solution)/shard_map/attend/pallas_call | solution.py:207
  53.7 0.8 copy-done.4
  54.5 0.0 collective-permute-done.refs_1_
  54.5 0.1 collective-permute-done.1.refs_2_
  54.6 0.0 collective-permute-done.2.refs_3_
  54.6 2.2 %collective-permute-start.10 = (bf16[2,1024,128]{2,1,0:T(8,128)(2,1)S(1)}, bf16[2,1024,128]{2,1,0:T(8,128)(2,1)S(1)}, u32[]{:S(2)}, u32[]{:S(2)}) collective-permute-start(bf16[2,1024,128]{2,1,0:T(8,128)(2,1)S(1)} %collective-permute-done.refs_1_), channel_id=1, source_target_pairs={{0,8},{8,0},{16,24},{24,16},{32,40},{40,32},{48,56},{56,48},{1,9},... | collective-permute-start | bytes 1572872 | tf_op jit(solution)/shard_map/ppermute | solution.py:373
  56.8 0.1 collective-permute-start.11
  56.9 0.4 collective-permute-start.12
  57.3 0.1 collective-permute-start.9
  57.4 0.9 collective-permute-done.10.refs_5_
  58.3 2.8 %collective-permute-start.7 = (bf16[8,128,128]{2,1,0:T(8,128)(2,1)}, bf16[8,128,128]{2,1,0:T(8,128)(2,1)}, u32[]{:S(2)}, u32[]{:S(2)}) collective-permute-start(bf16[8,128,128]{2,1,0:T(8,128)(2,1)} %get-tuple-element.36), channel_id=1, source_target_pairs={{0,128},{64,192},{128,0},{192,64},{1,129},{65,193},{129,1},{193,65... | collective-permute-start | bytes 786440 | tf_op jit(solution)/shard_map/ppermute | solution.py:373
  61.1 0.0 collective-permute-done.11.refs_6_
  61.1 0.5 collective-permute-start.8
  61.6 4.2 %all-to-all-start.2 = ((bf16[8,128,128]{2,1,0:T(8,128)(2,1)}), bf16[8,128,128]{2,1,0:T(8,128)(2,1)S(1)}, u32[]{:S(2)}, u32[]{:S(2)}) async-start(bf16[8,128,128]{2,1,0:T(8,128)(2,1)} %get-tuple-element.32.y_ref), calls=%async_computation.2 | async-start | bytes 524288 | tf_op jit(solution)/shard_map/all_to_all | solution.py:381
  65.8 2.6 %shard_map.79.first_ref = f32[1024,128]{1,0:T(8,128)S(1)} custom-call(s32[1]{0:T(128)} %bitcast.6.place_ref, bf16[8,128,128]{2,1,0:T(8,128)(2,1)} %get-tuple-element.32.y_ref, bf16[2,1024,128]{2,1,0:T(8,128)(2,1)S(1)} %copy-done.1, bf16[2,1024,128]{2,1,0:T(8,128)(2,1)S(1)} %collective-permute-done.refs_1_, ...), custom_call_target="tpu_custom_call" | custom-call | flops 2000000000 | bytes 4000000 | tf_op jit(solution)/shard_map/pallas_call | solution.py:281
  68.4 4.7 %collective-permute-done.7.part2 = bf16[8,128,128]{2,1,0:T(8,128)(2,1)} collective-permute-done((bf16[8,128,128]{2,1,0:T(8,128)(2,1)}, bf16[8,128,128]{2,1,0:T(8,128)(2,1)}, u32[]{:S(2)}, u32[]{:S(2)}) %collective-permute-start.7) | collective-permute-done | bytes 262176 | tf_op jit(solution)/shard_map/ppermute | solution.py:373
  73.1 2.1 %collective-permute-done.8.part3 = bf16[8,128,128]{2,1,0:T(8,128)(2,1)} collective-permute-done((bf16[8,128,128]{2,1,0:T(8,128)(2,1)}, bf16[8,128,128]{2,1,0:T(8,128)(2,1)}, u32[]{:S(2)}, u32[]{:S(2)}) %collective-permute-start.8) | collective-permute-done | bytes 262176 | tf_op jit(solution)/shard_map/ppermute | solution.py:373
  75.2 4.1 %shard_map.80 = (bf16[256,8,128]{2,1,0:T(8,128)(2,1)}, bf16[4,128,128]{2,1,0:T(8,128)(2,1)S(1)}, bf16[4,128,128]{2,1,0:T(8,128)(2,1)S(1)}) custom-call(s32[1]{0:T(128)} %bitcast.6.place_ref, f32[8,128,128]{2,1,0:T(8,128)S(1)} %copy-done.5, bf16[8,128,128]{2,1,0:T(8,128)(2,1)} %collective-permute-done.6.part1, ...), custom_call_target="tpu_custom_call" | custom-call | flops 2000000000 | bytes 4000000 | tf_op jit(solution)/shard_map/pallas_call | solution.py:281
  79.3 0.0 copy-start.2
  79.3 0.6 copy-done.2
  80.0 13.8 %all-to-all-start.3 = ((bf16[256,8,128]{2,1,0:T(8,128)(2,1)}), bf16[256,8,128]{2,1,0:T(8,128)(2,1)S(1)}, u32[]{:S(2)}, u32[]{:S(2)}) async-start(bf16[256,8,128]{2,1,0:T(8,128)(2,1)} %get-tuple-element.48), calls=%async_computation.3 | async-start | bytes 1048576 | tf_op jit(solution)/shard_map/all_to_all | solution.py:414
  93.8 2.2 %collective-permute-start.13 = (bf16[4,128,128]{2,1,0:T(8,128)(2,1)}, bf16[4,128,128]{2,1,0:T(8,128)(2,1)S(1)}, u32[]{:S(2)}, u32[]{:S(2)}) collective-permute-start(bf16[4,128,128]{2,1,0:T(8,128)(2,1)} %copy-done.2), channel_id=1, source_target_pairs={{0,8},{8,0},{16,24},{24,16},{32,40},{40,32},{48,56},{56,48},{1,9},... | collective-permute-start | bytes 393224 | tf_op jit(solution)/shard_map/ppermute | solution.py:373
  96.0 1.2 %collective-permute-done.13.got_ref = bf16[4,128,128]{2,1,0:T(8,128)(2,1)S(1)} collective-permute-done((bf16[4,128,128]{2,1,0:T(8,128)(2,1)}, bf16[4,128,128]{2,1,0:T(8,128)(2,1)S(1)}, u32[]{:S(2)}, u32[]{:S(2)}) %collective-permute-start.13) | collective-permute-done | bytes 131104 | tf_op jit(solution)/shard_map/ppermute | solution.py:373
  97.3 0.1 collective-permute-start.14
  97.4 2.0 %collective-permute-start.15 = (bf16[2,128,128]{2,1,0:T(8,128)(2,1)S(1)}, bf16[2,128,128]{2,1,0:T(8,128)(2,1)S(1)}, u32[]{:S(2)}, u32[]{:S(2)}) collective-permute-start(bf16[2,128,128]{2,1,0:T(8,128)(2,1)S(1)} %get-tuple-element.45), channel_id=1, source_target_pairs={{0,32},{8,40},{16,48},{24,56},{32,0},{40,8},{48,16},{56,24},{1,33}... | collective-permute-start | bytes 196616 | tf_op jit(solution)/shard_map/ppermute | solution.py:373
  99.3 1.9 %collective-permute-start.16 = (bf16[2,128,128]{2,1,0:T(8,128)(2,1)S(1)}, bf16[2,128,128]{2,1,0:T(8,128)(2,1)S(1)}, u32[]{:S(2)}, u32[]{:S(2)}) collective-permute-start(bf16[2,128,128]{2,1,0:T(8,128)(2,1)S(1)} %get-tuple-element.46), channel_id=1, source_target_pairs={{0,48},{8,56},{16,32},{24,40},{32,16},{40,24},{48,0},{56,8},{1,49}... | collective-permute-start | bytes 196616 | tf_op jit(solution)/shard_map/ppermute | solution.py:373
  101.2 2.2 %copy-done = bf16[4,1024,512]{2,1,0:T(8,128)(2,1)S(1)} copy-done((bf16[4,1024,512]{2,1,0:T(8,128)(2,1)S(1)}, bf16[4,1024,512]{2,1,0:T(8,128)(2,1)}, u32[]{:S(2)}) %copy-start) | copy-done | bytes 4194328
  103.4 1.2 %shard_map.78 = (bf16[128,1024]{1,0:T(8,128)(2,1)}, f32[128,1024]{1,0:T(8,128)S(1)}) custom-call(bf16[8,128,128]{2,1,0:T(8,128)(2,1)S(1)} %all-to-all-done.2.y_ref, bf16[4,1024,512]{2,1,0:T(8,128)(2,1)S(1)} %copy-done, bf16[4,1024,512]{2,1,0:T(8,128)(2,1)S(1)} %copy-done), custom_call_target="tpu_custom_call" | custom-call | flops 500000000 | bytes 4000000 | tf_op jit(solution)/shard_map/pallas_call | solution.py:350
  104.6 0.0 collective-permute-done.15.refs_1_
  104.6 2.6 %collective-permute-done.16.refs_2_ = bf16[2,128,128]{2,1,0:T(8,128)(2,1)S(1)} collective-permute-done((bf16[2,128,128]{2,1,0:T(8,128)(2,1)S(1)}, bf16[2,128,128]{2,1,0:T(8,128)(2,1)S(1)}, u32[]{:S(2)}, u32[]{:S(2)}) %collective-permute-start.16) | collective-permute-done | bytes 65568 | tf_op jit(solution)/shard_map/ppermute | solution.py:373
  107.3 1.5 %shard_map.82 = bf16[128,1024]{1,0:T(8,128)(2,1)} custom-call(s32[1]{0:T(128)} %bitcast.6.place_ref, bf16[4,128,128]{2,1,0:T(8,128)(2,1)S(1)} %get-tuple-element.42.keep_ref, bf16[4,128,128]{2,1,0:T(8,128)(2,1)S(1)} %collective-permute-done.13.got_ref, bf16[2,128,128]{2,1,0:T(8,128)(2,1)S(1)} %collective-permute-done.14.refs_0_, ...), custom_call_target="tpu_custom_call" | custom-call | flops 500000000 | bytes 4000000 | tf_op jit(solution)/shard_map/pallas_call | solution.py:350
  108.8 6.4 %all-to-all-done.3.in_ref = bf16[256,8,128]{2,1,0:T(8,128)(2,1)S(1)} async-done(((bf16[256,8,128]{2,1,0:T(8,128)(2,1)}), bf16[256,8,128]{2,1,0:T(8,128)(2,1)S(1)}, u32[]{:S(2)}, u32[]{:S(2)}) %all-to-all-start.3) | async-done | bytes 524320 | tf_op jit(solution)/shard_map/all_to_all | solution.py:414
  115.3 0.8 shard_map.83
  (18 shorter events, 0.1 us)
Async XLA Ops:
  0.6 24.9 %copy-start.6 = (s32[1,32,27]{1,0,2:T(1,128)S(1)}, s32[1,32,27]{1,0,2:T(1,128)}, u32[]{:S(2)}) copy-start(s32[1,32,27]{1,0,2:T(1,128)} %param.8) | copy-start | bytes 10372
  0.6 32.4 %copy-start.3 = (s32[1,32]{1,0:T(1,128)S(1)}, s32[1,32]{1,0:T(1,128)}, u32[]{:S(2)}) copy-start(s32[1,32]{1,0:T(1,128)} %param.9) | copy-start | bytes 388
  3.4 13.0 %all-to-all-start = ((bf16[8,128,128]{2,1,0:T(8,128)(2,1)}), bf16[8,128,128]{2,1,0:T(8,128)(2,1)S(1)}, u32[]{:S(2)}, u32[]{:S(2)}) async-start(bf16[8,128,128]{2,1,0:T(8,128)(2,1)} %shard_map.77), calls=%async_computation | async-start | bytes 524288 | tf_op jit(solution)/shard_map/all_to_all | solution.py:381
  16.5 12.9 %collective-permute-start.3 = (bf16[8,128,128]{2,1,0:T(8,128)(2,1)S(1)}, bf16[8,128,128]{2,1,0:T(8,128)(2,1)S(1)}, u32[]{:S(2)}, u32[]{:S(2)}) collective-permute-start(bf16[8,128,128]{2,1,0:T(8,128)(2,1)S(1)} %all-to-all-done.kv0), channel_id=1, source_target_pairs={{0,64},{64,0},{128,192},{192,128},{1,65},{65,1},{129,193},{193,129... | collective-permute-start | bytes 786440 | tf_op jit(solution)/shard_map/ppermute | solution.py:373
  17.0 15.2 %collective-permute-start.4 = (bf16[8,128,128]{2,1,0:T(8,128)(2,1)S(1)}, bf16[8,128,128]{2,1,0:T(8,128)(2,1)S(1)}, u32[]{:S(2)}, u32[]{:S(2)}) collective-permute-start(bf16[8,128,128]{2,1,0:T(8,128)(2,1)S(1)} %all-to-all-done.kv0), channel_id=1, source_target_pairs={{0,128},{64,192},{128,0},{192,64},{1,129},{65,193},{129,1},{193,65... | collective-permute-start | bytes 786440 | tf_op jit(solution)/shard_map/ppermute | solution.py:373
  19.6 13.4 %collective-permute-start.5 = (bf16[8,128,128]{2,1,0:T(8,128)(2,1)S(1)}, bf16[8,128,128]{2,1,0:T(8,128)(2,1)S(1)}, u32[]{:S(2)}, u32[]{:S(2)}) collective-permute-start(bf16[8,128,128]{2,1,0:T(8,128)(2,1)S(1)} %all-to-all-done.kv0), channel_id=1, source_target_pairs={{0,192},{64,128},{128,64},{192,0},{1,193},{65,129},{129,65},{193,1... | collective-permute-start | bytes 786440 | tf_op jit(solution)/shard_map/ppermute | solution.py:373
  20.3 11.9 %all-to-all-start.1 = ((bf16[8,128,128]{2,1,0:T(8,128)(2,1)}), bf16[8,128,128]{2,1,0:T(8,128)(2,1)S(1)}, u32[]{:S(2)}, u32[]{:S(2)}) async-start(bf16[8,128,128]{2,1,0:T(8,128)(2,1)} %get-tuple-element.29), calls=%async_computation.1 | async-start | bytes 524288 | tf_op jit(solution)/shard_map/all_to_all | solution.py:381
  25.6 28.9 %collective-permute-start = (bf16[2,1024,128]{2,1,0:T(8,128)(2,1)}, bf16[2,1024,128]{2,1,0:T(8,128)(2,1)S(1)}, u32[]{:S(2)}, u32[]{:S(2)}) collective-permute-start(bf16[2,1024,128]{2,1,0:T(8,128)(2,1)} %get-tuple-element.38.refs_0_), channel_id=1, source_target_pairs={{0,16},{8,24},{16,0},{24,8},{32,48},{40,56},{48,32},{56,40},{1,17}... | collective-permute-start | bytes 1572872 | tf_op jit(solution)/shard_map/ppermute | solution.py:373
  27.0 27.6 %collective-permute-start.1 = (bf16[2,1024,128]{2,1,0:T(8,128)(2,1)}, bf16[2,1024,128]{2,1,0:T(8,128)(2,1)S(1)}, u32[]{:S(2)}, u32[]{:S(2)}) collective-permute-start(bf16[2,1024,128]{2,1,0:T(8,128)(2,1)} %get-tuple-element.38.refs_0_), channel_id=1, source_target_pairs={{0,32},{8,40},{16,48},{24,56},{32,0},{40,8},{48,16},{56,24},{1,33}... | collective-permute-start | bytes 1572872 | tf_op jit(solution)/shard_map/ppermute | solution.py:373
  29.4 25.2 %collective-permute-start.2 = (bf16[2,1024,128]{2,1,0:T(8,128)(2,1)}, bf16[2,1024,128]{2,1,0:T(8,128)(2,1)S(1)}, u32[]{:S(2)}, u32[]{:S(2)}) collective-permute-start(bf16[2,1024,128]{2,1,0:T(8,128)(2,1)} %get-tuple-element.38.refs_0_), channel_id=1, source_target_pairs={{0,48},{8,56},{16,32},{24,40},{32,16},{40,24},{48,0},{56,8},{1,49}... | collective-permute-start | bytes 1572872 | tf_op jit(solution)/shard_map/ppermute | solution.py:373
  33.0 24.3 %copy-start.1 = (bf16[2,1024,128]{2,1,0:T(8,128)(2,1)S(1)}, bf16[2,1024,128]{2,1,0:T(8,128)(2,1)}, u32[]{:S(2)}) copy-start(bf16[2,1024,128]{2,1,0:T(8,128)(2,1)} %get-tuple-element.38.refs_0_) | copy-start | bytes 1572868
  53.7 0.8 copy-start.4
  54.6 3.7 %collective-permute-start.10 = (bf16[2,1024,128]{2,1,0:T(8,128)(2,1)S(1)}, bf16[2,1024,128]{2,1,0:T(8,128)(2,1)S(1)}, u32[]{:S(2)}, u32[]{:S(2)}) collective-permute-start(bf16[2,1024,128]{2,1,0:T(8,128)(2,1)S(1)} %collective-permute-done.refs_1_), channel_id=1, source_target_pairs={{0,8},{8,0},{16,24},{24,16},{32,40},{40,32},{48,56},{56,48},{1,9},... | collective-permute-start | bytes 1572872 | tf_op jit(solution)/shard_map/ppermute | solution.py:373
  56.8 4.4 %collective-permute-start.11 = (bf16[2,1024,128]{2,1,0:T(8,128)(2,1)S(1)}, bf16[2,1024,128]{2,1,0:T(8,128)(2,1)S(1)}, u32[]{:S(2)}, u32[]{:S(2)}) collective-permute-start(bf16[2,1024,128]{2,1,0:T(8,128)(2,1)S(1)} %collective-permute-done.1.refs_2_), channel_id=1, source_target_pairs={{0,8},{8,0},{16,24},{24,16},{32,40},{40,32},{48,56},{56,48},{1,9},... | collective-permute-start | bytes 1572872 | tf_op jit(solution)/shard_map/ppermute | solution.py:373
  56.9 9.0 %collective-permute-start.12 = (bf16[2,1024,128]{2,1,0:T(8,128)(2,1)S(1)}, bf16[2,1024,128]{2,1,0:T(8,128)(2,1)}, u32[]{:S(2)}, u32[]{:S(2)}) collective-permute-start(bf16[2,1024,128]{2,1,0:T(8,128)(2,1)S(1)} %collective-permute-done.2.refs_3_), channel_id=1, source_target_pairs={{0,8},{8,0},{16,24},{24,16},{32,40},{40,32},{48,56},{56,48},{1,9},... | collective-permute-start | bytes 1572872 | tf_op jit(solution)/shard_map/ppermute | solution.py:373
  57.3 8.5 %collective-permute-start.9 = (bf16[2,1024,128]{2,1,0:T(8,128)(2,1)S(1)}, bf16[2,1024,128]{2,1,0:T(8,128)(2,1)}, u32[]{:S(2)}, u32[]{:S(2)}) collective-permute-start(bf16[2,1024,128]{2,1,0:T(8,128)(2,1)S(1)} %copy-done.1), channel_id=1, source_target_pairs={{0,8},{8,0},{16,24},{24,16},{32,40},{40,32},{48,56},{56,48},{1,9},... | collective-permute-start | bytes 1572872 | tf_op jit(solution)/shard_map/ppermute | solution.py:373
  57.4 11.0 %collective-permute-start.6 = (bf16[8,128,128]{2,1,0:T(8,128)(2,1)}, bf16[8,128,128]{2,1,0:T(8,128)(2,1)}, u32[]{:S(2)}, u32[]{:S(2)}) collective-permute-start(bf16[8,128,128]{2,1,0:T(8,128)(2,1)} %get-tuple-element.35), channel_id=1, source_target_pairs={{0,64},{64,0},{128,192},{192,128},{1,65},{65,1},{129,193},{193,129... | collective-permute-start | bytes 786440 | tf_op jit(solution)/shard_map/ppermute | solution.py:373
  58.3 14.8 %collective-permute-start.7 = (bf16[8,128,128]{2,1,0:T(8,128)(2,1)}, bf16[8,128,128]{2,1,0:T(8,128)(2,1)}, u32[]{:S(2)}, u32[]{:S(2)}) collective-permute-start(bf16[8,128,128]{2,1,0:T(8,128)(2,1)} %get-tuple-element.36), channel_id=1, source_target_pairs={{0,128},{64,192},{128,0},{192,64},{1,129},{65,193},{129,1},{193,65... | collective-permute-start | bytes 786440 | tf_op jit(solution)/shard_map/ppermute | solution.py:373
  61.1 14.0 %collective-permute-start.8 = (bf16[8,128,128]{2,1,0:T(8,128)(2,1)}, bf16[8,128,128]{2,1,0:T(8,128)(2,1)}, u32[]{:S(2)}, u32[]{:S(2)}) collective-permute-start(bf16[8,128,128]{2,1,0:T(8,128)(2,1)} %get-tuple-element.37), channel_id=1, source_target_pairs={{0,192},{64,128},{128,64},{192,0},{1,193},{65,129},{129,65},{193,1... | collective-permute-start | bytes 786440 | tf_op jit(solution)/shard_map/ppermute | solution.py:373
  61.6 18.4 %all-to-all-start.2 = ((bf16[8,128,128]{2,1,0:T(8,128)(2,1)}), bf16[8,128,128]{2,1,0:T(8,128)(2,1)S(1)}, u32[]{:S(2)}, u32[]{:S(2)}) async-start(bf16[8,128,128]{2,1,0:T(8,128)(2,1)} %get-tuple-element.32.y_ref), calls=%async_computation.2 | async-start | bytes 524288 | tf_op jit(solution)/shard_map/all_to_all | solution.py:381
  65.8 9.4 %copy-start.5 = (f32[8,128,128]{2,1,0:T(8,128)S(1)}, f32[8,128,128]{2,1,0:T(8,128)}, u32[]{:S(2)}) copy-start(f32[8,128,128]{2,1,0:T(8,128)} %copy-done.4) | copy-start | bytes 1572868
  79.3 0.7 copy-start.2
  80.0 35.3 %all-to-all-start.3 = ((bf16[256,8,128]{2,1,0:T(8,128)(2,1)}), bf16[256,8,128]{2,1,0:T(8,128)(2,1)S(1)}, u32[]{:S(2)}, u32[]{:S(2)}) async-start(bf16[256,8,128]{2,1,0:T(8,128)(2,1)} %get-tuple-element.48), calls=%async_computation.3 | async-start | bytes 1048576 | tf_op jit(solution)/shard_map/all_to_all | solution.py:414
  93.8 3.4 %collective-permute-start.13 = (bf16[4,128,128]{2,1,0:T(8,128)(2,1)}, bf16[4,128,128]{2,1,0:T(8,128)(2,1)S(1)}, u32[]{:S(2)}, u32[]{:S(2)}) collective-permute-start(bf16[4,128,128]{2,1,0:T(8,128)(2,1)} %copy-done.2), channel_id=1, source_target_pairs={{0,8},{8,0},{16,24},{24,16},{32,40},{40,32},{48,56},{56,48},{1,9},... | collective-permute-start | bytes 393224 | tf_op jit(solution)/shard_map/ppermute | solution.py:373
  97.3 7.3 %collective-permute-start.14 = (bf16[2,128,128]{2,1,0:T(8,128)(2,1)S(1)}, bf16[2,128,128]{2,1,0:T(8,128)(2,1)S(1)}, u32[]{:S(2)}, u32[]{:S(2)}) collective-permute-start(bf16[2,128,128]{2,1,0:T(8,128)(2,1)S(1)} %get-tuple-element.44), channel_id=1, source_target_pairs={{0,16},{8,24},{16,0},{24,8},{32,48},{40,56},{48,32},{56,40},{1,17}... | collective-permute-start | bytes 196616 | tf_op jit(solution)/shard_map/ppermute | solution.py:373
  97.4 7.3 %collective-permute-start.15 = (bf16[2,128,128]{2,1,0:T(8,128)(2,1)S(1)}, bf16[2,128,128]{2,1,0:T(8,128)(2,1)S(1)}, u32[]{:S(2)}, u32[]{:S(2)}) collective-permute-start(bf16[2,128,128]{2,1,0:T(8,128)(2,1)S(1)} %get-tuple-element.45), channel_id=1, source_target_pairs={{0,32},{8,40},{16,48},{24,56},{32,0},{40,8},{48,16},{56,24},{1,33}... | collective-permute-start | bytes 196616 | tf_op jit(solution)/shard_map/ppermute | solution.py:373
  99.3 7.9 %collective-permute-start.16 = (bf16[2,128,128]{2,1,0:T(8,128)(2,1)S(1)}, bf16[2,128,128]{2,1,0:T(8,128)(2,1)S(1)}, u32[]{:S(2)}, u32[]{:S(2)}) collective-permute-start(bf16[2,128,128]{2,1,0:T(8,128)(2,1)S(1)} %get-tuple-element.46), channel_id=1, source_target_pairs={{0,48},{8,56},{16,32},{24,40},{32,16},{40,24},{48,0},{56,8},{1,49}... | collective-permute-start | bytes 196616 | tf_op jit(solution)/shard_map/ppermute | solution.py:373
  101.2 2.2 %copy-start = (bf16[4,1024,512]{2,1,0:T(8,128)(2,1)S(1)}, bf16[4,1024,512]{2,1,0:T(8,128)(2,1)}, u32[]{:S(2)}) copy-start(bf16[4,1024,512]{2,1,0:T(8,128)(2,1)} %refs_5_.1) | copy-start | bytes 12582916

commit v5 on v4

--- a/solution.py
+++ b/solution.py
@@ -10,7 +10,7 @@
 HEAD_DIM = 64
 BLOCK = 128
 MAXN = 27
-LARGE, SMALL = 8, 4
+LARGE = 8
 SLOTS = 28
 BF = jnp.bfloat16
 F32 = jnp.float32
@@ -48,10 +48,12 @@
 
 
 def keys_kernel(tok_ref, w_ref, kv_ref, rows):
-    step = pl.program_id(0)
-    rows[step] = dot(tok_ref[...], w_ref[0]).astype(BF)
-
-    @pl.when(step == 1)
+    step, part = pl.program_id(0), pl.program_id(1)
+    size = w_ref.shape[2]
+    cols = pl.ds(pl.multiple_of(part * size, size), size)
+    rows[step, :, cols] = dot(tok_ref[...], w_ref[0]).astype(BF)
+
+    @pl.when((step == 1) & (part == pl.num_programs(1) - 1))
     def _():
         by_head(rows, kv_ref)
 
@@ -72,16 +74,17 @@
         by_head(rows, qd_ref)
 
 
-def project(kernel, arrays, weights, pick, outs):
+def project(kernel, arrays, weights, pick, outs, cuts=1):
     rows, width = arrays[0].shape
+    columns = HEADS * HEAD_DIM
     return pl.pallas_call(
         kernel,
-        grid=(2,),
-        in_specs=[pl.BlockSpec((rows, width), lambda step: (0, 0)) for _ in arrays]
-        + [pl.BlockSpec((1, width, HEADS * HEAD_DIM), lambda step: (pick(step), 0, 0))],
-        out_specs=[pl.BlockSpec(out, lambda step: (0, 0, 0)) for out in outs],
+        grid=(2, cuts),
+        in_specs=[pl.BlockSpec((rows, width), lambda step, part: (0, 0)) for _ in arrays]
+        + [pl.BlockSpec((1, width, columns // cuts), lambda step, part: (pick(step), 0, part))],
+        out_specs=[pl.BlockSpec(out, lambda step, part: (0, 0, 0)) for out in outs],
         out_shape=[jax.ShapeDtypeStruct(out, BF) for out in outs],
-        scratch_shapes=[pltpu.VMEM((2, rows, HEADS * HEAD_DIM), BF)],
+        scratch_shapes=[pltpu.VMEM((2, rows, columns), BF)],
         cost_estimate=pl.CostEstimate(
             flops=1_000_000_000, bytes_accessed=4_000_000, transcendentals=0
         ),
@@ -115,14 +118,17 @@
                 kvt[idx] = kvs[idx].T
 
     count = counts_ref[block]
-    large = (count + SMALL - 1) // LARGE
-    small = (count - large * LARGE + SMALL - 1) // SMALL
+    eights = (count + 1) // 8
+    rest = count - eights * 8
+    fours = (rest + 1) // 4
+    twos = (rest - fours * 4 + 1) // 2
 
     def sweep(visit, carry):
-        carry = lax.fori_loop(0, large, lambda i, c: visit(LARGE, i * LARGE, c), carry)
-        return lax.fori_loop(
-            0, small, lambda i, c: visit(SMALL, large * LARGE + i * SMALL, c), carry
-        )
+        after = eights * 8
+        carry = lax.fori_loop(0, eights, lambda i, c: visit(8, i * 8, c), carry)
+        carry = lax.fori_loop(0, fours, lambda i, c: visit(4, after + i * 4, c), carry)
+        after = after + fours * 4
+        return lax.fori_loop(0, twos, lambda i, c: visit(2, after + i * 2, c), carry)
 
     def place(slot):
         raw = lists_ref[block, jnp.minimum(slot, MAXN - 1)]
@@ -379,7 +385,10 @@
     group = lax.axis_index(ROW).astype(jnp.int32).reshape(1)
     place = lax.axis_index(HEAD).astype(jnp.int32).reshape(1)
     swap = lambda array: lax.all_to_all(array, HEAD, 0, 0, tiled=True)
-    (kv,) = project(keys_kernel, [tokens[0]], weights, lambda step: step + 1, [(HEADS, BLOCK, 128)])
+    (kv,) = project(
+        keys_kernel, [tokens[0]], weights, lambda step: step + 1,
+        [(HEADS, BLOCK, 128)], 2,
+    )
     kv = swap(kv)
     qd, xt = project(
         queries_kernel, [tokens[0], cotangent[0]], weights,

time: 117 us -> 117 us (level)
  waiting for transfers between devices: 25.1 us -> 26.3 us
  transfers between devices with their start and end apart: 21 -> 21, of which waited for: 10 -> 10; matrix products, arithmetic and copies ran while one was open for 0% -> 0% of each run, Pallas kernels for 29% -> 28%
where the time goes in v5:
time: 117 us
  starting transfers between devices  49.1 us (42%)
  Pallas kernels  36.9 us (32%)
  waiting for transfers between devices  26.3 us (22%)
  local copies, waits for them, and re-layouts  3.74 us (3%)
    ppermute x17, starting transfers between devices, across(): lax.ppermute(array, axes, [(i, i ^ flip) for i in range(lax.axis_size(axe...  20.3 us
    pallas_call x1, Pallas kernels, attend(): pl.pallas_call(attend_kernel, grid_spec=pltpu.PrefetchScalarGridSpec(num_...  19.8 us
    all_to_all x3, starting transfers between devices, body(): swap = lambda array: lax.all_to_all(array, HEAD, 0, 0, tiled=True)  15.7 us
    ppermute x17, waiting for transfers between devices, across(): lax.ppermute(array, axes, [(i, i ^ flip) for i in range(lax.axis_size(axe...  13.6 us
    all_to_all x1, starting transfers between devices, body(): terms = lax.all_to_all(terms, SEQ + ('rep',), 0, 0, tiled=True)  13.2 us
    pallas_call x2, Pallas kernels, project(): pl.pallas_call(kernel, grid=(2, cuts), in_specs=[pl.BlockSpec((rows, widt...  6.8 us
    pallas_call x2, Pallas kernels, grads_call(): pl.pallas_call(kernel, in_specs=[pl.BlockSpec(memory_space=pltpu.SMEM)] +...  6.7 us
    all_to_all x1, waiting for transfers between devices, body(): terms = lax.all_to_all(terms, SEQ + ('rep',), 0, 0, tiled=True)  6.43 us
  transfers between devices with their start and end apart: 21, of which 10 were waited for; matrix products, arithmetic and copies ran while one was open for 0% of the time, Pallas kernels for 28%

profile of v5, /device:TPU:1, one launch (start us, length us, event | category | flops | bytes accessed | tf_op | source)
XLA Modules:
  0.0 116.8 jit_solution(5597954973847517194)
XLA Ops:
  0.7 3.8 %shard_map.77 = bf16[8,128,128]{2,1,0:T(8,128)(2,1)} custom-call(bf16[128,1024]{1,0:T(8,128)(2,1)} %bitcast.10, bf16[4,1024,512]{2,1,0:T(8,128)(2,1)} %refs_5_.1), custom_call_target="tpu_custom_call" | custom-call | flops 1000000000 | bytes 4000000 | tf_op jit(solution)/shard_map/pallas_call | solution.py:80
  4.5 6.5 %all-to-all-start = ((bf16[8,128,128]{2,1,0:T(8,128)(2,1)}), bf16[8,128,128]{2,1,0:T(8,128)(2,1)S(1)}, u32[]{:S(2)}, u32[]{:S(2)}) async-start(bf16[8,128,128]{2,1,0:T(8,128)(2,1)} %shard_map.77), calls=%async_computation | async-start | bytes 524288 | tf_op jit(solution)/shard_map/all_to_all | solution.py:387
  11.0 3.0 %shard_map.76 = (bf16[8,128,128]{2,1,0:T(8,128)(2,1)}, bf16[2,1024,128]{2,1,0:T(8,128)(2,1)}) custom-call(bf16[128,1024]{1,0:T(8,128)(2,1)} %bitcast.11, bf16[128,1024]{1,0:T(8,128)(2,1)} %bitcast.12, bf16[4,1024,512]{2,1,0:T(8,128)(2,1)} %refs_5_.1), custom_call_target="tpu_custom_call" | custom-call | flops 1000000000 | bytes 4000000 | tf_op jit(solution)/shard_map/pallas_call | solution.py:80
  14.0 3.5 %all-to-all-done.kv0 = bf16[8,128,128]{2,1,0:T(8,128)(2,1)S(1)} async-done(((bf16[8,128,128]{2,1,0:T(8,128)(2,1)}), bf16[8,128,128]{2,1,0:T(8,128)(2,1)S(1)}, u32[]{:S(2)}, u32[]{:S(2)}) %all-to-all-start) | async-done | bytes 262176 | tf_op jit(solution)/shard_map/all_to_all | solution.py:387
  17.5 0.5 collective-permute-start.3
  18.0 2.6 %collective-permute-start.4 = (bf16[8,128,128]{2,1,0:T(8,128)(2,1)S(1)}, bf16[8,128,128]{2,1,0:T(8,128)(2,1)S(1)}, u32[]{:S(2)}, u32[]{:S(2)}) collective-permute-start(bf16[8,128,128]{2,1,0:T(8,128)(2,1)S(1)} %all-to-all-done.kv0), channel_id=1, source_target_pairs={{0,128},{64,192},{128,0},{192,64},{1,129},{65,193},{129,1},{193,65... | collective-permute-start | bytes 786440 | tf_op jit(solution)/shard_map/ppermute | solution.py:379
  20.6 0.7 collective-permute-start.5
  21.3 5.2 %all-to-all-start.1 = ((bf16[8,128,128]{2,1,0:T(8,128)(2,1)}), bf16[8,128,128]{2,1,0:T(8,128)(2,1)S(1)}, u32[]{:S(2)}, u32[]{:S(2)}) async-start(bf16[8,128,128]{2,1,0:T(8,128)(2,1)} %get-tuple-element.29), calls=%async_computation.1 | async-start | bytes 524288 | tf_op jit(solution)/shard_map/all_to_all | solution.py:387
  26.5 0.1 copy.8
  26.6 1.4 %collective-permute-start = (bf16[2,1024,128]{2,1,0:T(8,128)(2,1)}, bf16[2,1024,128]{2,1,0:T(8,128)(2,1)S(1)}, u32[]{:S(2)}, u32[]{:S(2)}) collective-permute-start(bf16[2,1024,128]{2,1,0:T(8,128)(2,1)} %get-tuple-element.38.refs_0_), channel_id=1, source_target_pairs={{0,16},{8,24},{16,0},{24,8},{32,48},{40,56},{48,32},{56,40},{1,17}... | collective-permute-start | bytes 1572872 | tf_op jit(solution)/shard_map/ppermute | solution.py:379
  28.0 2.4 %collective-permute-start.1 = (bf16[2,1024,128]{2,1,0:T(8,128)(2,1)}, bf16[2,1024,128]{2,1,0:T(8,128)(2,1)S(1)}, u32[]{:S(2)}, u32[]{:S(2)}) collective-permute-start(bf16[2,1024,128]{2,1,0:T(8,128)(2,1)} %get-tuple-element.38.refs_0_), channel_id=1, source_target_pairs={{0,32},{8,40},{16,48},{24,56},{32,0},{40,8},{48,16},{56,24},{1,33}... | collective-permute-start | bytes 1572872 | tf_op jit(solution)/shard_map/ppermute | solution.py:379
  30.4 0.0 collective-permute-done.3.kv1
  30.4 0.1 collective-permute-start.2
  30.5 2.7 %all-to-all-done.1.qd_ref = bf16[8,128,128]{2,1,0:T(8,128)(2,1)S(1)} async-done(((bf16[8,128,128]{2,1,0:T(8,128)(2,1)}), bf16[8,128,128]{2,1,0:T(8,128)(2,1)S(1)}, u32[]{:S(2)}, u32[]{:S(2)}) %all-to-all-start.1) | async-done | bytes 262176 | tf_op jit(solution)/shard_map/all_to_all | solution.py:387
  33.2 0.0 collective-permute-done.4.kv2
  33.2 0.8 collective-permute-done.5.kv3
  34.1 19.8 %attend.1 = (bf16[8,128,128]{2,1,0:T(8,128)(2,1)}, f32[8,128,128]{2,1,0:T(8,128)S(1)}, bf16[8,128,128]{2,1,0:T(8,128)(2,1)}, bf16[8,128,128]{2,1,0:T(8,128)(2,1)}, bf16[8,128,128]{2,1,0:T(8,128)(2,1)}) custom-call(s32[32,27]{1,0:T(8,128)S(1)} %bitcast.8, s32[32]{0:T(128)S(1)} %bitcast.9, s32[1]{0:T(128)} %bitcast.4.group_ref, ...), custom_call_target="tpu_custom_call" | custom-call | flops 30000001024 | bytes 4000000 | tf_op jit(solution)/shard_map/attend/pallas_call | solution.py:213
  53.9 0.8 copy-done.4
  54.7 0.0 collective-permute-done.refs_1_
  54.7 0.9 collective-permute-done.1.refs_2_
  55.6 1.8 %collective-permute-start.10 = (bf16[2,1024,128]{2,1,0:T(8,128)(2,1)S(1)}, bf16[2,1024,128]{2,1,0:T(8,128)(2,1)S(1)}, u32[]{:S(2)}, u32[]{:S(2)}) collective-permute-start(bf16[2,1024,128]{2,1,0:T(8,128)(2,1)S(1)} %collective-permute-done.refs_1_), channel_id=1, source_target_pairs={{0,8},{8,0},{16,24},{24,16},{32,40},{40,32},{48,56},{56,48},{1,9},... | collective-permute-start | bytes 1572872 | tf_op jit(solution)/shard_map/ppermute | solution.py:379
  57.4 0.0 collective-permute-start.11
  57.4 0.5 collective-permute-start.12
  57.9 0.0 collective-permute-start.9
  57.9 0.0 collective-permute-start.6
  57.9 1.0 collective-permute-done.10.refs_5_
  59.0 3.6 %collective-permute-start.7 = (bf16[8,128,128]{2,1,0:T(8,128)(2,1)}, bf16[8,128,128]{2,1,0:T(8,128)(2,1)}, u32[]{:S(2)}, u32[]{:S(2)}) collective-permute-start(bf16[8,128,128]{2,1,0:T(8,128)(2,1)} %get-tuple-element.36), channel_id=1, source_target_pairs={{0,128},{64,192},{128,0},{192,64},{1,129},{65,193},{129,1},{193,65... | collective-permute-start | bytes 786440 | tf_op jit(solution)/shard_map/ppermute | solution.py:379
  62.5 0.5 collective-permute-start.8
  63.0 4.0 %all-to-all-start.2 = ((bf16[8,128,128]{2,1,0:T(8,128)(2,1)}), bf16[8,128,128]{2,1,0:T(8,128)(2,1)S(1)}, u32[]{:S(2)}, u32[]{:S(2)}) async-start(bf16[8,128,128]{2,1,0:T(8,128)(2,1)} %get-tuple-element.32.y_ref), calls=%async_computation.2 | async-start | bytes 524288 | tf_op jit(solution)/shard_map/all_to_all | solution.py:387
  67.0 2.6 %shard_map.79.first_ref = f32[1024,128]{1,0:T(8,128)S(1)} custom-call(s32[1]{0:T(128)} %bitcast.6.place_ref, bf16[8,128,128]{2,1,0:T(8,128)(2,1)} %get-tuple-element.32.y_ref, bf16[2,1024,128]{2,1,0:T(8,128)(2,1)S(1)} %copy-done.1, bf16[2,1024,128]{2,1,0:T(8,128)(2,1)S(1)} %collective-permute-done.refs_1_, ...), custom_call_target="tpu_custom_call" | custom-call | flops 2000000000 | bytes 4000000 | tf_op jit(solution)/shard_map/pallas_call | solution.py:287
  69.6 4.9 %collective-permute-done.7.part2 = bf16[8,128,128]{2,1,0:T(8,128)(2,1)} collective-permute-done((bf16[8,128,128]{2,1,0:T(8,128)(2,1)}, bf16[8,128,128]{2,1,0:T(8,128)(2,1)}, u32[]{:S(2)}, u32[]{:S(2)}) %collective-permute-start.7) | collective-permute-done | bytes 262176 | tf_op jit(solution)/shard_map/ppermute | solution.py:379
  74.5 2.1 %collective-permute-done.8.part3 = bf16[8,128,128]{2,1,0:T(8,128)(2,1)} collective-permute-done((bf16[8,128,128]{2,1,0:T(8,128)(2,1)}, bf16[8,128,128]{2,1,0:T(8,128)(2,1)}, u32[]{:S(2)}, u32[]{:S(2)}) %collective-permute-start.8) | collective-permute-done | bytes 262176 | tf_op jit(solution)/shard_map/ppermute | solution.py:379
  76.6 4.1 %shard_map.80 = (bf16[256,8,128]{2,1,0:T(8,128)(2,1)}, bf16[4,128,128]{2,1,0:T(8,128)(2,1)S(1)}, bf16[4,128,128]{2,1,0:T(8,128)(2,1)S(1)}) custom-call(s32[1]{0:T(128)} %bitcast.6.place_ref, f32[8,128,128]{2,1,0:T(8,128)S(1)} %copy-done.5, bf16[8,128,128]{2,1,0:T(8,128)(2,1)} %collective-permute-done.6.part1, ...), custom_call_target="tpu_custom_call" | custom-call | flops 2000000000 | bytes 4000000 | tf_op jit(solution)/shard_map/pallas_call | solution.py:287
  80.7 0.0 copy-start.2
  80.7 0.6 copy-done.2
  81.4 13.2 %all-to-all-start.3 = ((bf16[256,8,128]{2,1,0:T(8,128)(2,1)}), bf16[256,8,128]{2,1,0:T(8,128)(2,1)S(1)}, u32[]{:S(2)}, u32[]{:S(2)}) async-start(bf16[256,8,128]{2,1,0:T(8,128)(2,1)} %get-tuple-element.48), calls=%async_computation.3 | async-start | bytes 1048576 | tf_op jit(solution)/shard_map/all_to_all | solution.py:423
  94.6 2.2 %collective-permute-start.13 = (bf16[4,128,128]{2,1,0:T(8,128)(2,1)}, bf16[4,128,128]{2,1,0:T(8,128)(2,1)S(1)}, u32[]{:S(2)}, u32[]{:S(2)}) collective-permute-start(bf16[4,128,128]{2,1,0:T(8,128)(2,1)} %copy-done.2), channel_id=1, source_target_pairs={{0,8},{8,0},{16,24},{24,16},{32,40},{40,32},{48,56},{56,48},{1,9},... | collective-permute-start | bytes 393224 | tf_op jit(solution)/shard_map/ppermute | solution.py:379
  96.8 1.2 %collective-permute-done.13.got_ref = bf16[4,128,128]{2,1,0:T(8,128)(2,1)S(1)} collective-permute-done((bf16[4,128,128]{2,1,0:T(8,128)(2,1)}, bf16[4,128,128]{2,1,0:T(8,128)(2,1)S(1)}, u32[]{:S(2)}, u32[]{:S(2)}) %collective-permute-start.13) | collective-permute-done | bytes 131104 | tf_op jit(solution)/shard_map/ppermute | solution.py:379
  98.0 0.1 collective-permute-start.14
  98.1 2.0 %collective-permute-start.15 = (bf16[2,128,128]{2,1,0:T(8,128)(2,1)S(1)}, bf16[2,128,128]{2,1,0:T(8,128)(2,1)S(1)}, u32[]{:S(2)}, u32[]{:S(2)}) collective-permute-start(bf16[2,128,128]{2,1,0:T(8,128)(2,1)S(1)} %get-tuple-element.45), channel_id=1, source_target_pairs={{0,32},{8,40},{16,48},{24,56},{32,0},{40,8},{48,16},{56,24},{1,33}... | collective-permute-start | bytes 196616 | tf_op jit(solution)/shard_map/ppermute | solution.py:379
  100.1 1.9 %collective-permute-start.16 = (bf16[2,128,128]{2,1,0:T(8,128)(2,1)S(1)}, bf16[2,128,128]{2,1,0:T(8,128)(2,1)S(1)}, u32[]{:S(2)}, u32[]{:S(2)}) collective-permute-start(bf16[2,128,128]{2,1,0:T(8,128)(2,1)S(1)} %get-tuple-element.46), channel_id=1, source_target_pairs={{0,48},{8,56},{16,32},{24,40},{32,16},{40,24},{48,0},{56,8},{1,49}... | collective-permute-start | bytes 196616 | tf_op jit(solution)/shard_map/ppermute | solution.py:379
  101.9 2.2 %copy-done = bf16[4,1024,512]{2,1,0:T(8,128)(2,1)S(1)} copy-done((bf16[4,1024,512]{2,1,0:T(8,128)(2,1)S(1)}, bf16[4,1024,512]{2,1,0:T(8,128)(2,1)}, u32[]{:S(2)}) %copy-start) | copy-done | bytes 4194328
  104.1 1.2 %shard_map.78 = (bf16[128,1024]{1,0:T(8,128)(2,1)}, f32[128,1024]{1,0:T(8,128)S(1)}) custom-call(bf16[8,128,128]{2,1,0:T(8,128)(2,1)S(1)} %all-to-all-done.2.y_ref, bf16[4,1024,512]{2,1,0:T(8,128)(2,1)S(1)} %copy-done, bf16[4,1024,512]{2,1,0:T(8,128)(2,1)S(1)} %copy-done), custom_call_target="tpu_custom_call" | custom-call | flops 500000000 | bytes 4000000 | tf_op jit(solution)/shard_map/pallas_call | solution.py:356
  105.4 0.0 collective-permute-done.15.refs_1_
  105.4 2.6 %collective-permute-done.16.refs_2_ = bf16[2,128,128]{2,1,0:T(8,128)(2,1)S(1)} collective-permute-done((bf16[2,128,128]{2,1,0:T(8,128)(2,1)S(1)}, bf16[2,128,128]{2,1,0:T(8,128)(2,1)S(1)}, u32[]{:S(2)}, u32[]{:S(2)}) %collective-permute-start.16) | collective-permute-done | bytes 65568 | tf_op jit(solution)/shard_map/ppermute | solution.py:379
  108.0 1.5 %shard_map.82 = bf16[128,1024]{1,0:T(8,128)(2,1)} custom-call(s32[1]{0:T(128)} %bitcast.6.place_ref, bf16[4,128,128]{2,1,0:T(8,128)(2,1)S(1)} %get-tuple-element.42.keep_ref, bf16[4,128,128]{2,1,0:T(8,128)(2,1)S(1)} %collective-permute-done.13.got_ref, bf16[2,128,128]{2,1,0:T(8,128)(2,1)S(1)} %collective-permute-done.14.refs_0_, ...), custom_call_target="tpu_custom_call" | custom-call | flops 500000000 | bytes 4000000 | tf_op jit(solution)/shard_map/pallas_call | solution.py:356
  109.6 6.4 %all-to-all-done.3.in_ref = bf16[256,8,128]{2,1,0:T(8,128)(2,1)S(1)} async-done(((bf16[256,8,128]{2,1,0:T(8,128)(2,1)}), bf16[256,8,128]{2,1,0:T(8,128)(2,1)S(1)}, u32[]{:S(2)}, u32[]{:S(2)}) %all-to-all-start.3) | async-done | bytes 524320 | tf_op jit(solution)/shard_map/all_to_all | solution.py:423
  116.0 0.8 shard_map.83
  (18 shorter events, 0.1 us)
Async XLA Ops:
  0.6 25.9 %copy-start.6 = (s32[1,32,27]{1,0,2:T(1,128)S(1)}, s32[1,32,27]{1,0,2:T(1,128)}, u32[]{:S(2)}) copy-start(s32[1,32,27]{1,0,2:T(1,128)} %param.8) | copy-start | bytes 10372
  0.6 33.4 %copy-start.3 = (s32[1,32]{1,0:T(1,128)S(1)}, s32[1,32]{1,0:T(1,128)}, u32[]{:S(2)}) copy-start(s32[1,32]{1,0:T(1,128)} %param.9) | copy-start | bytes 388
  4.5 13.0 %all-to-all-start = ((bf16[8,128,128]{2,1,0:T(8,128)(2,1)}), bf16[8,128,128]{2,1,0:T(8,128)(2,1)S(1)}, u32[]{:S(2)}, u32[]{:S(2)}) async-start(bf16[8,128,128]{2,1,0:T(8,128)(2,1)} %shard_map.77), calls=%async_computation | async-start | bytes 524288 | tf_op jit(solution)/shard_map/all_to_all | solution.py:387
  17.5 12.9 %collective-permute-start.3 = (bf16[8,128,128]{2,1,0:T(8,128)(2,1)S(1)}, bf16[8,128,128]{2,1,0:T(8,128)(2,1)S(1)}, u32[]{:S(2)}, u32[]{:S(2)}) collective-permute-start(bf16[8,128,128]{2,1,0:T(8,128)(2,1)S(1)} %all-to-all-done.kv0), channel_id=1, source_target_pairs={{0,64},{64,0},{128,192},{192,128},{1,65},{65,1},{129,193},{193,129... | collective-permute-start | bytes 786440 | tf_op jit(solution)/shard_map/ppermute | solution.py:379
  18.0 15.2 %collective-permute-start.4 = (bf16[8,128,128]{2,1,0:T(8,128)(2,1)S(1)}, bf16[8,128,128]{2,1,0:T(8,128)(2,1)S(1)}, u32[]{:S(2)}, u32[]{:S(2)}) collective-permute-start(bf16[8,128,128]{2,1,0:T(8,128)(2,1)S(1)} %all-to-all-done.kv0), channel_id=1, source_target_pairs={{0,128},{64,192},{128,0},{192,64},{1,129},{65,193},{129,1},{193,65... | collective-permute-start | bytes 786440 | tf_op jit(solution)/shard_map/ppermute | solution.py:379
  20.6 13.4 %collective-permute-start.5 = (bf16[8,128,128]{2,1,0:T(8,128)(2,1)S(1)}, bf16[8,128,128]{2,1,0:T(8,128)(2,1)S(1)}, u32[]{:S(2)}, u32[]{:S(2)}) collective-permute-start(bf16[8,128,128]{2,1,0:T(8,128)(2,1)S(1)} %all-to-all-done.kv0), channel_id=1, source_target_pairs={{0,192},{64,128},{128,64},{192,0},{1,193},{65,129},{129,65},{193,1... | collective-permute-start | bytes 786440 | tf_op jit(solution)/shard_map/ppermute | solution.py:379
  21.3 11.9 %all-to-all-start.1 = ((bf16[8,128,128]{2,1,0:T(8,128)(2,1)}), bf16[8,128,128]{2,1,0:T(8,128)(2,1)S(1)}, u32[]{:S(2)}, u32[]{:S(2)}) async-start(bf16[8,128,128]{2,1,0:T(8,128)(2,1)} %get-tuple-element.29), calls=%async_computation.1 | async-start | bytes 524288 | tf_op jit(solution)/shard_map/all_to_all | solution.py:387
  26.6 28.1 %collective-permute-start = (bf16[2,1024,128]{2,1,0:T(8,128)(2,1)}, bf16[2,1024,128]{2,1,0:T(8,128)(2,1)S(1)}, u32[]{:S(2)}, u32[]{:S(2)}) collective-permute-start(bf16[2,1024,128]{2,1,0:T(8,128)(2,1)} %get-tuple-element.38.refs_0_), channel_id=1, source_target_pairs={{0,16},{8,24},{16,0},{24,8},{32,48},{40,56},{48,32},{56,40},{1,17}... | collective-permute-start | bytes 1572872 | tf_op jit(solution)/shard_map/ppermute | solution.py:379
  28.0 27.6 %collective-permute-start.1 = (bf16[2,1024,128]{2,1,0:T(8,128)(2,1)}, bf16[2,1024,128]{2,1,0:T(8,128)(2,1)S(1)}, u32[]{:S(2)}, u32[]{:S(2)}) collective-permute-start(bf16[2,1024,128]{2,1,0:T(8,128)(2,1)} %get-tuple-element.38.refs_0_), channel_id=1, source_target_pairs={{0,32},{8,40},{16,48},{24,56},{32,0},{40,8},{48,16},{56,24},{1,33}... | collective-permute-start | bytes 1572872 | tf_op jit(solution)/shard_map/ppermute | solution.py:379
  30.4 25.2 %collective-permute-start.2 = (bf16[2,1024,128]{2,1,0:T(8,128)(2,1)}, bf16[2,1024,128]{2,1,0:T(8,128)(2,1)S(1)}, u32[]{:S(2)}, u32[]{:S(2)}) collective-permute-start(bf16[2,1024,128]{2,1,0:T(8,128)(2,1)} %get-tuple-element.38.refs_0_), channel_id=1, source_target_pairs={{0,48},{8,56},{16,32},{24,40},{32,16},{40,24},{48,0},{56,8},{1,49}... | collective-permute-start | bytes 1572872 | tf_op jit(solution)/shard_map/ppermute | solution.py:379
  34.1 23.9 %copy-start.1 = (bf16[2,1024,128]{2,1,0:T(8,128)(2,1)S(1)}, bf16[2,1024,128]{2,1,0:T(8,128)(2,1)}, u32[]{:S(2)}) copy-start(bf16[2,1024,128]{2,1,0:T(8,128)(2,1)} %get-tuple-element.38.refs_0_) | copy-start | bytes 1572868
  53.9 0.8 copy-start.4
  55.6 3.3 %collective-permute-start.10 = (bf16[2,1024,128]{2,1,0:T(8,128)(2,1)S(1)}, bf16[2,1024,128]{2,1,0:T(8,128)(2,1)S(1)}, u32[]{:S(2)}, u32[]{:S(2)}) collective-permute-start(bf16[2,1024,128]{2,1,0:T(8,128)(2,1)S(1)} %collective-permute-done.refs_1_), channel_id=1, source_target_pairs={{0,8},{8,0},{16,24},{24,16},{32,40},{40,32},{48,56},{56,48},{1,9},... | collective-permute-start | bytes 1572872 | tf_op jit(solution)/shard_map/ppermute | solution.py:379
  57.4 5.1 %collective-permute-start.11 = (bf16[2,1024,128]{2,1,0:T(8,128)(2,1)S(1)}, bf16[2,1024,128]{2,1,0:T(8,128)(2,1)S(1)}, u32[]{:S(2)}, u32[]{:S(2)}) collective-permute-start(bf16[2,1024,128]{2,1,0:T(8,128)(2,1)S(1)} %collective-permute-done.1.refs_2_), channel_id=1, source_target_pairs={{0,8},{8,0},{16,24},{24,16},{32,40},{40,32},{48,56},{56,48},{1,9},... | collective-permute-start | bytes 1572872 | tf_op jit(solution)/shard_map/ppermute | solution.py:379
  57.4 9.6 %collective-permute-start.12 = (bf16[2,1024,128]{2,1,0:T(8,128)(2,1)S(1)}, bf16[2,1024,128]{2,1,0:T(8,128)(2,1)}, u32[]{:S(2)}, u32[]{:S(2)}) collective-permute-start(bf16[2,1024,128]{2,1,0:T(8,128)(2,1)S(1)} %collective-permute-done.2.refs_3_), channel_id=1, source_target_pairs={{0,8},{8,0},{16,24},{24,16},{32,40},{40,32},{48,56},{56,48},{1,9},... | collective-permute-start | bytes 1572872 | tf_op jit(solution)/shard_map/ppermute | solution.py:379
  57.9 9.1 %collective-permute-start.9 = (bf16[2,1024,128]{2,1,0:T(8,128)(2,1)S(1)}, bf16[2,1024,128]{2,1,0:T(8,128)(2,1)}, u32[]{:S(2)}, u32[]{:S(2)}) collective-permute-start(bf16[2,1024,128]{2,1,0:T(8,128)(2,1)S(1)} %copy-done.1), channel_id=1, source_target_pairs={{0,8},{8,0},{16,24},{24,16},{32,40},{40,32},{48,56},{56,48},{1,9},... | collective-permute-start | bytes 1572872 | tf_op jit(solution)/shard_map/ppermute | solution.py:379
  57.9 11.6 %collective-permute-start.6 = (bf16[8,128,128]{2,1,0:T(8,128)(2,1)}, bf16[8,128,128]{2,1,0:T(8,128)(2,1)}, u32[]{:S(2)}, u32[]{:S(2)}) collective-permute-start(bf16[8,128,128]{2,1,0:T(8,128)(2,1)} %get-tuple-element.35), channel_id=1, source_target_pairs={{0,64},{64,0},{128,192},{192,128},{1,65},{65,1},{129,193},{193,129... | collective-permute-start | bytes 786440 | tf_op jit(solution)/shard_map/ppermute | solution.py:379
  59.0 15.5 %collective-permute-start.7 = (bf16[8,128,128]{2,1,0:T(8,128)(2,1)}, bf16[8,128,128]{2,1,0:T(8,128)(2,1)}, u32[]{:S(2)}, u32[]{:S(2)}) collective-permute-start(bf16[8,128,128]{2,1,0:T(8,128)(2,1)} %get-tuple-element.36), channel_id=1, source_target_pairs={{0,128},{64,192},{128,0},{192,64},{1,129},{65,193},{129,1},{193,65... | collective-permute-start | bytes 786440 | tf_op jit(solution)/shard_map/ppermute | solution.py:379
  62.5 14.0 %collective-permute-start.8 = (bf16[8,128,128]{2,1,0:T(8,128)(2,1)}, bf16[8,128,128]{2,1,0:T(8,128)(2,1)}, u32[]{:S(2)}, u32[]{:S(2)}) collective-permute-start(bf16[8,128,128]{2,1,0:T(8,128)(2,1)} %get-tuple-element.37), channel_id=1, source_target_pairs={{0,192},{64,128},{128,64},{192,0},{1,193},{65,129},{129,65},{193,1... | collective-permute-start | bytes 786440 | tf_op jit(solution)/shard_map/ppermute | solution.py:379
  63.0 18.4 %all-to-all-start.2 = ((bf16[8,128,128]{2,1,0:T(8,128)(2,1)}), bf16[8,128,128]{2,1,0:T(8,128)(2,1)S(1)}, u32[]{:S(2)}, u32[]{:S(2)}) async-start(bf16[8,128,128]{2,1,0:T(8,128)(2,1)} %get-tuple-element.32.y_ref), calls=%async_computation.2 | async-start | bytes 524288 | tf_op jit(solution)/shard_map/all_to_all | solution.py:387
  67.0 9.6 %copy-start.5 = (f32[8,128,128]{2,1,0:T(8,128)S(1)}, f32[8,128,128]{2,1,0:T(8,128)}, u32[]{:S(2)}) copy-start(f32[8,128,128]{2,1,0:T(8,128)} %copy-done.4) | copy-start | bytes 1572868
  80.7 0.7 copy-start.2
  81.4 34.6 %all-to-all-start.3 = ((bf16[256,8,128]{2,1,0:T(8,128)(2,1)}), bf16[256,8,128]{2,1,0:T(8,128)(2,1)S(1)}, u32[]{:S(2)}, u32[]{:S(2)}) async-start(bf16[256,8,128]{2,1,0:T(8,128)(2,1)} %get-tuple-element.48), calls=%async_computation.3 | async-start | bytes 1048576 | tf_op jit(solution)/shard_map/all_to_all | solution.py:423
  94.6 3.4 %collective-permute-start.13 = (bf16[4,128,128]{2,1,0:T(8,128)(2,1)}, bf16[4,128,128]{2,1,0:T(8,128)(2,1)S(1)}, u32[]{:S(2)}, u32[]{:S(2)}) collective-permute-start(bf16[4,128,128]{2,1,0:T(8,128)(2,1)} %copy-done.2), channel_id=1, source_target_pairs={{0,8},{8,0},{16,24},{24,16},{32,40},{40,32},{48,56},{56,48},{1,9},... | collective-permute-start | bytes 393224 | tf_op jit(solution)/shard_map/ppermute | solution.py:379
  98.0 7.4 %collective-permute-start.14 = (bf16[2,128,128]{2,1,0:T(8,128)(2,1)S(1)}, bf16[2,128,128]{2,1,0:T(8,128)(2,1)S(1)}, u32[]{:S(2)}, u32[]{:S(2)}) collective-permute-start(bf16[2,128,128]{2,1,0:T(8,128)(2,1)S(1)} %get-tuple-element.44), channel_id=1, source_target_pairs={{0,16},{8,24},{16,0},{24,8},{32,48},{40,56},{48,32},{56,40},{1,17}... | collective-permute-start | bytes 196616 | tf_op jit(solution)/shard_map/ppermute | solution.py:379
  98.1 7.3 %collective-permute-start.15 = (bf16[2,128,128]{2,1,0:T(8,128)(2,1)S(1)}, bf16[2,128,128]{2,1,0:T(8,128)(2,1)S(1)}, u32[]{:S(2)}, u32[]{:S(2)}) collective-permute-start(bf16[2,128,128]{2,1,0:T(8,128)(2,1)S(1)} %get-tuple-element.45), channel_id=1, source_target_pairs={{0,32},{8,40},{16,48},{24,56},{32,0},{40,8},{48,16},{56,24},{1,33}... | collective-permute-start | bytes 196616 | tf_op jit(solution)/shard_map/ppermute | solution.py:379
  100.1 7.9 %collective-permute-start.16 = (bf16[2,128,128]{2,1,0:T(8,128)(2,1)S(1)}, bf16[2,128,128]{2,1,0:T(8,128)(2,1)S(1)}, u32[]{:S(2)}, u32[]{:S(2)}) collective-permute-start(bf16[2,128,128]{2,1,0:T(8,128)(2,1)S(1)} %get-tuple-element.46), channel_id=1, source_target_pairs={{0,48},{8,56},{16,32},{24,40},{32,16},{40,24},{48,0},{56,8},{1,49}... | collective-permute-start | bytes 196616 | tf_op jit(solution)/shard_map/ppermute | solution.py:379
  101.9 2.2 %copy-start = (bf16[4,1024,512]{2,1,0:T(8,128)(2,1)S(1)}, bf16[4,1024,512]{2,1,0:T(8,128)(2,1)}, u32[]{:S(2)}) copy-start(bf16[4,1024,512]{2,1,0:T(8,128)(2,1)} %refs_5_.1) | copy-start | bytes 12582916

commit v6 on v5

--- a/solution.py
+++ b/solution.py
@@ -48,12 +48,10 @@
 
 
 def keys_kernel(tok_ref, w_ref, kv_ref, rows):
-    step, part = pl.program_id(0), pl.program_id(1)
-    size = w_ref.shape[2]
-    cols = pl.ds(pl.multiple_of(part * size, size), size)
-    rows[step, :, cols] = dot(tok_ref[...], w_ref[0]).astype(BF)
-
-    @pl.when((step == 1) & (part == pl.num_programs(1) - 1))
+    step = pl.program_id(0)
+    rows[step] = dot(tok_ref[...], w_ref[0]).astype(BF)
+
+    @pl.when(step == 1)
     def _():
         by_head(rows, kv_ref)
 
@@ -74,15 +72,15 @@
         by_head(rows, qd_ref)
 
 
-def project(kernel, arrays, weights, pick, outs, cuts=1):
+def project(kernel, arrays, weights, pick, outs):
     rows, width = arrays[0].shape
     columns = HEADS * HEAD_DIM
     return pl.pallas_call(
         kernel,
-        grid=(2, cuts),
-        in_specs=[pl.BlockSpec((rows, width), lambda step, part: (0, 0)) for _ in arrays]
-        + [pl.BlockSpec((1, width, columns // cuts), lambda step, part: (pick(step), 0, part))],
-        out_specs=[pl.BlockSpec(out, lambda step, part: (0, 0, 0)) for out in outs],
+        grid=(2,),
+        in_specs=[pl.BlockSpec((rows, width), lambda step: (0, 0)) for _ in arrays]
+        + [pl.BlockSpec((1, width, columns), lambda step: (pick(step), 0, 0))],
+        out_specs=[pl.BlockSpec(out, lambda step: (0, 0, 0)) for out in outs],
         out_shape=[jax.ShapeDtypeStruct(out, BF) for out in outs],
         scratch_shapes=[pltpu.VMEM((2, rows, columns), BF)],
         cost_estimate=pl.CostEstimate(
@@ -95,7 +93,7 @@
 
 def attend_kernel(
     lists_ref, counts_ref, group_ref,
-    qd_ref, kv0, kv1, kv2, kv3,
+    qd_ref, kv0, kv1, kv2_low, kv2_high, kv3,
     y_ref, out0, out1, out2, out3,
     kvs, kvt, acc, s_scr, p_scr, ds_scr, n_scr, w_in, w_back, places, sems,
 ):
@@ -106,16 +104,18 @@
     @pl.when(step == 0)
     def _():
         copies = [
-            pltpu.make_async_copy(ref, kvs.at[pl.ds(8 * part, 8)], sems.at[part])
-            for part, ref in enumerate((kv0, kv1, kv2, kv3))
+            pltpu.make_async_copy(ref, kvs.at[pl.ds(start, ref.shape[0])], sems.at[index])
+            for index, (start, ref) in enumerate(
+                ((0, kv0), (8, kv1), (16, kv2_low), (20, kv2_high), (24, kv3))
+            )
         ]
         for copy in copies:
             copy.start()
         acc[...] = jnp.zeros_like(acc)
-        for part, copy in enumerate(copies):
+        for copy in copies:
             copy.wait()
-            for idx in range(8 * part, 8 * part + 8):
-                kvt[idx] = kvs[idx].T
+        for idx in range(32):
+            kvt[idx] = kvs[idx].T
 
     count = counts_ref[block]
     eights = (count + 1) // 8
@@ -215,7 +215,7 @@
         grid_spec=pltpu.PrefetchScalarGridSpec(
             num_scalar_prefetch=3,
             grid=(8,),
-            in_specs=[each] + hbm(4),
+            in_specs=[each] + hbm(5),
             out_specs=[each] + [piece] * 4,
             scratch_shapes=[
                 pltpu.VMEM((32, 128, 128), BF),
@@ -228,7 +228,7 @@
                 pltpu.VMEM((128, 256), BF),
                 pltpu.VMEM((256, 128), BF),
                 pltpu.SMEM((SLOTS,), jnp.int32),
-                pltpu.SemaphoreType.DMA((4,)),
+                pltpu.SemaphoreType.DMA((5,)),
             ],
         ),
         out_shape=[shape(BF), shape(F32), shape(BF), shape(BF), shape(BF)],
@@ -387,7 +387,7 @@
     swap = lambda array: lax.all_to_all(array, HEAD, 0, 0, tiled=True)
     (kv,) = project(
         keys_kernel, [tokens[0]], weights, lambda step: step + 1,
-        [(HEADS, BLOCK, 128)], 2,
+        [(HEADS, BLOCK, 128)],
     )
     kv = swap(kv)
     qd, xt = project(
@@ -395,7 +395,9 @@
         lambda step: 3 * step, [(HEADS, BLOCK, 128), (2, width, BLOCK)],
     )
     qd, xt, kv = lax.optimization_barrier((qd, xt, kv))
-    kvs = [kv] + [across(kv, ROW, k) for k in (1, 2, 3)]
+    one, three = across(kv, ROW, 1), across(kv, ROW, 3)
+    low, high = across(one[:4], ROW, 3), across(three[4:], ROW, 1)
+    kvs = [kv, one, low, high, three]
     qd = swap(qd)
     xs = [xt] + [across(xt, HEAD, k) for k in (2, 4, 6)]
     y, *parts = attend(neighbour_lists[0], neighbour_counts[0], group, qd, kvs)

time: 117 us -> 121 us (1.034)
  local copies, waits for them, and re-layouts: 3.74 us -> 8.78 us
  waiting for transfers between devices: 26.3 us -> 21.4 us
  starting transfers between devices: 49.1 us -> 52.9 us
    unnamed x15 -> x25, local copies, waits for them, and re-layouts: 3.74 us -> 8.76 us
    ppermute x17 -> x18, waiting for transfers between devices: 13.6 us -> 10.4 us  [across(): lax.ppermute(array, axes, [(i, i ^ flip) for i in range(lax.axis_size(axe...]
    ppermute x17 -> x18, starting transfers between devices: 20.3 us -> 23.1 us  [across(): lax.ppermute(array, axes, [(i, i ^ flip) for i in range(lax.axis_size(axe...]
    all_to_all x3, waiting for transfers between devices: 6.26 us -> 4.53 us  [body(): swap = lambda array: lax.all_to_all(array, HEAD, 0, 0, tiled=True)]
  transfers between devices with their start and end apart: 21 -> 22, of which waited for: 10 -> 7; matrix products, arithmetic and copies ran while one was open for 0% -> 0% of each run, Pallas kernels for 28% -> 27%
where the time goes in v6:
time: 121 us; the launch traced here: 120 us
  starting transfers between devices  52.9 us (44%)
  Pallas kernels  35.9 us (30%)
  waiting for transfers between devices  21.4 us (18%)
  local copies, waits for them, and re-layouts  8.78 us (7%)
    ppermute x18, starting transfers between devices, across(): lax.ppermute(array, axes, [(i, i ^ flip) for i in range(lax.axis_size(axe...  23.1 us
    pallas_call x1, Pallas kernels, attend(): pl.pallas_call(attend_kernel, grid_spec=pltpu.PrefetchScalarGridSpec(num_...  20 us
    all_to_all x3, starting transfers between devices, body(): swap = lambda array: lax.all_to_all(array, HEAD, 0, 0, tiled=True)  15.5 us
    all_to_all x1, starting transfers between devices, body(): terms = lax.all_to_all(terms, SEQ + ('rep',), 0, 0, tiled=True)  14.3 us
    ppermute x18, waiting for transfers between devices, across(): lax.ppermute(array, axes, [(i, i ^ flip) for i in range(lax.axis_size(axe...  10.4 us
    unnamed x25, local copies, waits for them, and re-layouts  8.76 us
    pallas_call x2, Pallas kernels, grads_call(): pl.pallas_call(kernel, in_specs=[pl.BlockSpec(memory_space=pltpu.SMEM)] +...  6.6 us
    all_to_all x1, waiting for transfers between devices, body(): terms = lax.all_to_all(terms, SEQ + ('rep',), 0, 0, tiled=True)  6.52 us
  transfers between devices with their start and end apart: 22, of which 7 were waited for; matrix products, arithmetic and copies ran while one was open for 0% of the time, Pallas kernels for 27%

profile of v6, /device:TPU:1, one launch (start us, length us, event | category | flops | bytes accessed | tf_op | source)
XLA Modules:
  0.0 119.8 jit_solution(3463248623529425020)
XLA Ops:
  0.6 2.8 %shard_map.77 = bf16[8,128,128]{2,1,0:T(8,128)(2,1)} custom-call(bf16[128,1024]{1,0:T(8,128)(2,1)} %bitcast.10, bf16[4,1024,512]{2,1,0:T(8,128)(2,1)} %refs_5_.1), custom_call_target="tpu_custom_call" | custom-call | flops 1000000000 | bytes 4000000 | tf_op jit(solution)/shard_map/pallas_call | solution.py:78
  3.4 6.6 %all-to-all-start = ((bf16[8,128,128]{2,1,0:T(8,128)(2,1)}), bf16[8,128,128]{2,1,0:T(8,128)(2,1)S(1)}, u32[]{:S(2)}, u32[]{:S(2)}) async-start(bf16[8,128,128]{2,1,0:T(8,128)(2,1)} %shard_map.77), calls=%async_computation | async-start | bytes 524288 | tf_op jit(solution)/shard_map/all_to_all | solution.py:387
  10.1 3.0 %shard_map.76 = (bf16[8,128,128]{2,1,0:T(8,128)(2,1)}, bf16[2,1024,128]{2,1,0:T(8,128)(2,1)}) custom-call(bf16[128,1024]{1,0:T(8,128)(2,1)} %bitcast.11, bf16[128,1024]{1,0:T(8,128)(2,1)} %bitcast.12, bf16[4,1024,512]{2,1,0:T(8,128)(2,1)} %refs_5_.1), custom_call_target="tpu_custom_call" | custom-call | flops 1000000000 | bytes 4000000 | tf_op jit(solution)/shard_map/pallas_call | solution.py:78
  13.1 3.5 %all-to-all-done.kv0 = bf16[8,128,128]{2,1,0:T(8,128)(2,1)S(1)} async-done(((bf16[8,128,128]{2,1,0:T(8,128)(2,1)}), bf16[8,128,128]{2,1,0:T(8,128)(2,1)S(1)}, u32[]{:S(2)}, u32[]{:S(2)}) %all-to-all-start) | async-done | bytes 262176 | tf_op jit(solution)/shard_map/all_to_all | solution.py:387
  16.6 0.5 collective-permute-start.3
  17.1 1.9 %collective-permute-start.5 = (bf16[8,128,128]{2,1,0:T(8,128)(2,1)S(1)}, bf16[8,128,128]{2,1,0:T(8,128)(2,1)S(1)}, u32[]{:S(2)}, u32[]{:S(2)}) collective-permute-start(bf16[8,128,128]{2,1,0:T(8,128)(2,1)S(1)} %all-to-all-done.kv0), channel_id=1, source_target_pairs={{0,192},{64,128},{128,64},{192,0},{1,193},{65,129},{129,65},{193,1... | collective-permute-start | bytes 786440 | tf_op jit(solution)/shard_map/ppermute | solution.py:379
  19.0 4.9 %all-to-all-start.1 = ((bf16[8,128,128]{2,1,0:T(8,128)(2,1)}), bf16[8,128,128]{2,1,0:T(8,128)(2,1)S(1)}, u32[]{:S(2)}, u32[]{:S(2)}) async-start(bf16[8,128,128]{2,1,0:T(8,128)(2,1)} %get-tuple-element.29), calls=%async_computation.1 | async-start | bytes 524288 | tf_op jit(solution)/shard_map/all_to_all | solution.py:387
  23.9 0.0 collective-permute-done.3.kv1
  23.9 1.5 %collective-permute-start.4 = (bf16[4,128,128]{2,1,0:T(8,128)(2,1)S(1)}, bf16[4,128,128]{2,1,0:T(8,128)(2,1)S(1)}, u32[]{:S(2)}, u32[]{:S(2)}) collective-permute-start(bf16[4,128,128]{2,1,0:T(8,128)(2,1)S(1)} %slice.8), channel_id=1, source_target_pairs={{0,192},{64,128},{128,64},{192,0},{1,193},{65,129},{129,65},{193,1... | collective-permute-start | bytes 393224 | tf_op jit(solution)/shard_map/ppermute | solution.py:379
  25.5 0.1 collective-permute-start.6
  25.6 0.1 copy.8
  25.7 0.7 collective-permute-start
  26.4 2.4 %collective-permute-start.1 = (bf16[2,1024,128]{2,1,0:T(8,128)(2,1)}, bf16[2,1024,128]{2,1,0:T(8,128)(2,1)S(1)}, u32[]{:S(2)}, u32[]{:S(2)}) collective-permute-start(bf16[2,1024,128]{2,1,0:T(8,128)(2,1)} %get-tuple-element.38.refs_0_), channel_id=1, source_target_pairs={{0,32},{8,40},{16,48},{24,56},{32,0},{40,8},{48,16},{56,24},{1,33}... | collective-permute-start | bytes 1572872 | tf_op jit(solution)/shard_map/ppermute | solution.py:379
  28.8 0.7 collective-permute-start.2
  29.6 1.1 all-to-all-done.1.qd_ref
  30.7 0.7 copy-done.6
  31.3 0.9 copy-done.7
  32.2 0.7 copy-done.8
  32.9 20.0 %attend.1 = (bf16[8,128,128]{2,1,0:T(8,128)(2,1)}, f32[8,128,128]{2,1,0:T(8,128)S(1)}, bf16[8,128,128]{2,1,0:T(8,128)(2,1)}, bf16[8,128,128]{2,1,0:T(8,128)(2,1)}, bf16[8,128,128]{2,1,0:T(8,128)(2,1)S(1)}) custom-call(s32[32,27]{1,0:T(8,128)S(1)} %bitcast.8, s32[32]{0:T(128)S(1)} %bitcast.9, s32[1]{0:T(128)} %bitcast.4.group_ref, ...), custom_call_target="tpu_custom_call" | custom-call | flops 30000001024 | bytes 4000000 | tf_op jit(solution)/shard_map/attend/pallas_call | solution.py:213
  52.9 0.8 copy-done.9
  53.7 2.2 %collective-permute-start.10 = (bf16[2,1024,128]{2,1,0:T(8,128)(2,1)S(1)}, bf16[2,1024,128]{2,1,0:T(8,128)(2,1)S(1)}, u32[]{:S(2)}, u32[]{:S(2)}) collective-permute-start(bf16[2,1024,128]{2,1,0:T(8,128)(2,1)S(1)} %copy-done.1), channel_id=1, source_target_pairs={{0,8},{8,0},{16,24},{24,16},{32,40},{40,32},{48,56},{56,48},{1,9},... | collective-permute-start | bytes 1572872 | tf_op jit(solution)/shard_map/ppermute | solution.py:379
  55.8 0.1 collective-permute-start.11
  55.9 0.4 collective-permute-start.12
  56.3 0.1 collective-permute-start.13
  56.4 1.3 %collective-permute-start.7 = (bf16[8,128,128]{2,1,0:T(8,128)(2,1)}, bf16[8,128,128]{2,1,0:T(8,128)(2,1)}, u32[]{:S(2)}, u32[]{:S(2)}) collective-permute-start(bf16[8,128,128]{2,1,0:T(8,128)(2,1)} %get-tuple-element.35), channel_id=1, source_target_pairs={{0,64},{64,0},{128,192},{192,128},{1,65},{65,1},{129,193},{193,129... | collective-permute-start | bytes 786440 | tf_op jit(solution)/shard_map/ppermute | solution.py:379
  57.8 4.8 %collective-permute-start.8 = (bf16[8,128,128]{2,1,0:T(8,128)(2,1)}, bf16[8,128,128]{2,1,0:T(8,128)(2,1)}, u32[]{:S(2)}, u32[]{:S(2)}) collective-permute-start(bf16[8,128,128]{2,1,0:T(8,128)(2,1)} %get-tuple-element.36), channel_id=1, source_target_pairs={{0,128},{64,192},{128,0},{192,64},{1,129},{65,193},{129,1},{193,65... | collective-permute-start | bytes 786440 | tf_op jit(solution)/shard_map/ppermute | solution.py:379
  62.6 0.8 copy-done.2
  63.4 4.0 %all-to-all-start.2 = ((bf16[8,128,128]{2,1,0:T(8,128)(2,1)}), bf16[8,128,128]{2,1,0:T(8,128)(2,1)S(1)}, u32[]{:S(2)}, u32[]{:S(2)}) async-start(bf16[8,128,128]{2,1,0:T(8,128)(2,1)} %get-tuple-element.32.y_ref), calls=%async_computation.2 | async-start | bytes 524288 | tf_op jit(solution)/shard_map/all_to_all | solution.py:387
  67.4 1.0 copy-done.3
  68.4 2.6 %shard_map.79.first_ref = f32[1024,128]{1,0:T(8,128)S(1)} custom-call(s32[1]{0:T(128)} %bitcast.6.place_ref, bf16[8,128,128]{2,1,0:T(8,128)(2,1)} %get-tuple-element.32.y_ref, bf16[2,1024,128]{2,1,0:T(8,128)(2,1)S(1)} %copy-done.1, bf16[2,1024,128]{2,1,0:T(8,128)(2,1)S(1)} %collective-permute-done.refs_1_, ...), custom_call_target="tpu_custom_call" | custom-call | flops 2000000000 | bytes 4000000 | tf_op jit(solution)/shard_map/pallas_call | solution.py:287
  71.0 2.9 %collective-permute-done.8.part2 = bf16[8,128,128]{2,1,0:T(8,128)(2,1)} collective-permute-done((bf16[8,128,128]{2,1,0:T(8,128)(2,1)}, bf16[8,128,128]{2,1,0:T(8,128)(2,1)}, u32[]{:S(2)}, u32[]{:S(2)}) %collective-permute-start.8) | collective-permute-done | bytes 262176 | tf_op jit(solution)/shard_map/ppermute | solution.py:379
  74.0 3.6 %collective-permute-done.9.part3 = bf16[8,128,128]{2,1,0:T(8,128)(2,1)S(1)} collective-permute-done((bf16[8,128,128]{2,1,0:T(8,128)(2,1)S(1)}, bf16[8,128,128]{2,1,0:T(8,128)(2,1)S(1)}, u32[]{:S(2)}, u32[]{:S(2)}) %collective-permute-start.9) | collective-permute-done | bytes 262176 | tf_op jit(solution)/shard_map/ppermute | solution.py:379
  77.6 0.7 copy-done.4
  78.3 0.9 copy-done.5
  79.2 4.0 %shard_map.80 = (bf16[256,8,128]{2,1,0:T(8,128)(2,1)}, bf16[4,128,128]{2,1,0:T(8,128)(2,1)S(1)}, bf16[4,128,128]{2,1,0:T(8,128)(2,1)S(1)}) custom-call(s32[1]{0:T(128)} %bitcast.6.place_ref, f32[8,128,128]{2,1,0:T(8,128)S(1)} %copy-done.10, bf16[8,128,128]{2,1,0:T(8,128)(2,1)} %collective-permute-done.7.part1, ...), custom_call_target="tpu_custom_call" | custom-call | flops 2000000000 | bytes 4000000 | tf_op jit(solution)/shard_map/pallas_call | solution.py:287
  83.3 14.3 %all-to-all-start.3 = ((bf16[256,8,128]{2,1,0:T(8,128)(2,1)}), bf16[256,8,128]{2,1,0:T(8,128)(2,1)S(1)}, u32[]{:S(2)}, u32[]{:S(2)}) async-start(bf16[256,8,128]{2,1,0:T(8,128)(2,1)} %get-tuple-element.48), calls=%async_computation.3 | async-start | bytes 1048576 | tf_op jit(solution)/shard_map/all_to_all | solution.py:425
  97.6 2.2 %collective-permute-start.14 = (bf16[4,128,128]{2,1,0:T(8,128)(2,1)S(1)}, bf16[4,128,128]{2,1,0:T(8,128)(2,1)S(1)}, u32[]{:S(2)}, u32[]{:S(2)}) collective-permute-start(bf16[4,128,128]{2,1,0:T(8,128)(2,1)S(1)} %get-tuple-element.43), channel_id=1, source_target_pairs={{0,8},{8,0},{16,24},{24,16},{32,40},{40,32},{48,56},{56,48},{1,9},... | collective-permute-start | bytes 393224 | tf_op jit(solution)/shard_map/ppermute | solution.py:379
  99.8 1.0 collective-permute-done.14.got_ref
  100.8 0.1 collective-permute-start.15
  100.9 2.0 %collective-permute-start.16 = (bf16[2,128,128]{2,1,0:T(8,128)(2,1)S(1)}, bf16[2,128,128]{2,1,0:T(8,128)(2,1)S(1)}, u32[]{:S(2)}, u32[]{:S(2)}) collective-permute-start(bf16[2,128,128]{2,1,0:T(8,128)(2,1)S(1)} %get-tuple-element.45), channel_id=1, source_target_pairs={{0,32},{8,40},{16,48},{24,56},{32,0},{40,8},{48,16},{56,24},{1,33}... | collective-permute-start | bytes 196616 | tf_op jit(solution)/shard_map/ppermute | solution.py:379
  102.9 1.9 %collective-permute-start.17 = (bf16[2,128,128]{2,1,0:T(8,128)(2,1)S(1)}, bf16[2,128,128]{2,1,0:T(8,128)(2,1)S(1)}, u32[]{:S(2)}, u32[]{:S(2)}) collective-permute-start(bf16[2,128,128]{2,1,0:T(8,128)(2,1)S(1)} %get-tuple-element.46), channel_id=1, source_target_pairs={{0,48},{8,56},{16,32},{24,40},{32,16},{40,24},{48,0},{56,8},{1,49}... | collective-permute-start | bytes 196616 | tf_op jit(solution)/shard_map/ppermute | solution.py:379
  104.7 2.2 %copy-done = bf16[4,1024,512]{2,1,0:T(8,128)(2,1)S(1)} copy-done((bf16[4,1024,512]{2,1,0:T(8,128)(2,1)S(1)}, bf16[4,1024,512]{2,1,0:T(8,128)(2,1)}, u32[]{:S(2)}) %copy-start) | copy-done | bytes 4194328
  106.9 1.2 %shard_map.78 = (bf16[128,1024]{1,0:T(8,128)(2,1)}, f32[128,1024]{1,0:T(8,128)S(1)}) custom-call(bf16[8,128,128]{2,1,0:T(8,128)(2,1)S(1)} %all-to-all-done.2.y_ref, bf16[4,1024,512]{2,1,0:T(8,128)(2,1)S(1)} %copy-done, bf16[4,1024,512]{2,1,0:T(8,128)(2,1)S(1)} %copy-done), custom_call_target="tpu_custom_call" | custom-call | flops 500000000 | bytes 4000000 | tf_op jit(solution)/shard_map/pallas_call | solution.py:356
  108.1 0.0 collective-permute-done.16.refs_1_
  108.2 2.8 %collective-permute-done.17.refs_2_ = bf16[2,128,128]{2,1,0:T(8,128)(2,1)S(1)} collective-permute-done((bf16[2,128,128]{2,1,0:T(8,128)(2,1)S(1)}, bf16[2,128,128]{2,1,0:T(8,128)(2,1)S(1)}, u32[]{:S(2)}, u32[]{:S(2)}) %collective-permute-start.17) | collective-permute-done | bytes 65568 | tf_op jit(solution)/shard_map/ppermute | solution.py:379
  110.9 1.5 %shard_map.82 = bf16[128,1024]{1,0:T(8,128)(2,1)} custom-call(s32[1]{0:T(128)} %bitcast.6.place_ref, bf16[4,128,128]{2,1,0:T(8,128)(2,1)S(1)} %get-tuple-element.42.keep_ref, bf16[4,128,128]{2,1,0:T(8,128)(2,1)S(1)} %collective-permute-done.14.got_ref, bf16[2,128,128]{2,1,0:T(8,128)(2,1)S(1)} %collective-permute-done.15.refs_0_, ...), custom_call_target="tpu_custom_call" | custom-call | flops 500000000 | bytes 4000000 | tf_op jit(solution)/shard_map/pallas_call | solution.py:356
  112.5 6.5 %all-to-all-done.3.in_ref = bf16[256,8,128]{2,1,0:T(8,128)(2,1)S(1)} async-done(((bf16[256,8,128]{2,1,0:T(8,128)(2,1)}), bf16[256,8,128]{2,1,0:T(8,128)(2,1)S(1)}, u32[]{:S(2)}, u32[]{:S(2)}) %all-to-all-start.3) | async-done | bytes 524320 | tf_op jit(solution)/shard_map/all_to_all | solution.py:425
  119.0 0.8 shard_map.83
  (32 shorter events, 0.1 us)
Async XLA Ops:
  3.4 22.2 %copy-start.11 = (s32[1,32,27]{1,0,2:T(1,128)S(1)}, s32[1,32,27]{1,0,2:T(1,128)}, u32[]{:S(2)}) copy-start(s32[1,32,27]{1,0,2:T(1,128)} %param.8) | copy-start | bytes 10372
  3.4 13.1 %all-to-all-start = ((bf16[8,128,128]{2,1,0:T(8,128)(2,1)}), bf16[8,128,128]{2,1,0:T(8,128)(2,1)S(1)}, u32[]{:S(2)}, u32[]{:S(2)}) async-start(bf16[8,128,128]{2,1,0:T(8,128)(2,1)} %shard_map.77), calls=%async_computation | async-start | bytes 524288 | tf_op jit(solution)/shard_map/all_to_all | solution.py:387
  16.6 7.4 %collective-permute-start.3 = (bf16[8,128,128]{2,1,0:T(8,128)(2,1)S(1)}, bf16[8,128,128]{2,1,0:T(8,128)(2,1)S(1)}, u32[]{:S(2)}, u32[]{:S(2)}) collective-permute-start(bf16[8,128,128]{2,1,0:T(8,128)(2,1)S(1)} %all-to-all-done.kv0), channel_id=1, source_target_pairs={{0,64},{64,0},{128,192},{192,128},{1,65},{65,1},{129,193},{193,129... | collective-permute-start | bytes 786440 | tf_op jit(solution)/shard_map/ppermute | solution.py:379
  17.1 8.4 %collective-permute-start.5 = (bf16[8,128,128]{2,1,0:T(8,128)(2,1)S(1)}, bf16[8,128,128]{2,1,0:T(8,128)(2,1)S(1)}, u32[]{:S(2)}, u32[]{:S(2)}) collective-permute-start(bf16[8,128,128]{2,1,0:T(8,128)(2,1)S(1)} %all-to-all-done.kv0), channel_id=1, source_target_pairs={{0,192},{64,128},{128,64},{192,0},{1,193},{65,129},{129,65},{193,1... | collective-permute-start | bytes 786440 | tf_op jit(solution)/shard_map/ppermute | solution.py:379
  19.0 11.6 %all-to-all-start.1 = ((bf16[8,128,128]{2,1,0:T(8,128)(2,1)}), bf16[8,128,128]{2,1,0:T(8,128)(2,1)S(1)}, u32[]{:S(2)}, u32[]{:S(2)}) async-start(bf16[8,128,128]{2,1,0:T(8,128)(2,1)} %get-tuple-element.29), calls=%async_computation.1 | async-start | bytes 524288 | tf_op jit(solution)/shard_map/all_to_all | solution.py:387
  23.9 6.7 %collective-permute-start.4 = (bf16[4,128,128]{2,1,0:T(8,128)(2,1)S(1)}, bf16[4,128,128]{2,1,0:T(8,128)(2,1)S(1)}, u32[]{:S(2)}, u32[]{:S(2)}) collective-permute-start(bf16[4,128,128]{2,1,0:T(8,128)(2,1)S(1)} %slice.8), channel_id=1, source_target_pairs={{0,192},{64,128},{128,64},{192,0},{1,193},{65,129},{129,65},{193,1... | collective-permute-start | bytes 393224 | tf_op jit(solution)/shard_map/ppermute | solution.py:379
  25.5 5.2 %collective-permute-start.6 = (bf16[4,128,128]{2,1,0:T(8,128)(2,1)S(1)}, bf16[4,128,128]{2,1,0:T(8,128)(2,1)S(1)}, u32[]{:S(2)}, u32[]{:S(2)}) collective-permute-start(bf16[4,128,128]{2,1,0:T(8,128)(2,1)S(1)} %slice.9), channel_id=1, source_target_pairs={{0,64},{64,0},{128,192},{192,128},{1,65},{65,1},{129,193},{193,129... | collective-permute-start | bytes 393224 | tf_op jit(solution)/shard_map/ppermute | solution.py:379
  25.7 28.0 %collective-permute-start = (bf16[2,1024,128]{2,1,0:T(8,128)(2,1)}, bf16[2,1024,128]{2,1,0:T(8,128)(2,1)S(1)}, u32[]{:S(2)}, u32[]{:S(2)}) collective-permute-start(bf16[2,1024,128]{2,1,0:T(8,128)(2,1)} %get-tuple-element.38.refs_0_), channel_id=1, source_target_pairs={{0,16},{8,24},{16,0},{24,8},{32,48},{40,56},{48,32},{56,40},{1,17}... | collective-permute-start | bytes 1572872 | tf_op jit(solution)/shard_map/ppermute | solution.py:379
  26.4 27.2 %collective-permute-start.1 = (bf16[2,1024,128]{2,1,0:T(8,128)(2,1)}, bf16[2,1024,128]{2,1,0:T(8,128)(2,1)S(1)}, u32[]{:S(2)}, u32[]{:S(2)}) collective-permute-start(bf16[2,1024,128]{2,1,0:T(8,128)(2,1)} %get-tuple-element.38.refs_0_), channel_id=1, source_target_pairs={{0,32},{8,40},{16,48},{24,56},{32,0},{40,8},{48,16},{56,24},{1,33}... | collective-permute-start | bytes 1572872 | tf_op jit(solution)/shard_map/ppermute | solution.py:379
  28.8 24.8 %collective-permute-start.2 = (bf16[2,1024,128]{2,1,0:T(8,128)(2,1)}, bf16[2,1024,128]{2,1,0:T(8,128)(2,1)S(1)}, u32[]{:S(2)}, u32[]{:S(2)}) collective-permute-start(bf16[2,1024,128]{2,1,0:T(8,128)(2,1)} %get-tuple-element.38.refs_0_), channel_id=1, source_target_pairs={{0,48},{8,56},{16,32},{24,40},{32,16},{40,24},{48,0},{56,8},{1,49}... | collective-permute-start | bytes 1572872 | tf_op jit(solution)/shard_map/ppermute | solution.py:379
  30.6 0.7 copy-start.6
  31.3 0.9 copy-start.7
  32.2 0.7 copy-start.8
  32.9 20.8 %copy-start.1 = (bf16[2,1024,128]{2,1,0:T(8,128)(2,1)S(1)}, bf16[2,1024,128]{2,1,0:T(8,128)(2,1)}, u32[]{:S(2)}) copy-start(bf16[2,1024,128]{2,1,0:T(8,128)(2,1)} %get-tuple-element.38.refs_0_) | copy-start | bytes 1572868
  52.9 0.8 copy-start.9
  53.7 4.1 %collective-permute-start.10 = (bf16[2,1024,128]{2,1,0:T(8,128)(2,1)S(1)}, bf16[2,1024,128]{2,1,0:T(8,128)(2,1)S(1)}, u32[]{:S(2)}, u32[]{:S(2)}) collective-permute-start(bf16[2,1024,128]{2,1,0:T(8,128)(2,1)S(1)} %copy-done.1), channel_id=1, source_target_pairs={{0,8},{8,0},{16,24},{24,16},{32,40},{40,32},{48,56},{56,48},{1,9},... | collective-permute-start | bytes 1572872 | tf_op jit(solution)/shard_map/ppermute | solution.py:379
  55.8 6.8 %collective-permute-start.11 = (bf16[2,1024,128]{2,1,0:T(8,128)(2,1)S(1)}, bf16[2,1024,128]{2,1,0:T(8,128)(2,1)S(1)}, u32[]{:S(2)}, u32[]{:S(2)}) collective-permute-start(bf16[2,1024,128]{2,1,0:T(8,128)(2,1)S(1)} %collective-permute-done.refs_1_), channel_id=1, source_target_pairs={{0,8},{8,0},{16,24},{24,16},{32,40},{40,32},{48,56},{56,48},{1,9},... | collective-permute-start | bytes 1572872 | tf_op jit(solution)/shard_map/ppermute | solution.py:379
  55.9 11.5 %collective-permute-start.12 = (bf16[2,1024,128]{2,1,0:T(8,128)(2,1)S(1)}, bf16[2,1024,128]{2,1,0:T(8,128)(2,1)}, u32[]{:S(2)}, u32[]{:S(2)}) collective-permute-start(bf16[2,1024,128]{2,1,0:T(8,128)(2,1)S(1)} %collective-permute-done.1.refs_2_), channel_id=1, source_target_pairs={{0,8},{8,0},{16,24},{24,16},{32,40},{40,32},{48,56},{56,48},{1,9},... | collective-permute-start | bytes 1572872 | tf_op jit(solution)/shard_map/ppermute | solution.py:379
  56.3 11.1 %collective-permute-start.13 = (bf16[2,1024,128]{2,1,0:T(8,128)(2,1)S(1)}, bf16[2,1024,128]{2,1,0:T(8,128)(2,1)}, u32[]{:S(2)}, u32[]{:S(2)}) collective-permute-start(bf16[2,1024,128]{2,1,0:T(8,128)(2,1)S(1)} %collective-permute-done.2.refs_3_), channel_id=1, source_target_pairs={{0,8},{8,0},{16,24},{24,16},{32,40},{40,32},{48,56},{56,48},{1,9},... | collective-permute-start | bytes 1572872 | tf_op jit(solution)/shard_map/ppermute | solution.py:379
  56.4 14.6 %collective-permute-start.7 = (bf16[8,128,128]{2,1,0:T(8,128)(2,1)}, bf16[8,128,128]{2,1,0:T(8,128)(2,1)}, u32[]{:S(2)}, u32[]{:S(2)}) collective-permute-start(bf16[8,128,128]{2,1,0:T(8,128)(2,1)} %get-tuple-element.35), channel_id=1, source_target_pairs={{0,64},{64,0},{128,192},{192,128},{1,65},{65,1},{129,193},{193,129... | collective-permute-start | bytes 786440 | tf_op jit(solution)/shard_map/ppermute | solution.py:379
  57.8 16.2 %collective-permute-start.8 = (bf16[8,128,128]{2,1,0:T(8,128)(2,1)}, bf16[8,128,128]{2,1,0:T(8,128)(2,1)}, u32[]{:S(2)}, u32[]{:S(2)}) collective-permute-start(bf16[8,128,128]{2,1,0:T(8,128)(2,1)} %get-tuple-element.36), channel_id=1, source_target_pairs={{0,128},{64,192},{128,0},{192,64},{1,129},{65,193},{129,1},{193,65... | collective-permute-start | bytes 786440 | tf_op jit(solution)/shard_map/ppermute | solution.py:379
  62.6 0.8 copy-start.2
  63.4 14.2 %collective-permute-start.9 = (bf16[8,128,128]{2,1,0:T(8,128)(2,1)S(1)}, bf16[8,128,128]{2,1,0:T(8,128)(2,1)S(1)}, u32[]{:S(2)}, u32[]{:S(2)}) collective-permute-start(bf16[8,128,128]{2,1,0:T(8,128)(2,1)S(1)} %get-tuple-element.37), channel_id=1, source_target_pairs={{0,192},{64,128},{128,64},{192,0},{1,193},{65,129},{129,65},{193,1... | collective-permute-start | bytes 786440 | tf_op jit(solution)/shard_map/ppermute | solution.py:379
  63.4 19.9 %all-to-all-start.2 = ((bf16[8,128,128]{2,1,0:T(8,128)(2,1)}), bf16[8,128,128]{2,1,0:T(8,128)(2,1)S(1)}, u32[]{:S(2)}, u32[]{:S(2)}) async-start(bf16[8,128,128]{2,1,0:T(8,128)(2,1)} %get-tuple-element.32.y_ref), calls=%async_computation.2 | async-start | bytes 524288 | tf_op jit(solution)/shard_map/all_to_all | solution.py:387
  67.4 1.0 copy-start.3
  68.4 9.9 %copy-start.10 = (f32[8,128,128]{2,1,0:T(8,128)S(1)}, f32[8,128,128]{2,1,0:T(8,128)}, u32[]{:S(2)}) copy-start(f32[8,128,128]{2,1,0:T(8,128)} %copy-done.9) | copy-start | bytes 1572868
  77.6 0.7 copy-start.4
  78.3 1.0 copy-start.5
  83.3 35.7 %all-to-all-start.3 = ((bf16[256,8,128]{2,1,0:T(8,128)(2,1)}), bf16[256,8,128]{2,1,0:T(8,128)(2,1)S(1)}, u32[]{:S(2)}, u32[]{:S(2)}) async-start(bf16[256,8,128]{2,1,0:T(8,128)(2,1)} %get-tuple-element.48), calls=%async_computation.3 | async-start | bytes 1048576 | tf_op jit(solution)/shard_map/all_to_all | solution.py:425
  97.6 3.2 %collective-permute-start.14 = (bf16[4,128,128]{2,1,0:T(8,128)(2,1)S(1)}, bf16[4,128,128]{2,1,0:T(8,128)(2,1)S(1)}, u32[]{:S(2)}, u32[]{:S(2)}) collective-permute-start(bf16[4,128,128]{2,1,0:T(8,128)(2,1)S(1)} %get-tuple-element.43), channel_id=1, source_target_pairs={{0,8},{8,0},{16,24},{24,16},{32,40},{40,32},{48,56},{56,48},{1,9},... | collective-permute-start | bytes 393224 | tf_op jit(solution)/shard_map/ppermute | solution.py:379
  100.8 7.3 %collective-permute-start.15 = (bf16[2,128,128]{2,1,0:T(8,128)(2,1)S(1)}, bf16[2,128,128]{2,1,0:T(8,128)(2,1)S(1)}, u32[]{:S(2)}, u32[]{:S(2)}) collective-permute-start(bf16[2,128,128]{2,1,0:T(8,128)(2,1)S(1)} %get-tuple-element.44), channel_id=1, source_target_pairs={{0,16},{8,24},{16,0},{24,8},{32,48},{40,56},{48,32},{56,40},{1,17}... | collective-permute-start | bytes 196616 | tf_op jit(solution)/shard_map/ppermute | solution.py:379
  100.9 7.3 %collective-permute-start.16 = (bf16[2,128,128]{2,1,0:T(8,128)(2,1)S(1)}, bf16[2,128,128]{2,1,0:T(8,128)(2,1)S(1)}, u32[]{:S(2)}, u32[]{:S(2)}) collective-permute-start(bf16[2,128,128]{2,1,0:T(8,128)(2,1)S(1)} %get-tuple-element.45), channel_id=1, source_target_pairs={{0,32},{8,40},{16,48},{24,56},{32,0},{40,8},{48,16},{56,24},{1,33}... | collective-permute-start | bytes 196616 | tf_op jit(solution)/shard_map/ppermute | solution.py:379
  102.9 8.1 %collective-permute-start.17 = (bf16[2,128,128]{2,1,0:T(8,128)(2,1)S(1)}, bf16[2,128,128]{2,1,0:T(8,128)(2,1)S(1)}, u32[]{:S(2)}, u32[]{:S(2)}) collective-permute-start(bf16[2,128,128]{2,1,0:T(8,128)(2,1)S(1)} %get-tuple-element.46), channel_id=1, source_target_pairs={{0,48},{8,56},{16,32},{24,40},{32,16},{40,24},{48,0},{56,8},{1,49}... | collective-permute-start | bytes 196616 | tf_op jit(solution)/shard_map/ppermute | solution.py:379
  104.7 2.2 %copy-start = (bf16[4,1024,512]{2,1,0:T(8,128)(2,1)S(1)}, bf16[4,1024,512]{2,1,0:T(8,128)(2,1)}, u32[]{:S(2)}) copy-start(bf16[4,1024,512]{2,1,0:T(8,128)(2,1)} %refs_5_.1) | copy-start | bytes 12582916

commit v7 on v5

--- a/solution.py
+++ b/solution.py
@@ -48,12 +48,10 @@
 
 
 def keys_kernel(tok_ref, w_ref, kv_ref, rows):
-    step, part = pl.program_id(0), pl.program_id(1)
-    size = w_ref.shape[2]
-    cols = pl.ds(pl.multiple_of(part * size, size), size)
-    rows[step, :, cols] = dot(tok_ref[...], w_ref[0]).astype(BF)
-
-    @pl.when((step == 1) & (part == pl.num_programs(1) - 1))
+    step = pl.program_id(0)
+    rows[step] = dot(tok_ref[...], w_ref[0]).astype(BF)
+
+    @pl.when(step == 1)
     def _():
         by_head(rows, kv_ref)
 
@@ -74,15 +72,15 @@
         by_head(rows, qd_ref)
 
 
-def project(kernel, arrays, weights, pick, outs, cuts=1):
+def project(kernel, arrays, weights, pick, outs):
     rows, width = arrays[0].shape
     columns = HEADS * HEAD_DIM
     return pl.pallas_call(
         kernel,
-        grid=(2, cuts),
-        in_specs=[pl.BlockSpec((rows, width), lambda step, part: (0, 0)) for _ in arrays]
-        + [pl.BlockSpec((1, width, columns // cuts), lambda step, part: (pick(step), 0, part))],
-        out_specs=[pl.BlockSpec(out, lambda step, part: (0, 0, 0)) for out in outs],
+        grid=(2,),
+        in_specs=[pl.BlockSpec((rows, width), lambda step: (0, 0)) for _ in arrays]
+        + [pl.BlockSpec((1, width, columns), lambda step: (pick(step), 0, 0))],
+        out_specs=[pl.BlockSpec(out, lambda step: (0, 0, 0)) for out in outs],
         out_shape=[jax.ShapeDtypeStruct(out, BF) for out in outs],
         scratch_shapes=[pltpu.VMEM((2, rows, columns), BF)],
         cost_estimate=pl.CostEstimate(
@@ -387,7 +385,7 @@
     swap = lambda array: lax.all_to_all(array, HEAD, 0, 0, tiled=True)
     (kv,) = project(
         keys_kernel, [tokens[0]], weights, lambda step: step + 1,
-        [(HEADS, BLOCK, 128)], 2,
+        [(HEADS, BLOCK, 128)],
     )
     kv = swap(kv)
     qd, xt = project(

time: 117 us -> 116 us (level)
  no operation moved by 1% of the time
where the time goes in v7:
time: 116 us
  starting transfers between devices  49.1 us (42%)
  Pallas kernels  35.9 us (31%)
  waiting for transfers between devices  26.3 us (23%)
  local copies, waits for them, and re-layouts  3.74 us (3%)
    ppermute x17, starting transfers between devices, across(): lax.ppermute(array, axes, [(i, i ^ flip) for i in range(lax.axis_size(axe...  20.3 us
    pallas_call x1, Pallas kernels, attend(): pl.pallas_call(attend_kernel, grid_spec=pltpu.PrefetchScalarGridSpec(num_...  19.9 us
    all_to_all x3, starting transfers between devices, body(): swap = lambda array: lax.all_to_all(array, HEAD, 0, 0, tiled=True)  15.7 us
    ppermute x17, waiting for transfers between devices, across(): lax.ppermute(array, axes, [(i, i ^ flip) for i in range(lax.axis_size(axe...  13.6 us
    all_to_all x1, starting transfers between devices, body(): terms = lax.all_to_all(terms, SEQ + ('rep',), 0, 0, tiled=True)  13.2 us
    pallas_call x2, Pallas kernels, grads_call(): pl.pallas_call(kernel, in_specs=[pl.BlockSpec(memory_space=pltpu.SMEM)] +...  6.7 us
    all_to_all x1, waiting for transfers between devices, body(): terms = lax.all_to_all(terms, SEQ + ('rep',), 0, 0, tiled=True)  6.43 us
    all_to_all x3, waiting for transfers between devices, body(): swap = lambda array: lax.all_to_all(array, HEAD, 0, 0, tiled=True)  6.26 us
  transfers between devices with their start and end apart: 21, of which 10 were waited for; matrix products, arithmetic and copies ran while one was open for 0% of the time, Pallas kernels for 28%

profile of v7, /device:TPU:1, one launch (start us, length us, event | category | flops | bytes accessed | tf_op | source)
XLA Modules:
  0.0 115.7 jit_solution(7379706117557245391)
XLA Ops:
  0.7 2.8 %shard_map.77 = bf16[8,128,128]{2,1,0:T(8,128)(2,1)} custom-call(bf16[128,1024]{1,0:T(8,128)(2,1)} %bitcast.10, bf16[4,1024,512]{2,1,0:T(8,128)(2,1)} %refs_5_.1), custom_call_target="tpu_custom_call" | custom-call | flops 1000000000 | bytes 4000000 | tf_op jit(solution)/shard_map/pallas_call | solution.py:78
  3.4 6.5 %all-to-all-start = ((bf16[8,128,128]{2,1,0:T(8,128)(2,1)}), bf16[8,128,128]{2,1,0:T(8,128)(2,1)S(1)}, u32[]{:S(2)}, u32[]{:S(2)}) async-start(bf16[8,128,128]{2,1,0:T(8,128)(2,1)} %shard_map.77), calls=%async_computation | async-start | bytes 524288 | tf_op jit(solution)/shard_map/all_to_all | solution.py:385
  10.0 3.0 %shard_map.76 = (bf16[8,128,128]{2,1,0:T(8,128)(2,1)}, bf16[2,1024,128]{2,1,0:T(8,128)(2,1)}) custom-call(bf16[128,1024]{1,0:T(8,128)(2,1)} %bitcast.11, bf16[128,1024]{1,0:T(8,128)(2,1)} %bitcast.12, bf16[4,1024,512]{2,1,0:T(8,128)(2,1)} %refs_5_.1), custom_call_target="tpu_custom_call" | custom-call | flops 1000000000 | bytes 4000000 | tf_op jit(solution)/shard_map/pallas_call | solution.py:78
  12.9 3.5 %all-to-all-done.kv0 = bf16[8,128,128]{2,1,0:T(8,128)(2,1)S(1)} async-done(((bf16[8,128,128]{2,1,0:T(8,128)(2,1)}), bf16[8,128,128]{2,1,0:T(8,128)(2,1)S(1)}, u32[]{:S(2)}, u32[]{:S(2)}) %all-to-all-start) | async-done | bytes 262176 | tf_op jit(solution)/shard_map/all_to_all | solution.py:385
  16.5 0.5 collective-permute-start.3
  17.0 2.6 %collective-permute-start.4 = (bf16[8,128,128]{2,1,0:T(8,128)(2,1)S(1)}, bf16[8,128,128]{2,1,0:T(8,128)(2,1)S(1)}, u32[]{:S(2)}, u32[]{:S(2)}) collective-permute-start(bf16[8,128,128]{2,1,0:T(8,128)(2,1)S(1)} %all-to-all-done.kv0), channel_id=1, source_target_pairs={{0,128},{64,192},{128,0},{192,64},{1,129},{65,193},{129,1},{193,65... | collective-permute-start | bytes 786440 | tf_op jit(solution)/shard_map/ppermute | solution.py:377
  19.6 0.7 collective-permute-start.5
  20.3 5.2 %all-to-all-start.1 = ((bf16[8,128,128]{2,1,0:T(8,128)(2,1)}), bf16[8,128,128]{2,1,0:T(8,128)(2,1)S(1)}, u32[]{:S(2)}, u32[]{:S(2)}) async-start(bf16[8,128,128]{2,1,0:T(8,128)(2,1)} %get-tuple-element.29), calls=%async_computation.1 | async-start | bytes 524288 | tf_op jit(solution)/shard_map/all_to_all | solution.py:385
  25.5 0.1 copy.8
  25.6 1.4 %collective-permute-start = (bf16[2,1024,128]{2,1,0:T(8,128)(2,1)}, bf16[2,1024,128]{2,1,0:T(8,128)(2,1)S(1)}, u32[]{:S(2)}, u32[]{:S(2)}) collective-permute-start(bf16[2,1024,128]{2,1,0:T(8,128)(2,1)} %get-tuple-element.38.refs_0_), channel_id=1, source_target_pairs={{0,16},{8,24},{16,0},{24,8},{32,48},{40,56},{48,32},{56,40},{1,17}... | collective-permute-start | bytes 1572872 | tf_op jit(solution)/shard_map/ppermute | solution.py:377
  27.0 2.4 %collective-permute-start.1 = (bf16[2,1024,128]{2,1,0:T(8,128)(2,1)}, bf16[2,1024,128]{2,1,0:T(8,128)(2,1)S(1)}, u32[]{:S(2)}, u32[]{:S(2)}) collective-permute-start(bf16[2,1024,128]{2,1,0:T(8,128)(2,1)} %get-tuple-element.38.refs_0_), channel_id=1, source_target_pairs={{0,32},{8,40},{16,48},{24,56},{32,0},{40,8},{48,16},{56,24},{1,33}... | collective-permute-start | bytes 1572872 | tf_op jit(solution)/shard_map/ppermute | solution.py:377
  29.4 0.1 collective-permute-start.2
  29.5 2.7 %all-to-all-done.1.qd_ref = bf16[8,128,128]{2,1,0:T(8,128)(2,1)S(1)} async-done(((bf16[8,128,128]{2,1,0:T(8,128)(2,1)}), bf16[8,128,128]{2,1,0:T(8,128)(2,1)S(1)}, u32[]{:S(2)}, u32[]{:S(2)}) %all-to-all-start.1) | async-done | bytes 262176 | tf_op jit(solution)/shard_map/all_to_all | solution.py:385
  32.2 0.0 collective-permute-done.4.kv2
  32.2 0.8 collective-permute-done.5.kv3
  33.0 19.9 %attend.1 = (bf16[8,128,128]{2,1,0:T(8,128)(2,1)}, f32[8,128,128]{2,1,0:T(8,128)S(1)}, bf16[8,128,128]{2,1,0:T(8,128)(2,1)}, bf16[8,128,128]{2,1,0:T(8,128)(2,1)}, bf16[8,128,128]{2,1,0:T(8,128)(2,1)}) custom-call(s32[32,27]{1,0:T(8,128)S(1)} %bitcast.8, s32[32]{0:T(128)S(1)} %bitcast.9, s32[1]{0:T(128)} %bitcast.4.group_ref, ...), custom_call_target="tpu_custom_call" | custom-call | flops 30000001024 | bytes 4000000 | tf_op jit(solution)/shard_map/attend/pallas_call | solution.py:211
  52.9 0.8 copy-done.4
  53.7 0.9 collective-permute-done.1.refs_2_
  54.6 0.0 collective-permute-done.2.refs_3_
  54.6 1.8 %collective-permute-start.10 = (bf16[2,1024,128]{2,1,0:T(8,128)(2,1)S(1)}, bf16[2,1024,128]{2,1,0:T(8,128)(2,1)S(1)}, u32[]{:S(2)}, u32[]{:S(2)}) collective-permute-start(bf16[2,1024,128]{2,1,0:T(8,128)(2,1)S(1)} %collective-permute-done.refs_1_), channel_id=1, source_target_pairs={{0,8},{8,0},{16,24},{24,16},{32,40},{40,32},{48,56},{56,48},{1,9},... | collective-permute-start | bytes 1572872 | tf_op jit(solution)/shard_map/ppermute | solution.py:377
  56.4 0.0 collective-permute-start.11
  56.4 0.5 collective-permute-start.12
  56.9 0.0 collective-permute-start.9
  56.9 0.0 collective-permute-start.6
  56.9 1.0 collective-permute-done.10.refs_5_
  57.9 3.6 %collective-permute-start.7 = (bf16[8,128,128]{2,1,0:T(8,128)(2,1)}, bf16[8,128,128]{2,1,0:T(8,128)(2,1)}, u32[]{:S(2)}, u32[]{:S(2)}) collective-permute-start(bf16[8,128,128]{2,1,0:T(8,128)(2,1)} %get-tuple-element.36), channel_id=1, source_target_pairs={{0,128},{64,192},{128,0},{192,64},{1,129},{65,193},{129,1},{193,65... | collective-permute-start | bytes 786440 | tf_op jit(solution)/shard_map/ppermute | solution.py:377
  61.5 0.0 collective-permute-done.11.refs_6_
  61.5 0.5 collective-permute-start.8
  62.0 4.0 %all-to-all-start.2 = ((bf16[8,128,128]{2,1,0:T(8,128)(2,1)}), bf16[8,128,128]{2,1,0:T(8,128)(2,1)S(1)}, u32[]{:S(2)}, u32[]{:S(2)}) async-start(bf16[8,128,128]{2,1,0:T(8,128)(2,1)} %get-tuple-element.32.y_ref), calls=%async_computation.2 | async-start | bytes 524288 | tf_op jit(solution)/shard_map/all_to_all | solution.py:385
  66.0 2.6 %shard_map.79.first_ref = f32[1024,128]{1,0:T(8,128)S(1)} custom-call(s32[1]{0:T(128)} %bitcast.6.place_ref, bf16[8,128,128]{2,1,0:T(8,128)(2,1)} %get-tuple-element.32.y_ref, bf16[2,1024,128]{2,1,0:T(8,128)(2,1)S(1)} %copy-done.1, bf16[2,1024,128]{2,1,0:T(8,128)(2,1)S(1)} %collective-permute-done.refs_1_, ...), custom_call_target="tpu_custom_call" | custom-call | flops 2000000000 | bytes 4000000 | tf_op jit(solution)/shard_map/pallas_call | solution.py:285
  68.6 4.9 %collective-permute-done.7.part2 = bf16[8,128,128]{2,1,0:T(8,128)(2,1)} collective-permute-done((bf16[8,128,128]{2,1,0:T(8,128)(2,1)}, bf16[8,128,128]{2,1,0:T(8,128)(2,1)}, u32[]{:S(2)}, u32[]{:S(2)}) %collective-permute-start.7) | collective-permute-done | bytes 262176 | tf_op jit(solution)/shard_map/ppermute | solution.py:377
  73.5 2.1 %collective-permute-done.8.part3 = bf16[8,128,128]{2,1,0:T(8,128)(2,1)} collective-permute-done((bf16[8,128,128]{2,1,0:T(8,128)(2,1)}, bf16[8,128,128]{2,1,0:T(8,128)(2,1)}, u32[]{:S(2)}, u32[]{:S(2)}) %collective-permute-start.8) | collective-permute-done | bytes 262176 | tf_op jit(solution)/shard_map/ppermute | solution.py:377
  75.5 4.1 %shard_map.80 = (bf16[256,8,128]{2,1,0:T(8,128)(2,1)}, bf16[4,128,128]{2,1,0:T(8,128)(2,1)S(1)}, bf16[4,128,128]{2,1,0:T(8,128)(2,1)S(1)}) custom-call(s32[1]{0:T(128)} %bitcast.6.place_ref, f32[8,128,128]{2,1,0:T(8,128)S(1)} %copy-done.5, bf16[8,128,128]{2,1,0:T(8,128)(2,1)} %collective-permute-done.6.part1, ...), custom_call_target="tpu_custom_call" | custom-call | flops 2000000000 | bytes 4000000 | tf_op jit(solution)/shard_map/pallas_call | solution.py:285
  79.7 0.0 copy-start.2
  79.7 0.6 copy-done.2
  80.3 13.2 %all-to-all-start.3 = ((bf16[256,8,128]{2,1,0:T(8,128)(2,1)}), bf16[256,8,128]{2,1,0:T(8,128)(2,1)S(1)}, u32[]{:S(2)}, u32[]{:S(2)}) async-start(bf16[256,8,128]{2,1,0:T(8,128)(2,1)} %get-tuple-element.48), calls=%async_computation.3 | async-start | bytes 1048576 | tf_op jit(solution)/shard_map/all_to_all | solution.py:421
  93.5 2.2 %collective-permute-start.13 = (bf16[4,128,128]{2,1,0:T(8,128)(2,1)}, bf16[4,128,128]{2,1,0:T(8,128)(2,1)S(1)}, u32[]{:S(2)}, u32[]{:S(2)}) collective-permute-start(bf16[4,128,128]{2,1,0:T(8,128)(2,1)} %copy-done.2), channel_id=1, source_target_pairs={{0,8},{8,0},{16,24},{24,16},{32,40},{40,32},{48,56},{56,48},{1,9},... | collective-permute-start | bytes 393224 | tf_op jit(solution)/shard_map/ppermute | solution.py:377
  95.8 1.2 %collective-permute-done.13.got_ref = bf16[4,128,128]{2,1,0:T(8,128)(2,1)S(1)} collective-permute-done((bf16[4,128,128]{2,1,0:T(8,128)(2,1)}, bf16[4,128,128]{2,1,0:T(8,128)(2,1)S(1)}, u32[]{:S(2)}, u32[]{:S(2)}) %collective-permute-start.13) | collective-permute-done | bytes 131104 | tf_op jit(solution)/shard_map/ppermute | solution.py:377
  97.0 0.1 collective-permute-start.14
  97.1 2.0 %collective-permute-start.15 = (bf16[2,128,128]{2,1,0:T(8,128)(2,1)S(1)}, bf16[2,128,128]{2,1,0:T(8,128)(2,1)S(1)}, u32[]{:S(2)}, u32[]{:S(2)}) collective-permute-start(bf16[2,128,128]{2,1,0:T(8,128)(2,1)S(1)} %get-tuple-element.45), channel_id=1, source_target_pairs={{0,32},{8,40},{16,48},{24,56},{32,0},{40,8},{48,16},{56,24},{1,33}... | collective-permute-start | bytes 196616 | tf_op jit(solution)/shard_map/ppermute | solution.py:377
  99.1 1.9 %collective-permute-start.16 = (bf16[2,128,128]{2,1,0:T(8,128)(2,1)S(1)}, bf16[2,128,128]{2,1,0:T(8,128)(2,1)S(1)}, u32[]{:S(2)}, u32[]{:S(2)}) collective-permute-start(bf16[2,128,128]{2,1,0:T(8,128)(2,1)S(1)} %get-tuple-element.46), channel_id=1, source_target_pairs={{0,48},{8,56},{16,32},{24,40},{32,16},{40,24},{48,0},{56,8},{1,49}... | collective-permute-start | bytes 196616 | tf_op jit(solution)/shard_map/ppermute | solution.py:377
  100.9 2.2 %copy-done = bf16[4,1024,512]{2,1,0:T(8,128)(2,1)S(1)} copy-done((bf16[4,1024,512]{2,1,0:T(8,128)(2,1)S(1)}, bf16[4,1024,512]{2,1,0:T(8,128)(2,1)}, u32[]{:S(2)}) %copy-start) | copy-done | bytes 4194328
  103.1 1.2 %shard_map.78 = (bf16[128,1024]{1,0:T(8,128)(2,1)}, f32[128,1024]{1,0:T(8,128)S(1)}) custom-call(bf16[8,128,128]{2,1,0:T(8,128)(2,1)S(1)} %all-to-all-done.2.y_ref, bf16[4,1024,512]{2,1,0:T(8,128)(2,1)S(1)} %copy-done, bf16[4,1024,512]{2,1,0:T(8,128)(2,1)S(1)} %copy-done), custom_call_target="tpu_custom_call" | custom-call | flops 500000000 | bytes 4000000 | tf_op jit(solution)/shard_map/pallas_call | solution.py:354
  104.3 0.0 collective-permute-done.15.refs_1_
  104.3 2.6 %collective-permute-done.16.refs_2_ = bf16[2,128,128]{2,1,0:T(8,128)(2,1)S(1)} collective-permute-done((bf16[2,128,128]{2,1,0:T(8,128)(2,1)S(1)}, bf16[2,128,128]{2,1,0:T(8,128)(2,1)S(1)}, u32[]{:S(2)}, u32[]{:S(2)}) %collective-permute-start.16) | collective-permute-done | bytes 65568 | tf_op jit(solution)/shard_map/ppermute | solution.py:377
  107.0 1.5 %shard_map.82 = bf16[128,1024]{1,0:T(8,128)(2,1)} custom-call(s32[1]{0:T(128)} %bitcast.6.place_ref, bf16[4,128,128]{2,1,0:T(8,128)(2,1)S(1)} %get-tuple-element.42.keep_ref, bf16[4,128,128]{2,1,0:T(8,128)(2,1)S(1)} %collective-permute-done.13.got_ref, bf16[2,128,128]{2,1,0:T(8,128)(2,1)S(1)} %collective-permute-done.14.refs_0_, ...), custom_call_target="tpu_custom_call" | custom-call | flops 500000000 | bytes 4000000 | tf_op jit(solution)/shard_map/pallas_call | solution.py:354
  108.5 6.4 %all-to-all-done.3.in_ref = bf16[256,8,128]{2,1,0:T(8,128)(2,1)S(1)} async-done(((bf16[256,8,128]{2,1,0:T(8,128)(2,1)}), bf16[256,8,128]{2,1,0:T(8,128)(2,1)S(1)}, u32[]{:S(2)}, u32[]{:S(2)}) %all-to-all-start.3) | async-done | bytes 524320 | tf_op jit(solution)/shard_map/all_to_all | solution.py:421
  115.0 0.8 shard_map.83
  (18 shorter events, 0.1 us)
Async XLA Ops:
  0.6 24.9 %copy-start.6 = (s32[1,32,27]{1,0,2:T(1,128)S(1)}, s32[1,32,27]{1,0,2:T(1,128)}, u32[]{:S(2)}) copy-start(s32[1,32,27]{1,0,2:T(1,128)} %param.8) | copy-start | bytes 10372
  0.6 32.4 %copy-start.3 = (s32[1,32]{1,0:T(1,128)S(1)}, s32[1,32]{1,0:T(1,128)}, u32[]{:S(2)}) copy-start(s32[1,32]{1,0:T(1,128)} %param.9) | copy-start | bytes 388
  3.4 13.0 %all-to-all-start = ((bf16[8,128,128]{2,1,0:T(8,128)(2,1)}), bf16[8,128,128]{2,1,0:T(8,128)(2,1)S(1)}, u32[]{:S(2)}, u32[]{:S(2)}) async-start(bf16[8,128,128]{2,1,0:T(8,128)(2,1)} %shard_map.77), calls=%async_computation | async-start | bytes 524288 | tf_op jit(solution)/shard_map/all_to_all | solution.py:385
  16.5 12.9 %collective-permute-start.3 = (bf16[8,128,128]{2,1,0:T(8,128)(2,1)S(1)}, bf16[8,128,128]{2,1,0:T(8,128)(2,1)S(1)}, u32[]{:S(2)}, u32[]{:S(2)}) collective-permute-start(bf16[8,128,128]{2,1,0:T(8,128)(2,1)S(1)} %all-to-all-done.kv0), channel_id=1, source_target_pairs={{0,64},{64,0},{128,192},{192,128},{1,65},{65,1},{129,193},{193,129... | collective-permute-start | bytes 786440 | tf_op jit(solution)/shard_map/ppermute | solution.py:377
  17.0 15.2 %collective-permute-start.4 = (bf16[8,128,128]{2,1,0:T(8,128)(2,1)S(1)}, bf16[8,128,128]{2,1,0:T(8,128)(2,1)S(1)}, u32[]{:S(2)}, u32[]{:S(2)}) collective-permute-start(bf16[8,128,128]{2,1,0:T(8,128)(2,1)S(1)} %all-to-all-done.kv0), channel_id=1, source_target_pairs={{0,128},{64,192},{128,0},{192,64},{1,129},{65,193},{129,1},{193,65... | collective-permute-start | bytes 786440 | tf_op jit(solution)/shard_map/ppermute | solution.py:377
  19.6 13.4 %collective-permute-start.5 = (bf16[8,128,128]{2,1,0:T(8,128)(2,1)S(1)}, bf16[8,128,128]{2,1,0:T(8,128)(2,1)S(1)}, u32[]{:S(2)}, u32[]{:S(2)}) collective-permute-start(bf16[8,128,128]{2,1,0:T(8,128)(2,1)S(1)} %all-to-all-done.kv0), channel_id=1, source_target_pairs={{0,192},{64,128},{128,64},{192,0},{1,193},{65,129},{129,65},{193,1... | collective-permute-start | bytes 786440 | tf_op jit(solution)/shard_map/ppermute | solution.py:377
  20.3 11.9 %all-to-all-start.1 = ((bf16[8,128,128]{2,1,0:T(8,128)(2,1)}), bf16[8,128,128]{2,1,0:T(8,128)(2,1)S(1)}, u32[]{:S(2)}, u32[]{:S(2)}) async-start(bf16[8,128,128]{2,1,0:T(8,128)(2,1)} %get-tuple-element.29), calls=%async_computation.1 | async-start | bytes 524288 | tf_op jit(solution)/shard_map/all_to_all | solution.py:385
  25.6 28.1 %collective-permute-start = (bf16[2,1024,128]{2,1,0:T(8,128)(2,1)}, bf16[2,1024,128]{2,1,0:T(8,128)(2,1)S(1)}, u32[]{:S(2)}, u32[]{:S(2)}) collective-permute-start(bf16[2,1024,128]{2,1,0:T(8,128)(2,1)} %get-tuple-element.38.refs_0_), channel_id=1, source_target_pairs={{0,16},{8,24},{16,0},{24,8},{32,48},{40,56},{48,32},{56,40},{1,17}... | collective-permute-start | bytes 1572872 | tf_op jit(solution)/shard_map/ppermute | solution.py:377
  27.0 27.6 %collective-permute-start.1 = (bf16[2,1024,128]{2,1,0:T(8,128)(2,1)}, bf16[2,1024,128]{2,1,0:T(8,128)(2,1)S(1)}, u32[]{:S(2)}, u32[]{:S(2)}) collective-permute-start(bf16[2,1024,128]{2,1,0:T(8,128)(2,1)} %get-tuple-element.38.refs_0_), channel_id=1, source_target_pairs={{0,32},{8,40},{16,48},{24,56},{32,0},{40,8},{48,16},{56,24},{1,33}... | collective-permute-start | bytes 1572872 | tf_op jit(solution)/shard_map/ppermute | solution.py:377
  29.4 25.2 %collective-permute-start.2 = (bf16[2,1024,128]{2,1,0:T(8,128)(2,1)}, bf16[2,1024,128]{2,1,0:T(8,128)(2,1)S(1)}, u32[]{:S(2)}, u32[]{:S(2)}) collective-permute-start(bf16[2,1024,128]{2,1,0:T(8,128)(2,1)} %get-tuple-element.38.refs_0_), channel_id=1, source_target_pairs={{0,48},{8,56},{16,32},{24,40},{32,16},{40,24},{48,0},{56,8},{1,49}... | collective-permute-start | bytes 1572872 | tf_op jit(solution)/shard_map/ppermute | solution.py:377
  33.0 23.9 %copy-start.1 = (bf16[2,1024,128]{2,1,0:T(8,128)(2,1)S(1)}, bf16[2,1024,128]{2,1,0:T(8,128)(2,1)}, u32[]{:S(2)}) copy-start(bf16[2,1024,128]{2,1,0:T(8,128)(2,1)} %get-tuple-element.38.refs_0_) | copy-start | bytes 1572868
  52.9 0.8 copy-start.4
  54.6 3.3 %collective-permute-start.10 = (bf16[2,1024,128]{2,1,0:T(8,128)(2,1)S(1)}, bf16[2,1024,128]{2,1,0:T(8,128)(2,1)S(1)}, u32[]{:S(2)}, u32[]{:S(2)}) collective-permute-start(bf16[2,1024,128]{2,1,0:T(8,128)(2,1)S(1)} %collective-permute-done.refs_1_), channel_id=1, source_target_pairs={{0,8},{8,0},{16,24},{24,16},{32,40},{40,32},{48,56},{56,48},{1,9},... | collective-permute-start | bytes 1572872 | tf_op jit(solution)/shard_map/ppermute | solution.py:377
  56.4 5.1 %collective-permute-start.11 = (bf16[2,1024,128]{2,1,0:T(8,128)(2,1)S(1)}, bf16[2,1024,128]{2,1,0:T(8,128)(2,1)S(1)}, u32[]{:S(2)}, u32[]{:S(2)}) collective-permute-start(bf16[2,1024,128]{2,1,0:T(8,128)(2,1)S(1)} %collective-permute-done.1.refs_2_), channel_id=1, source_target_pairs={{0,8},{8,0},{16,24},{24,16},{32,40},{40,32},{48,56},{56,48},{1,9},... | collective-permute-start | bytes 1572872 | tf_op jit(solution)/shard_map/ppermute | solution.py:377
  56.4 9.6 %collective-permute-start.12 = (bf16[2,1024,128]{2,1,0:T(8,128)(2,1)S(1)}, bf16[2,1024,128]{2,1,0:T(8,128)(2,1)}, u32[]{:S(2)}, u32[]{:S(2)}) collective-permute-start(bf16[2,1024,128]{2,1,0:T(8,128)(2,1)S(1)} %collective-permute-done.2.refs_3_), channel_id=1, source_target_pairs={{0,8},{8,0},{16,24},{24,16},{32,40},{40,32},{48,56},{56,48},{1,9},... | collective-permute-start | bytes 1572872 | tf_op jit(solution)/shard_map/ppermute | solution.py:377
  56.9 9.1 %collective-permute-start.9 = (bf16[2,1024,128]{2,1,0:T(8,128)(2,1)S(1)}, bf16[2,1024,128]{2,1,0:T(8,128)(2,1)}, u32[]{:S(2)}, u32[]{:S(2)}) collective-permute-start(bf16[2,1024,128]{2,1,0:T(8,128)(2,1)S(1)} %copy-done.1), channel_id=1, source_target_pairs={{0,8},{8,0},{16,24},{24,16},{32,40},{40,32},{48,56},{56,48},{1,9},... | collective-permute-start | bytes 1572872 | tf_op jit(solution)/shard_map/ppermute | solution.py:377
  56.9 11.6 %collective-permute-start.6 = (bf16[8,128,128]{2,1,0:T(8,128)(2,1)}, bf16[8,128,128]{2,1,0:T(8,128)(2,1)}, u32[]{:S(2)}, u32[]{:S(2)}) collective-permute-start(bf16[8,128,128]{2,1,0:T(8,128)(2,1)} %get-tuple-element.35), channel_id=1, source_target_pairs={{0,64},{64,0},{128,192},{192,128},{1,65},{65,1},{129,193},{193,129... | collective-permute-start | bytes 786440 | tf_op jit(solution)/shard_map/ppermute | solution.py:377
  57.9 15.5 %collective-permute-start.7 = (bf16[8,128,128]{2,1,0:T(8,128)(2,1)}, bf16[8,128,128]{2,1,0:T(8,128)(2,1)}, u32[]{:S(2)}, u32[]{:S(2)}) collective-permute-start(bf16[8,128,128]{2,1,0:T(8,128)(2,1)} %get-tuple-element.36), channel_id=1, source_target_pairs={{0,128},{64,192},{128,0},{192,64},{1,129},{65,193},{129,1},{193,65... | collective-permute-start | bytes 786440 | tf_op jit(solution)/shard_map/ppermute | solution.py:377
  61.5 14.0 %collective-permute-start.8 = (bf16[8,128,128]{2,1,0:T(8,128)(2,1)}, bf16[8,128,128]{2,1,0:T(8,128)(2,1)}, u32[]{:S(2)}, u32[]{:S(2)}) collective-permute-start(bf16[8,128,128]{2,1,0:T(8,128)(2,1)} %get-tuple-element.37), channel_id=1, source_target_pairs={{0,192},{64,128},{128,64},{192,0},{1,193},{65,129},{129,65},{193,1... | collective-permute-start | bytes 786440 | tf_op jit(solution)/shard_map/ppermute | solution.py:377
  62.0 18.4 %all-to-all-start.2 = ((bf16[8,128,128]{2,1,0:T(8,128)(2,1)}), bf16[8,128,128]{2,1,0:T(8,128)(2,1)S(1)}, u32[]{:S(2)}, u32[]{:S(2)}) async-start(bf16[8,128,128]{2,1,0:T(8,128)(2,1)} %get-tuple-element.32.y_ref), calls=%async_computation.2 | async-start | bytes 524288 | tf_op jit(solution)/shard_map/all_to_all | solution.py:385
  66.0 9.6 %copy-start.5 = (f32[8,128,128]{2,1,0:T(8,128)S(1)}, f32[8,128,128]{2,1,0:T(8,128)}, u32[]{:S(2)}) copy-start(f32[8,128,128]{2,1,0:T(8,128)} %copy-done.4) | copy-start | bytes 1572868
  79.7 0.7 copy-start.2
  80.3 34.6 %all-to-all-start.3 = ((bf16[256,8,128]{2,1,0:T(8,128)(2,1)}), bf16[256,8,128]{2,1,0:T(8,128)(2,1)S(1)}, u32[]{:S(2)}, u32[]{:S(2)}) async-start(bf16[256,8,128]{2,1,0:T(8,128)(2,1)} %get-tuple-element.48), calls=%async_computation.3 | async-start | bytes 1048576 | tf_op jit(solution)/shard_map/all_to_all | solution.py:421
  93.5 3.4 %collective-permute-start.13 = (bf16[4,128,128]{2,1,0:T(8,128)(2,1)}, bf16[4,128,128]{2,1,0:T(8,128)(2,1)S(1)}, u32[]{:S(2)}, u32[]{:S(2)}) collective-permute-start(bf16[4,128,128]{2,1,0:T(8,128)(2,1)} %copy-done.2), channel_id=1, source_target_pairs={{0,8},{8,0},{16,24},{24,16},{32,40},{40,32},{48,56},{56,48},{1,9},... | collective-permute-start | bytes 393224 | tf_op jit(solution)/shard_map/ppermute | solution.py:377
  97.0 7.4 %collective-permute-start.14 = (bf16[2,128,128]{2,1,0:T(8,128)(2,1)S(1)}, bf16[2,128,128]{2,1,0:T(8,128)(2,1)S(1)}, u32[]{:S(2)}, u32[]{:S(2)}) collective-permute-start(bf16[2,128,128]{2,1,0:T(8,128)(2,1)S(1)} %get-tuple-element.44), channel_id=1, source_target_pairs={{0,16},{8,24},{16,0},{24,8},{32,48},{40,56},{48,32},{56,40},{1,17}... | collective-permute-start | bytes 196616 | tf_op jit(solution)/shard_map/ppermute | solution.py:377
  97.1 7.3 %collective-permute-start.15 = (bf16[2,128,128]{2,1,0:T(8,128)(2,1)S(1)}, bf16[2,128,128]{2,1,0:T(8,128)(2,1)S(1)}, u32[]{:S(2)}, u32[]{:S(2)}) collective-permute-start(bf16[2,128,128]{2,1,0:T(8,128)(2,1)S(1)} %get-tuple-element.45), channel_id=1, source_target_pairs={{0,32},{8,40},{16,48},{24,56},{32,0},{40,8},{48,16},{56,24},{1,33}... | collective-permute-start | bytes 196616 | tf_op jit(solution)/shard_map/ppermute | solution.py:377
  99.1 7.9 %collective-permute-start.16 = (bf16[2,128,128]{2,1,0:T(8,128)(2,1)S(1)}, bf16[2,128,128]{2,1,0:T(8,128)(2,1)S(1)}, u32[]{:S(2)}, u32[]{:S(2)}) collective-permute-start(bf16[2,128,128]{2,1,0:T(8,128)(2,1)S(1)} %get-tuple-element.46), channel_id=1, source_target_pairs={{0,48},{8,56},{16,32},{24,40},{32,16},{40,24},{48,0},{56,8},{1,49}... | collective-permute-start | bytes 196616 | tf_op jit(solution)/shard_map/ppermute | solution.py:377
  100.9 2.2 %copy-start = (bf16[4,1024,512]{2,1,0:T(8,128)(2,1)S(1)}, bf16[4,1024,512]{2,1,0:T(8,128)(2,1)}, u32[]{:S(2)}) copy-start(bf16[4,1024,512]{2,1,0:T(8,128)(2,1)} %refs_5_.1) | copy-start | bytes 12582916
